TPU v7x, 256 devices: a whole 4x4x8 slice. The times are simulated.
256 devices in a mesh: dp: 64 (over y, z, core), tensor: 4 (over x).
Axes of the slice: x: 4, y: 4, z: 8, core: 2. Of those that a mesh axis runs over, the one named last changes fastest.
Arguments:
- queries: bfloat16 [32768, 4096], P('dp', 'tensor'), may hold values from -6 to 6
- passages: bfloat16 [16384, 4096], P('dp', 'tensor'), may hold values from -6 to 6
- neg_lists: int32 [512, 16], replicated, may hold values from -1 to 1023, as said below
- positives: int32 [32768], P('dp'), may hold values from 0 to 16383, as said below
Outputs:
- query_grad: bfloat16 [32768, 4096], P('dp', 'tensor')
- passage_grad: bfloat16 [16384, 4096], P('dp', 'tensor')
- query_loss: float32 [32768], P('dp')
Inputs may be any that keep to these rules, and one draw needn't show every extreme that they name: `neg_lists`: each row names distinct blocks, its live entries first and then -1, with 8 or more live. The rows of query blocks d * 8 to (d + 1) * 8 - 1 name at most 64 distinct blocks, and at most 1 distinct blocks of one owner, blocks d * 16 to (d + 1) * 16 - 1 belonging to index d of dp. `positives`: the positive of a query is a passage of a live block in its query block's row.
All inputs are finite; a program needn't handle non-finite values.
Results may differ from a plain program's by a relative error of at most 0.0051.
Values may be sent and summed in bfloat16 or wider, within the bound.
No kernel may reach another device: no remote copies, remote signals or barrier semaphores. Data moves between devices by JAX's collectives and lax.ppermute only.
A program may use at most 128 MiB of HBM per device.

v0:
```python
from functools import partial

import jax
import jax.numpy as jnp
from jax import lax
from jax.experimental import pallas as pl
from jax.experimental.pallas import tpu as pltpu
from jax.sharding import PartitionSpec as P

MINP = 64
NPRE = 7
PBLK = 16

EPS = 1e-06
INV_TEMP = 20.0

F32 = jnp.float32
BF16 = jnp.bfloat16

AUX = 8
COEF_AUX = 32


def vmem():
    return pl.BlockSpec(memory_space=pltpu.VMEM)


def smem():
    return pl.BlockSpec(memory_space=pltpu.SMEM)


def params():
    return pltpu.CompilerParams(vmem_limit_bytes=40 * 2**20)


def contract(a, b, da, db):
    return lax.dot_general(a, b, (((da,), (db,)), ((), ())), preferred_element_type=F32)


def eye(n):
    return lax.broadcasted_iota(jnp.int32, (n, n), 0) == lax.broadcasted_iota(jnp.int32, (n, n), 1)


def to_col(row):
    return jnp.sum(jnp.where(eye(row.shape[1]), row, 0.0), axis=1, keepdims=True)


def to_row(col):
    return jnp.sum(jnp.where(eye(col.shape[0]), col, 0.0), axis=0, keepdims=True)


def square_sums_as_row(half):
    wide = half.astype(F32)
    square = wide * wide
    high = square.astype(BF16)
    low = (square - high.astype(F32)).astype(BF16)
    ones = jnp.ones((8, half.shape[1]), BF16)
    return contract(ones, high, 1, 1) + contract(ones, low, 1, 1)


def square_sums_as_col(half):
    wide = half.astype(F32)
    return jnp.sum(wide * wide, axis=1, keepdims=True)


def terms(dots, qq_col, pp_row, ids_row, pos_col, weight):
    live = ids_row >= 0.0
    labels = jnp.where(ids_row == pos_col, 1.0, 0.0)
    a = lax.rsqrt(qq_col + EPS)
    b = jnp.where(live, lax.rsqrt(pp_row + EPS), 0.0)
    scale = (a * INV_TEMP) * b
    logits = dots * scale
    exponent = jnp.where(live, jnp.exp(logits), 0.0)
    total = jnp.sum(exponent, axis=1, keepdims=True)
    entropy = jnp.log(total) - jnp.sum(labels * logits, axis=1, keepdims=True)
    gradient = weight * (exponent * (1.0 / total) - labels)
    inner = gradient * logits
    row = (a * a) * jnp.sum(inner, axis=1, keepdims=True)
    col = (b * b) * jnp.sum(inner, axis=0, keepdims=True)
    return gradient * scale, row, col, weight * entropy


def take_blocks(pool_ref, slot_ref, block, count, out_ref):
    for n in range(count):
        slot = slot_ref[block * count + n]
        out_ref[n * PBLK : (n + 1) * PBLK, :] = pool_ref[pl.ds(slot * PBLK, PBLK), :]


def pack_kernel(wanted_ref, block_ref, out_ref):
    def step(d, carry):
        out_ref[d] = block_ref[jnp.maximum(wanted_ref[d], 0)]
        return carry

    lax.fori_loop(0, out_ref.shape[0], step, 0, unroll=8)


def dots_kernel(shards, per_shard, rows, slot_ref, shard_ref, query_ref, pool_ref, *refs):
    outs, cand_ref = refs[:-1], refs[-1]
    count = cand_ref.shape[0] // PBLK
    shard = shard_ref[0]
    for shift in range(shards):
        out_ref = outs[shift]
        target = lax.rem(shard + shift, shards)
        for k in range(per_shard):
            block = target * per_shard + k
            take_blocks(pool_ref, slot_ref, block, count, cand_ref)
            query = query_ref[pl.ds(block * rows, rows), :]
            cand = cand_ref[...]
            out_ref[k * rows : (k + 1) * rows, :] = contract(query, cand, 1, 1)
            base = per_shard * rows
            out_ref[base + k : base + k + 1, :] = square_sums_as_row(cand)[0:1, :]
            out_ref[base + per_shard : base + per_shard + 1, k * rows : (k + 1) * rows] = to_row(
                square_sums_as_col(query)
            )


def low_kernel(
    bounds, rows, slot_ref, shard_ref, query_ref, pool_ref, ids_ref, pos_ref,
    coef_ref, row_ref, col_ref, loss_ref, cand_ref, term_ref,
):
    count = cand_ref.shape[0] // PBLK
    levels = len(bounds)

    @pl.when(shard_ref[0] == 0)
    def _():
        row_ref[...] = jnp.zeros_like(row_ref)
        col_ref[...] = jnp.zeros_like(col_ref)

        def step(block, carry):
            take_blocks(pool_ref, slot_ref, block, count, cand_ref)
            ids = ids_ref[pl.ds(block, 1), :]
            pos = to_col(pos_ref[pl.ds(block, 1), :])
            dots = jnp.zeros((rows, cand_ref.shape[0]), F32)
            qq = jnp.zeros((rows, 1), F32)
            pp = jnp.zeros((8, cand_ref.shape[0]), F32)
            loss = jnp.zeros((rows, 1), F32)
            row_terms, col_terms = [], []
            for level, (low, high) in enumerate(bounds):
                query = query_ref[pl.ds(block * rows, rows), low:high]
                cand = cand_ref[:, low:high]
                dots = dots + contract(query, cand, 1, 1)
                qq = qq + square_sums_as_col(query)
                pp = pp + square_sums_as_row(cand)
                coef, row, col, part = terms(dots, qq, pp[0:1, :], ids, pos, float(high // MINP))
                term_ref[level] = coef
                row_terms.append(to_row(row))
                col_terms.append(col)
                loss = loss + part
            coef = jnp.zeros((rows, cand_ref.shape[0]), F32)
            row = jnp.zeros((1, rows), F32)
            col = jnp.zeros((1, cand_ref.shape[0]), F32)
            for level in reversed(range(levels)):
                coef = coef + term_ref[level]
                row = row + row_terms[level]
                col = col + col_terms[level]
                coef_ref[level, pl.ds(block * rows, rows), :] = coef
                row_ref[block, level : level + 1, :] = row
                col_ref[block, level : level + 1, :] = col
            loss_ref[pl.ds(block, 1), :] = to_row(loss)
            return carry

        lax.fori_loop(0, loss_ref.shape[0], step, 0)

    @pl.when(shard_ref[0] != 0)
    def _():
        loss_ref[...] = jnp.zeros_like(loss_ref)


def high_kernel(shards, per_shard, rows, weights, shard_ref, ids_ref, pos_ref, low_loss_ref, *refs):
    ins, outs = refs[:shards], refs[shards:]
    shard = shard_ref[0]
    base = per_shard * rows
    half_rows, half_cols, full_rows, full_cols = [], [], [], []
    losses = []
    width = ins[0].shape[1]
    coefs = []
    in_half = [
        jnp.where(lax.rem(shard - shift + shards, shards) < shards // 2, 1.0, 0.0)
        for shift in range(shards)
    ]
    aux_full = sum(ref[base : base + AUX, :] for ref in ins)
    aux_half = sum(ref[base : base + AUX, :] * keep for ref, keep in zip(ins, in_half))
    for k in range(per_shard):
        block = shard * per_shard + k
        ids = ids_ref[pl.ds(block, 1), :]
        pos = to_col(pos_ref[pl.ds(block, 1), :])
        span = slice(k * rows, (k + 1) * rows)
        dots_full = sum(ref[span, :] for ref in ins)
        dots_half = sum(ref[span, :] * keep for ref, keep in zip(ins, in_half))
        results = []
        for dots, aux, weight in (
            (dots_half, aux_half, weights[0]),
            (dots_full, aux_full, weights[1]),
        ):
            qq = to_col(aux[per_shard : per_shard + 1, span])
            results.append(terms(dots, qq, aux[k : k + 1, :], ids, pos, weight))
        (coef_h, row_h, col_h, loss_h), (coef_f, row_f, col_f, loss_f) = results
        coefs.append((coef_h + coef_f, coef_f))
        half_rows.append(to_row(row_h + row_f))
        full_rows.append(to_row(row_f))
        half_cols.append(col_h + col_f)
        full_cols.append(col_f)
        losses.append(to_row(loss_h + loss_f))
    per_row = width // rows
    low = [
        jnp.concatenate([low_loss_ref[r * per_row + j : r * per_row + j + 1, :] for j in range(per_row)], axis=1)
        for r in range(low_loss_ref.shape[0] // per_row)
    ]

    def aux_rows(rows_list, cols_list):
        line = jnp.concatenate(rows_list + losses, axis=1)
        table = jnp.concatenate(cols_list + [line] + low, axis=0)
        table = jnp.concatenate([table, jnp.zeros((AUX - table.shape[0], width), F32)], axis=0)
        first = table.astype(BF16).astype(F32)
        second = (table - first).astype(BF16).astype(F32)
        third = table - first - second
        return jnp.concatenate([first, second, third, jnp.zeros_like(table)], axis=0).astype(BF16)

    aux = (aux_rows(half_rows, half_cols), aux_rows(full_rows, full_cols))
    for shift in range(shards):
        out_ref = outs[shift]
        high_target = lax.rem(shard + shift, shards) >= shards // 2

        @pl.when(high_target)
        def _():
            for k in range(per_shard):
                out_ref[k * rows : (k + 1) * rows, :] = coefs[k][1].astype(BF16)
            out_ref[base : base + COEF_AUX, :] = aux[1]

        @pl.when(jnp.logical_not(high_target))
        def _():
            for k in range(per_shard):
                out_ref[k * rows : (k + 1) * rows, :] = coefs[k][0].astype(BF16)
            out_ref[base : base + COEF_AUX, :] = aux[0]


def grads_kernel(
    bounds, shards, per_shard, rows, loss_scale, slot_ref, shard_ref, query_ref, pool_ref, low_row_ref,
    low_col_ref, low_coef_hbm, *refs,
):
    ins = refs[:shards]
    query_grad_ref, slot_grad_ref, loss_ref = refs[shards : shards + 3]
    cand_ref, coef_ref, row_ref, col_ref, sum_ref, scale_ref, low_coef_ref, sem = refs[shards + 3 :]
    shard = shard_ref[0]
    base = per_shard * rows
    blocks = shards * per_shard
    count = cand_ref.shape[0] // PBLK
    width = query_ref.shape[1]
    cands = cand_ref.shape[0]
    copy = pltpu.make_async_copy(low_coef_hbm, low_coef_ref, sem)

    @pl.when(shard == 0)
    def _():
        copy.start()

    sum_ref[...] = jnp.zeros_like(sum_ref)
    scale_ref[...] = jnp.zeros_like(scale_ref)
    loss_low = jnp.zeros((AUX, cands), F32)
    for shift in range(shards):
        source = lax.rem(shard - shift + shards, shards)
        coef_ref[pl.ds(source * base, base), :] = ins[shift][:base, :]
        packed = ins[shift][base : base + COEF_AUX, :].astype(F32)
        aux = packed[:AUX] + packed[AUX : 2 * AUX] + packed[2 * AUX : 3 * AUX]
        for k in range(per_shard):
            col_ref[source * per_shard + k] = aux[k : k + 1, :]
            row_ref[source * per_shard + k] = aux[per_shard : per_shard + 1, k * rows : (k + 1) * rows]
        loss_ref[pl.ds(source, 1), :] = aux[per_shard : per_shard + 1, base:]
        loss_low = loss_low + jnp.where(source == 0, aux, 0.0)
    per_row = cands // base
    for r in range(shards):
        low = loss_low[per_shard + 1 + r // per_row : per_shard + 2 + r // per_row, :]
        low = low[:, (r % per_row) * base : (r % per_row + 1) * base]
        loss_ref[r : r + 1, :] = (loss_ref[r : r + 1, :] + low) * loss_scale

    def run(spans, low):
        levels = len(spans)

        def step(block, carry):
            take_blocks(pool_ref, slot_ref, block, count, cand_ref)
            rows_here = jnp.broadcast_to(row_ref[block], (8, rows))
            cols_here = jnp.broadcast_to(col_ref[block], (8, cands))
            if low:
                rows_here = rows_here + low_row_ref[block]
                cols_here = cols_here + low_col_ref[block]
            row_cols = jnp.concatenate(
                [jnp.concatenate([rows_here, jnp.zeros((8, 128 - rows), F32)], axis=1), jnp.zeros((120, 128), F32)],
                axis=0,
            ).T
            col_cols = jnp.concatenate([cols_here, jnp.zeros((120, cands), F32)], axis=0).T
            here = pl.ds(block * rows, rows)
            for n in range(count):
                slot = slot_ref[block * count + n]
                target = pl.ds(slot * PBLK, PBLK)
                scale_ref[target, :] = scale_ref[target, :] + col_cols[n * PBLK : (n + 1) * PBLK, :]
            for level, (lo, hi) in enumerate(spans):
                coef = coef_ref[here, :]
                if low:
                    coef = (coef.astype(F32) + low_coef_ref[level, here, :]).astype(BF16)
                query = query_ref[here, lo:hi]
                cand = cand_ref[:, lo:hi]
                grad = contract(coef, cand, 1, 0) - row_cols[:rows, level : level + 1] * query.astype(F32)
                query_grad_ref[here, lo:hi] = grad.astype(BF16)
                cand_grad = contract(coef, query, 0, 0)
                for n in range(count):
                    slot = slot_ref[block * count + n]
                    target = pl.ds(slot * PBLK, PBLK)
                    sum_ref[target, lo:hi] = sum_ref[target, lo:hi] + cand_grad[n * PBLK : (n + 1) * PBLK, :]
            return carry

        lax.fori_loop(0, blocks, step, 0)

        def finish(i, carry):
            here = pl.ds(i * 64, 64)
            for level, (lo, hi) in enumerate(spans):
                part = sum_ref[here, lo:hi] - scale_ref[here, level : level + 1] * pool_ref[here, lo:hi].astype(F32)
                slot_grad_ref[here, lo:hi] = part.astype(BF16)
            return carry

        lax.fori_loop(0, slot_grad_ref.shape[0] // 64, finish, 0)

    @pl.when(shard == 0)
    def _():
        copy.wait()
        run(bounds, True)

    @pl.when(shard != 0)
    def _():
        run([(0, width)], False)


def gather_kernel(wanted_ref, back_ref, out_ref, sum_ref):
    sum_ref[...] = jnp.zeros_like(sum_ref)

    def step(d, carry):
        target = jnp.maximum(wanted_ref[d], 0)
        keep = jnp.where(wanted_ref[d] >= 0, 1.0, 0.0)
        sum_ref[target] = sum_ref[target] + back_ref[d].astype(F32) * keep
        return carry

    lax.fori_loop(0, back_ref.shape[0], step, 0, unroll=4)
    out_ref[...] = sum_ref[...].astype(BF16)


def per_device(queries, passages, neg_lists, positives):
    peers = lax.axis_size("dp")
    shards = lax.axis_size("tensor")
    total_rows, width = queries.shape
    blocks = neg_lists.shape[0] // peers
    count = neg_lists.shape[1]
    rows = total_rows // blocks
    local_blocks = passages.shape[0] // PBLK
    cands = count * PBLK
    per_shard = blocks // shards
    base = per_shard * rows
    slots = peers
    my_index = lax.axis_index("dp")
    shard = lax.axis_index("tensor")
    sizes = [MINP * 2**level for level in range(NPRE)]
    low_sizes = [size for size in sizes if size <= width]
    high_sizes = [size for size in sizes if size > width]
    assert high_sizes == [width * shards // 2, width * shards] and low_sizes[-1] == width
    bounds = list(zip([0] + low_sizes[:-1], low_sizes))
    levels = len(bounds)
    weight_total = sum(size / MINP for size in sizes)

    flat = neg_lists.reshape(peers, blocks * count)
    mine = (flat >= 0) & (flat // local_blocks == my_index)
    wanted = jnp.max(jnp.where(mine, flat % local_blocks, -1), axis=1)
    own = lax.dynamic_slice_in_dim(neg_lists, my_index * blocks, blocks, 0)
    valid = own >= 0
    slot = jnp.where(valid, own // local_blocks, 0).reshape(blocks * count)
    ids = jnp.where(
        valid[:, :, None], own[:, :, None] * PBLK + jnp.arange(PBLK, dtype=jnp.int32)[None, None, :], -1
    )
    ids = ids.reshape(blocks, cands).astype(F32)
    pos = positives.reshape(blocks, rows).astype(F32)
    shard_arr = shard.reshape(1).astype(jnp.int32)

    panels = pl.pallas_call(
        pack_kernel,
        out_shape=jax.ShapeDtypeStruct((peers, PBLK, width), BF16),
        in_specs=[smem(), vmem()],
        out_specs=vmem(),
        compiler_params=params(),
        name="pack",
    )(wanted, passages.reshape(local_blocks, PBLK, width))
    pool = lax.all_to_all(panels, "dp", split_axis=0, concat_axis=0, tiled=True)
    pool = pool.reshape(slots * PBLK, width)

    message = jax.ShapeDtypeStruct((base + AUX, cands), F32)
    dots = pl.pallas_call(
        partial(dots_kernel, shards, per_shard, rows),
        out_shape=[message] * shards,
        in_specs=[smem(), smem(), vmem(), vmem()],
        out_specs=[vmem()] * shards,
        scratch_shapes=[pltpu.VMEM((cands, width), BF16)],
        compiler_params=params(),
        name="dots",
    )(slot, shard_arr, queries, pool)

    def exchange(parts):
        return [parts[0]] + [
            lax.ppermute(parts[s], "tensor", [(i, (i + s) % shards) for i in range(shards)])
            for s in range(1, shards)
        ]

    arrived = exchange(dots)
    low_coef, low_row, low_col, low_loss = pl.pallas_call(
        partial(low_kernel, bounds, rows),
        out_shape=[
            jax.ShapeDtypeStruct((levels, total_rows, cands), F32),
            jax.ShapeDtypeStruct((blocks, 8, rows), F32),
            jax.ShapeDtypeStruct((blocks, 8, cands), F32),
            jax.ShapeDtypeStruct((blocks, rows), F32),
        ],
        in_specs=[smem(), smem(), vmem(), vmem(), vmem(), vmem()],
        out_specs=[vmem()] * 4,
        scratch_shapes=[pltpu.VMEM((cands, width), BF16), pltpu.VMEM((levels, rows, cands), F32)],
        compiler_params=params(),
        name="low",
    )(slot, shard_arr, queries, pool, ids, pos)

    coef_message = jax.ShapeDtypeStruct((base + COEF_AUX, cands), BF16)
    coefs = pl.pallas_call(
        partial(high_kernel, shards, per_shard, rows, [size / MINP for size in high_sizes]),
        out_shape=[coef_message] * shards,
        in_specs=[smem()] + [vmem()] * (3 + shards),
        out_specs=[vmem()] * shards,
        compiler_params=params(),
        name="high",
    )(shard_arr, ids, pos, low_loss, *arrived)
    coefs = exchange(coefs)

    query_grad, slot_grad, loss = pl.pallas_call(
        partial(grads_kernel, bounds, shards, per_shard, rows, 1.0 / weight_total),
        out_shape=[
            jax.ShapeDtypeStruct((total_rows, width), BF16),
            jax.ShapeDtypeStruct((slots * PBLK, width), BF16),
            jax.ShapeDtypeStruct((shards, base), F32),
        ],
        in_specs=[smem(), smem()] + [vmem()] * 4 + [pl.BlockSpec(memory_space=pl.ANY)] + [vmem()] * shards,
        out_specs=[vmem()] * 3,
        scratch_shapes=[
            pltpu.VMEM((cands, width), BF16),
            pltpu.VMEM((total_rows, cands), BF16),
            pltpu.VMEM((blocks, 1, rows), F32),
            pltpu.VMEM((blocks, 1, cands), F32),
            pltpu.VMEM((slots * PBLK, width), F32),
            pltpu.VMEM((slots * PBLK, 128), F32),
            pltpu.VMEM((levels, total_rows, cands), F32),
            pltpu.SemaphoreType.DMA(()),
        ],
        compiler_params=params(),
        name="grads",
    )(slot, shard_arr, queries, pool, low_row, low_col, low_coef, *coefs)

    back = lax.all_to_all(
        slot_grad.reshape(slots, PBLK, width), "dp", split_axis=0, concat_axis=0, tiled=True
    )
    passage_grad = pl.pallas_call(
        gather_kernel,
        out_shape=jax.ShapeDtypeStruct((local_blocks, PBLK, width), BF16),
        in_specs=[smem(), vmem()],
        out_specs=vmem(),
        scratch_shapes=[pltpu.VMEM((local_blocks, PBLK, width), F32)],
        compiler_params=params(),
        name="collect",
    )(wanted, back)
    return (
        query_grad,
        passage_grad.reshape(local_blocks * PBLK, width),
        loss.reshape(total_rows),
    )


def solution(mesh):
    return jax.shard_map(
        per_device,
        mesh=mesh,
        in_specs=(P("dp", "tensor"), P("dp", "tensor"), P(), P("dp")),
        out_specs=(P("dp", "tensor"), P("dp", "tensor"), P("dp")),
        check_vma=False,
    )
```

profile of v0, /device:TPU:1, one launch (start us, length us, event | category | flops | bytes accessed | tf_op | source)
XLA Modules:
  0.0 164.2 jit_solution(14782832627303620840)
XLA Ops:
  0.6 0.8 fusion.2
  1.4 0.1 reduce_max.14
  1.5 0.1 reduce_max.18.wanted_ref
  1.7 0.0 copy-start.2
  1.7 1.0 copy-done.2
  2.7 0.7 pack.1
  3.4 0.0 copy-start.1
  3.4 1.3 copy-done.1
  4.8 0.0 copy-start.3
  4.8 0.0 copy-start
  4.8 13.3 %all-to-all-start = ((bf16[64,16,1024]{2,1,0:T(8,128)(2,1)}), bf16[64,16,1024]{2,1,0:T(8,128)(2,1)S(1)}, u32[]{:S(2)}, u32[]{:S(2)}) async-start(bf16[64,16,1024]{2,1,0:T(8,128)(2,1)} %copy-done.1), calls=%async_computation | async-start | bytes 4194304 | tf_op jit(solution)/shard_map/all_to_all | solution.py:387
  18.1 0.0 copy-done.3
  18.1 0.1 convert_element_type.10.pos_ref
  18.2 0.8 constant_dynamic-slice_fusion
  18.9 0.1 copy.14
  19.0 0.1 reshape.38.slot_ref
  19.1 0.1 add.38
  19.2 0.1 broadcast_in_dim.21
  19.3 0.1 broadcast_in_dim.22
  19.4 0.1 add.35
  19.5 0.1 add.36
  19.6 49.7 %all-to-all-done = bf16[64,16,1024]{2,1,0:T(8,128)(2,1)S(1)} async-done(((bf16[64,16,1024]{2,1,0:T(8,128)(2,1)}), bf16[64,16,1024]{2,1,0:T(8,128)(2,1)S(1)}, u32[]{:S(2)}, u32[]{:S(2)}) %all-to-all-start) | async-done | bytes 2097184 | tf_op jit(solution)/shard_map/all_to_all | solution.py:387
  69.3 0.0 copy-done
  69.3 4.1 %dots.1 = (f32[136,256]{1,0:T(8,128)S(1)}, f32[136,256]{1,0:T(8,128)S(1)}, f32[136,256]{1,0:T(8,128)S(1)}, f32[136,256]{1,0:T(8,128)S(1)}) custom-call(s32[128]{0:T(128)S(1)} %reshape.38.slot_ref, s32[1]{0:T(128)} %bitcast.shard_ref, bf16[512,1024]{1,0:T(8,128)(2,1)S(1)} %copy-done, bf16[1024,1024]{1,0:T(8,128)(2,1)S(1)} %bitcast.6), custom_call_target="tpu_custom_call" | custom-call | tf_op jit(solution)/shard_map/dots/pallas_call | solution.py:391
  73.5 1.2 collective-permute-start
  74.7 2.5 %collective-permute-start.1 = (f32[136,256]{1,0:T(8,128)S(1)}, f32[136,256]{1,0:T(8,128)S(1)}, u32[]{:S(2)}, u32[]{:S(2)}) collective-permute-start(f32[136,256]{1,0:T(8,128)S(1)} %get-tuple-element.24), channel_id=1, source_target_pairs={{0,2},{1,3},{2,0},{3,1},{4,6},{5,7},{6,4},{7,5},{8,10},{9,11},{10,... | collective-permute-start | bytes 417800 | tf_op jit(solution)/shard_map/ppermute | solution.py:403
  77.1 1.2 collective-permute-start.2
  78.3 7.6 %low.1 = (f32[5,512,256]{2,1,0:T(8,128)S(1)}, f32[8,8,64]{2,1,0:T(8,128)S(1)}, f32[8,8,256]{2,1,0:T(8,128)S(1)}, f32[8,64]{1,0:T(8,128)S(1)}) custom-call(s32[128]{0:T(128)S(1)} %reshape.38.slot_ref, s32[1]{0:T(128)} %bitcast.shard_ref, bf16[512,1024]{1,0:T(8,128)(2,1)S(1)} %copy-done, bf16[1024,1024]{1,0:T(8,128)(2,1)S(1)} %bitcast.7, ...), custom_call_target="tpu_custom_call" | custom-call | tf_op jit(solution)/shard_map/low/pallas_call | solution.py:408
  85.9 0.0 collective-permute-done.refs_1_
  85.9 0.0 collective-permute-done.1.refs_2_
  85.9 0.0 collective-permute-done.2.refs_3_
  85.9 0.5 high.1
  86.5 0.1 collective-permute-start.3
  86.6 0.8 collective-permute-start.4
  87.4 1.9 %collective-permute-start.5 = (bf16[160,256]{1,0:T(8,128)(2,1)S(1)}, bf16[160,256]{1,0:T(8,128)(2,1)S(1)}, u32[]{:S(2)}, u32[]{:S(2)}) collective-permute-start(bf16[160,256]{1,0:T(8,128)(2,1)S(1)} %get-tuple-element.29), channel_id=1, source_target_pairs={{0,3},{1,0},{2,1},{3,2},{4,7},{5,4},{6,5},{7,6},{8,11},{9,8},{10,9... | collective-permute-start | bytes 245768 | tf_op jit(solution)/shard_map/ppermute | solution.py:403
  89.2 2.7 %collective-permute-done.3.refs_1_ = bf16[160,256]{1,0:T(8,128)(2,1)S(1)} collective-permute-done((bf16[160,256]{1,0:T(8,128)(2,1)S(1)}, bf16[160,256]{1,0:T(8,128)(2,1)S(1)}, u32[]{:S(2)}, u32[]{:S(2)}) %collective-permute-start.3) | collective-permute-done | bytes 81952 | tf_op jit(solution)/shard_map/ppermute | solution.py:403
  91.9 0.0 collective-permute-done.4.refs_2_
  92.0 0.9 collective-permute-done.5.refs_3_
  92.8 10.6 %grads.1 = (bf16[512,1024]{1,0:T(8,128)(2,1)}, bf16[1024,1024]{1,0:T(8,128)(2,1)S(1)}, f32[4,128]{1,0:T(4,128)}) custom-call(s32[128]{0:T(128)S(1)} %reshape.38.slot_ref, s32[1]{0:T(128)} %bitcast.shard_ref, bf16[512,1024]{1,0:T(8,128)(2,1)S(1)} %copy-done, bf16[1024,1024]{1,0:T(8,128)(2,1)S(1)} %bitcast.8, f32[8,8,64]{2,1,0:T(8,128)S(1)} %get-tuple-element.18.low_row_ref, ...), custom_call_target="tpu_custom_call" | custom-call | tf_op jit(solution)/shard_map/grads/pallas_call | solution.py:434
  103.4 58.8 %all_to_all.10.back_ref = bf16[64,16,1024]{2,1,0:T(8,128)(2,1)S(1)} all-to-all(bf16[64,16,1024]{2,1,0:T(8,128)(2,1)S(1)} %bitcast.9), channel_id=1, replica_groups=mesh['dp'=64,'tensor'=4] {'dp'}, dimensions={0} | all-to-all | bytes 4194304 | tf_op jit(solution)/shard_map/all_to_all | solution.py:457
  162.2 2.0 %collect.1 = bf16[16,16,1024]{2,1,0:T(8,128)(2,1)} custom-call(s32[64]{0:T(128)S(1)} %reduce_max.18.wanted_ref, bf16[64,16,1024]{2,1,0:T(8,128)(2,1)S(1)} %all_to_all.10.back_ref), custom_call_target="tpu_custom_call" | custom-call | tf_op jit(solution)/shard_map/collect/pallas_call | solution.py:460
  (5 shorter events, 0.0 us)
Async XLA Ops:
  1.7 1.0 copy-start.2
  3.4 1.3 copy-start.1
  4.8 13.3 %copy-start.3 = (s32[512]{0:T(512)S(1)}, s32[512]{0:T(512)}, u32[]{:S(2)}) copy-start(s32[512]{0:T(512)} %param.7) | copy-start | bytes 6148
  4.8 64.5 %copy-start = (bf16[512,1024]{1,0:T(8,128)(2,1)S(1)}, bf16[512,1024]{1,0:T(8,128)(2,1)}, u32[]{:S(2)}) copy-start(bf16[512,1024]{1,0:T(8,128)(2,1)} %query_ref.5) | copy-start | bytes 3145732
  4.8 64.5 %all-to-all-start = ((bf16[64,16,1024]{2,1,0:T(8,128)(2,1)}), bf16[64,16,1024]{2,1,0:T(8,128)(2,1)S(1)}, u32[]{:S(2)}, u32[]{:S(2)}) async-start(bf16[64,16,1024]{2,1,0:T(8,128)(2,1)} %copy-done.1), calls=%async_computation | async-start | bytes 4194304 | tf_op jit(solution)/shard_map/all_to_all | solution.py:387
  73.5 12.4 %collective-permute-start = (f32[136,256]{1,0:T(8,128)S(1)}, f32[136,256]{1,0:T(8,128)S(1)}, u32[]{:S(2)}, u32[]{:S(2)}) collective-permute-start(f32[136,256]{1,0:T(8,128)S(1)} %get-tuple-element.23), channel_id=1, source_target_pairs={{0,1},{1,2},{2,3},{3,0},{4,5},{5,6},{6,7},{7,4},{8,9},{9,10},{10,1... | collective-permute-start | bytes 417800 | tf_op jit(solution)/shard_map/ppermute | solution.py:403
  74.7 11.2 %collective-permute-start.1 = (f32[136,256]{1,0:T(8,128)S(1)}, f32[136,256]{1,0:T(8,128)S(1)}, u32[]{:S(2)}, u32[]{:S(2)}) collective-permute-start(f32[136,256]{1,0:T(8,128)S(1)} %get-tuple-element.24), channel_id=1, source_target_pairs={{0,2},{1,3},{2,0},{3,1},{4,6},{5,7},{6,4},{7,5},{8,10},{9,11},{10,... | collective-permute-start | bytes 417800 | tf_op jit(solution)/shard_map/ppermute | solution.py:403
  77.1 8.8 %collective-permute-start.2 = (f32[136,256]{1,0:T(8,128)S(1)}, f32[136,256]{1,0:T(8,128)S(1)}, u32[]{:S(2)}, u32[]{:S(2)}) collective-permute-start(f32[136,256]{1,0:T(8,128)S(1)} %get-tuple-element.25), channel_id=1, source_target_pairs={{0,3},{1,0},{2,1},{3,2},{4,7},{5,4},{6,5},{7,6},{8,11},{9,8},{10,9... | collective-permute-start | bytes 417800 | tf_op jit(solution)/shard_map/ppermute | solution.py:403
  86.5 5.5 %collective-permute-start.3 = (bf16[160,256]{1,0:T(8,128)(2,1)S(1)}, bf16[160,256]{1,0:T(8,128)(2,1)S(1)}, u32[]{:S(2)}, u32[]{:S(2)}) collective-permute-start(bf16[160,256]{1,0:T(8,128)(2,1)S(1)} %get-tuple-element.27), channel_id=1, source_target_pairs={{0,1},{1,2},{2,3},{3,0},{4,5},{5,6},{6,7},{7,4},{8,9},{9,10},{10,1... | collective-permute-start | bytes 245768 | tf_op jit(solution)/shard_map/ppermute | solution.py:403
  86.6 5.4 %collective-permute-start.4 = (bf16[160,256]{1,0:T(8,128)(2,1)S(1)}, bf16[160,256]{1,0:T(8,128)(2,1)S(1)}, u32[]{:S(2)}, u32[]{:S(2)}) collective-permute-start(bf16[160,256]{1,0:T(8,128)(2,1)S(1)} %get-tuple-element.28), channel_id=1, source_target_pairs={{0,2},{1,3},{2,0},{3,1},{4,6},{5,7},{6,4},{7,5},{8,10},{9,11},{10,... | collective-permute-start | bytes 245768 | tf_op jit(solution)/shard_map/ppermute | solution.py:403
  87.4 5.5 %collective-permute-start.5 = (bf16[160,256]{1,0:T(8,128)(2,1)S(1)}, bf16[160,256]{1,0:T(8,128)(2,1)S(1)}, u32[]{:S(2)}, u32[]{:S(2)}) collective-permute-start(bf16[160,256]{1,0:T(8,128)(2,1)S(1)} %get-tuple-element.29), channel_id=1, source_target_pairs={{0,3},{1,0},{2,1},{3,2},{4,7},{5,4},{6,5},{7,6},{8,11},{9,8},{10,9... | collective-permute-start | bytes 245768 | tf_op jit(solution)/shard_map/ppermute | solution.py:403
where the time goes:
time: 165 us; the launch traced here: 164 us
  blocking collectives  58.8 us (36%)
  waiting for transfers between devices  53.3 us (32%)
  Pallas kernels  25.6 us (16%)
  starting transfers between devices  20.9 us (13%)
  local copies, waits for them, and re-layouts  3.89 us (2%)
    all_to_all x1, blocking collectives, per_device(): lax.all_to_all(slot_grad.reshape(slots, PBLK, width), 'dp', split_axis=0,...  58.8 us
    all_to_all x1, waiting for transfers between devices, per_device(): pool = lax.all_to_all(panels, 'dp', split_axis=0, concat_axis=0, tiled=True)  49.7 us
    all_to_all x1, starting transfers between devices, per_device(): pool = lax.all_to_all(panels, 'dp', split_axis=0, concat_axis=0, tiled=True)  13.3 us
    pallas_call x1, Pallas kernels, per_device(): pl.pallas_call(partial(grads_kernel, bounds, shards, per_shard, rows, 1.0...  10.6 us
    pallas_call x1, Pallas kernels, per_device(): pl.pallas_call(partial(low_kernel, bounds, rows), out_shape=[jax.ShapeDty...  7.61 us
    ppermute x6, starting transfers between devices, exchange(): lax.ppermute(parts[s], 'tensor', [(i, (i + s) % shards) for i in range(sh...  7.57 us
    pallas_call x1, Pallas kernels, per_device(): pl.pallas_call(partial(dots_kernel, shards, per_shard, rows), out_shape=[...  4.14 us
    ppermute x6, waiting for transfers between devices, exchange(): lax.ppermute(parts[s], 'tensor', [(i, (i + s) % shards) for i in range(sh...  3.58 us
  transfers between devices with their start and end apart: 7, of which 3 were waited for; matrix products, arithmetic and copies ran while one was open for 1% of the time, Pallas kernels for 5%

commit v1 on v0

v1 whole, which is shorter than its diff:
```python
from functools import partial

import jax
import jax.numpy as jnp
from jax import lax
from jax.experimental import pallas as pl
from jax.experimental.pallas import tpu as pltpu
from jax.sharding import PartitionSpec as P

MINP = 64
NPRE = 7
PBLK = 16

EPS = 1e-06
INV_TEMP = 20.0

F32 = jnp.float32
BF16 = jnp.bfloat16

AUX = 8
COEF_AUX = 32
LANES = 128
PIECE = 256
FULL = 4


def vmem():
    return pl.BlockSpec(memory_space=pltpu.VMEM)


def smem():
    return pl.BlockSpec(memory_space=pltpu.SMEM)


def hbm():
    return pl.BlockSpec(memory_space=pltpu.HBM)


def params():
    return pltpu.CompilerParams(vmem_limit_bytes=20 * 2**20)


def contract(a, b, da, db):
    return lax.dot_general(a, b, (((da,), (db,)), ((), ())), preferred_element_type=F32)


def eye(n):
    return lax.broadcasted_iota(jnp.int32, (n, n), 0) == lax.broadcasted_iota(jnp.int32, (n, n), 1)


def to_col(row):
    return jnp.sum(jnp.where(eye(row.shape[1]), row, 0.0), axis=1, keepdims=True)


def to_row(col):
    return jnp.sum(jnp.where(eye(col.shape[0]), col, 0.0), axis=0, keepdims=True)


def square_sums(half):
    wide = half.astype(F32)
    return jnp.sum(wide * wide, axis=1, keepdims=True)


def columns(table):
    table = jnp.concatenate([table, jnp.zeros((8, LANES - table.shape[1]), F32)], axis=1) if table.shape[1] < LANES else table
    return jnp.concatenate([table, jnp.zeros((LANES - 8, table.shape[1]), F32)], axis=0).T


def terms(dots, qq_col, pp_row, live, labels, weight):
    a = lax.rsqrt(qq_col + EPS)
    b = jnp.where(live, lax.rsqrt(pp_row + EPS), 0.0)
    scale = (a * INV_TEMP) * b
    logits = dots * scale
    exponent = jnp.where(live, jnp.exp(logits), 0.0)
    total = jnp.sum(exponent, axis=1, keepdims=True)
    gradient = weight * (exponent * (1.0 / total) - labels)
    inner = gradient * logits
    row = (a * a) * jnp.sum(inner, axis=1, keepdims=True)
    col = (b * b) * jnp.sum(inner, axis=0, keepdims=True)
    return gradient * scale, row, col, weight * jnp.log(total), weight * logits


def take_blocks(pool_ref, slot_ref, block, count, out_ref):
    for n in range(count):
        out_ref[n] = pool_ref[slot_ref[block * count + n]]


def pool_norms(pool_ref, norm_ref, bounds):
    step_slots = 8
    lane = lax.broadcasted_iota(jnp.int32, (step_slots * PBLK, LANES), 1)

    def step(i, carry):
        here = pl.ds(i * step_slots, step_slots)
        block = pool_ref[here]
        wide = block.reshape(step_slots * PBLK, block.shape[2]).astype(F32)
        square = wide * wide
        total = jnp.zeros((step_slots * PBLK, 1), F32)
        result = jnp.zeros((step_slots * PBLK, LANES), F32)
        for level, (low, high) in enumerate(bounds):
            total = total + jnp.sum(square[:, low:high], axis=1, keepdims=True)
            result = jnp.where(lane == level, total, result)
        norm_ref[here] = result.reshape(step_slots, PBLK, LANES)
        return carry

    lax.fori_loop(0, pool_ref.shape[0] // step_slots, step, 0)


def norm_rows(norm_ref, slot_ref, block, count):
    table = jnp.concatenate([norm_ref[slot_ref[block * count + n]] for n in range(count)], axis=0)
    return table.T[:8, :]


def pack_kernel(wanted_ref, block_ref, out_ref, sem):
    def step(d, carry):
        source = block_ref.at[jnp.maximum(wanted_ref[d], 0)]
        pltpu.make_async_copy(source, out_ref.at[d], sem).start()
        return carry

    lax.fori_loop(0, out_ref.shape[0], step, 0, unroll=8)
    pltpu.make_async_copy(out_ref, out_ref, sem).wait()


def dots_kernel(shards, per_shard, rows, shifts, slot_ref, shard_ref, query_ref, pool_ref, norm_ref, *refs):
    outs, cand_ref = refs[:-1], refs[-1]
    count, _, width = cand_ref.shape
    shard = shard_ref[0]
    base = per_shard * rows
    for shift, out_ref in zip(shifts, outs):
        target = lax.rem(shard + shift, shards)
        for k in range(per_shard):
            block = target * per_shard + k
            take_blocks(pool_ref, slot_ref, block, count, cand_ref)
            query = query_ref[pl.ds(block * rows, rows), :]
            cand = cand_ref[...].reshape(count * PBLK, width)
            out_ref[k * rows : (k + 1) * rows, :] = contract(query, cand, 1, 1)
            norms = norm_rows(norm_ref, slot_ref, block, count)
            out_ref[base + k : base + k + 1, :] = norms[FULL : FULL + 1, :]
            out_ref[base + per_shard : base + per_shard + 1, k * rows : (k + 1) * rows] = to_row(square_sums(query))


def first_dots_kernel(bounds, shards, per_shard, rows, shifts, slot_ref, shard_ref, query_ref, pool_ref, norm_ref, *refs):
    pool_norms(pool_ref, norm_ref, bounds)
    dots_kernel(shards, per_shard, rows, shifts, slot_ref, shard_ref, query_ref, pool_ref, norm_ref, *refs)


def prefix_dots(bounds, rows, block, query_ref, cand_ref, count):
    dots = None
    for low, high in bounds:
        query = query_ref[pl.ds(block * rows, rows), low:high]
        cand = cand_ref[:, :, low:high]
        part = contract(query, cand.reshape(count * PBLK, high - low), 1, 1)
        dots = part if dots is None else dots + part
        yield dots


def low_kernel(
    bounds, rows, slot_ref, shard_ref, query_ref, pool_ref, norm_ref, ids_ref, pos_ref,
    coef_hbm, row_ref, col_ref, loss_ref, cand_ref, term_ref, coef_ref, sem,
):
    count = cand_ref.shape[0]
    levels = len(bounds)
    cands = coef_hbm.shape[2]

    @pl.when(shard_ref[0] == 0)
    def _():
        row_ref[...] = jnp.zeros_like(row_ref)
        col_ref[...] = jnp.zeros_like(col_ref)

        def step(block, carry):
            take_blocks(pool_ref, slot_ref, block, count, cand_ref)
            pp = norm_rows(norm_ref, slot_ref, block, count)
            ids = ids_ref[pl.ds(block, 1), :]
            live = ids >= 0.0
            labels = jnp.where(ids == to_col(pos_ref[pl.ds(block, 1), :]), 1.0, 0.0)
            here = pl.ds(block * rows, rows)
            qq = jnp.zeros((rows, 1), F32)
            entropy = jnp.zeros((rows, 1), F32)
            logit_sum = jnp.zeros((rows, cands), F32)
            row_terms, col_terms = [], []
            sums = prefix_dots(bounds, rows, block, query_ref, cand_ref, count)
            for level, ((low, high), dots) in enumerate(zip(bounds, sums)):
                qq = qq + square_sums(query_ref[here, low:high])
                coef, row, col, part, logits = terms(
                    dots, qq, pp[level : level + 1, :], live, labels, float(high // MINP)
                )
                term_ref[level] = coef
                row_terms.append(row)
                col_terms.append(col)
                entropy = entropy + part
                logit_sum = logit_sum + logits
            loss = entropy - jnp.sum(labels * logit_sum, axis=1, keepdims=True)
            coef = jnp.zeros((rows, cands), F32)
            row = jnp.zeros((rows, 1), F32)
            col = jnp.zeros((1, cands), F32)
            for level in reversed(range(levels)):
                coef = coef + term_ref[level]
                row = row + row_terms[level]
                col = col + col_terms[level]
                coef_ref[level, here, :] = coef
                row_ref[block, level : level + 1, :] = to_row(row)
                col_ref[block, level : level + 1, :] = col
            loss_ref[pl.ds(block, 1), :] = to_row(loss)
            pltpu.make_async_copy(coef_ref.at[:, here], coef_hbm.at[:, here], sem).start()
            return carry

        lax.fori_loop(0, loss_ref.shape[0], step, 0)
        pltpu.make_async_copy(coef_ref, coef_hbm, sem).wait()

    @pl.when(shard_ref[0] != 0)
    def _():
        loss_ref[...] = jnp.zeros_like(loss_ref)


def high_kernel(shards, per_shard, rows, weights, shard_ref, ids_ref, pos_ref, low_loss_ref, *refs):
    ins, outs = refs[:shards], refs[shards:]
    shard = shard_ref[0]
    base = per_shard * rows
    width = ids_ref.shape[1]
    in_half = [
        jnp.where(lax.rem(shard - shift + shards, shards) < shards // 2, 1.0, 0.0)
        for shift in range(shards)
    ]

    def total(span, keep):
        pieces = [ref[span, :] * scale if keep else ref[span, :] for ref, scale in zip(ins, in_half)]
        return (pieces[0] + pieces[1]) + (pieces[2] + pieces[3])

    below = slice(base, base + AUX)
    half_rows, half_cols, full_rows, full_cols, losses, coefs = [], [], [], [], [], []
    aux_half, aux_full = total(below, True), total(below, False)
    for k in range(per_shard):
        block = shard * per_shard + k
        ids = ids_ref[pl.ds(block, 1), :]
        live = ids >= 0.0
        labels = jnp.where(ids == to_col(pos_ref[pl.ds(block, 1), :]), 1.0, 0.0)
        span = slice(k * rows, (k + 1) * rows)
        results = []
        for keep, aux, weight in ((True, aux_half, weights[0]), (False, aux_full, weights[1])):
            qq = to_col(aux[per_shard : per_shard + 1, span])
            results.append(terms(total(span, keep), qq, aux[k : k + 1, :], live, labels, weight))
        (coef_h, row_h, col_h, part_h, logit_h), (coef_f, row_f, col_f, part_f, logit_f) = results
        loss = part_h + part_f - jnp.sum(labels * (logit_h + logit_f), axis=1, keepdims=True)
        coefs.append(((coef_h + coef_f).astype(BF16), coef_f.astype(BF16)))
        half_rows.append(to_row(row_h + row_f))
        full_rows.append(to_row(row_f))
        half_cols.append(col_h + col_f)
        full_cols.append(col_f)
        losses.append(to_row(loss))
    per_row = width // rows
    low = [
        jnp.concatenate([low_loss_ref[r * per_row + j : r * per_row + j + 1, :] for j in range(per_row)], axis=1)
        for r in range(low_loss_ref.shape[0] // per_row)
    ]

    def aux_rows(rows_list, cols_list):
        line = jnp.concatenate(rows_list + losses, axis=1)
        table = jnp.concatenate(cols_list + [line] + low, axis=0)
        table = jnp.concatenate([table, jnp.zeros((AUX - table.shape[0], width), F32)], axis=0)
        first = table.astype(BF16).astype(F32)
        second = (table - first).astype(BF16).astype(F32)
        third = table - first - second
        return jnp.concatenate([first, second, third, jnp.zeros_like(table)], axis=0).astype(BF16)

    aux = (aux_rows(half_rows, half_cols), aux_rows(full_rows, full_cols))
    for shift in range(shards):
        out_ref = outs[shift]
        high_target = lax.rem(shard + shift, shards) >= shards // 2
        for which, chosen in ((1, high_target), (0, jnp.logical_not(high_target))):

            @pl.when(chosen)
            def _():
                for k in range(per_shard):
                    out_ref[k * rows : (k + 1) * rows, :] = coefs[k][which]
                out_ref[base : base + COEF_AUX, :] = aux[which]


def unpack_aux(ref, base):
    packed = ref[base : base + COEF_AUX, :].astype(F32)
    return packed[:AUX] + packed[AUX : 2 * AUX] + packed[2 * AUX : 3 * AUX]


def passage_kernel(
    bounds, shards, per_shard, rows, slot_ref, shard_ref, query_ref, pool_ref, low_col_ref, low_coef_hbm, *refs
):
    ins = refs[:shards]
    out_hbm, half_hbm, coef_ref, col_ref, spread_ref, scale_ref, out_ref, half_ref, low_coef_ref = refs[shards:-3]
    out_sem, half_sem, low_sem = refs[-3:]
    shard = shard_ref[0]
    base = per_shard * rows
    blocks = shards * per_shard
    slots, _, width = pool_ref.shape
    cands = coef_ref.shape[1]
    count = cands // PBLK

    load = pltpu.make_async_copy(low_coef_hbm, low_coef_ref, low_sem)

    @pl.when(shard == 0)
    def _():
        load.start()

    spread_ref[...] = jnp.zeros_like(spread_ref)
    scale_ref[...] = jnp.zeros_like(scale_ref)
    for shift in range(shards):
        source = lax.rem(shard - shift + shards, shards)
        coef_ref[pl.ds(source * base, base), :] = ins[shift][:base, :]
        aux = unpack_aux(ins[shift], base)
        for k in range(per_shard):
            col_ref[source * per_shard + k] = aux[k : k + 1, :]

    def run(spans, low):
        for block in range(blocks):
            cols = jnp.broadcast_to(col_ref[block], (8, cands))
            if low:
                cols = cols + low_col_ref[block]
            col_cols = columns(cols)
            for n in range(count):
                slot = slot_ref[block * count + n]
                scale_ref[slot] = scale_ref[slot] + col_cols[n * PBLK : (n + 1) * PBLK, :]
        for level, (lo, hi) in enumerate(spans):
            for block in range(blocks):
                here = pl.ds(block * rows, rows)
                coef = coef_ref[here, :].astype(F32)
                if low:
                    coef = coef + low_coef_ref[level, here, :]
                    half_ref[level, here, :] = coef.astype(BF16)
                turned = coef.T.astype(BF16)
                for n in range(count):
                    spread_ref[slot_ref[block * count + n], :, block * rows : (block + 1) * rows] = turned[
                        n * PBLK : (n + 1) * PBLK, :
                    ]
            spread = spread_ref[0:slots].reshape(slots * PBLK, blocks * rows)
            scale = scale_ref[0:slots].reshape(slots * PBLK, LANES)[:, level : level + 1]
            for start in range(lo, hi, PIECE):
                end = min(start + PIECE, hi)
                grad = contract(spread, query_ref[:, start:end], 1, 0)
                pool = pool_ref[:, :, start:end].reshape(slots * PBLK, end - start).astype(F32)
                out_ref[:, :, start:end] = (grad - scale * pool).astype(BF16).reshape(slots, PBLK, end - start)
                if end % LANES == 0:
                    done = pl.ds(start // LANES * LANES, end - start // LANES * LANES)
                    pltpu.make_async_copy(out_ref.at[:, :, done], out_hbm.at[:, :, done], out_sem).start()
        if low:
            copy = pltpu.make_async_copy(half_ref, half_hbm, half_sem)
            copy.start()
            copy.wait()
        pltpu.make_async_copy(out_ref, out_hbm, out_sem).wait()

    @pl.when(shard == 0)
    def _():
        load.wait()
        run(bounds, True)

    @pl.when(shard != 0)
    def _():
        run([(0, width)], False)


def query_kernel(
    bounds, shards, per_shard, rows, loss_scale, slot_ref, shard_ref, query_ref, pool_ref, low_row_ref,
    low_half_hbm, *refs,
):
    ins = refs[:shards]
    query_grad_ref, loss_ref = refs[shards : shards + 2]
    cand_ref, coef_ref, row_ref, low_half_ref, sem = refs[shards + 2 :]
    shard = shard_ref[0]
    base = per_shard * rows
    blocks = shards * per_shard
    count = cand_ref.shape[0]
    width = query_ref.shape[1]
    cands = coef_ref.shape[1]

    copy = pltpu.make_async_copy(low_half_hbm, low_half_ref, sem)

    @pl.when(shard == 0)
    def _():
        copy.start()

    loss_low = jnp.zeros((AUX, cands), F32)
    for shift in range(shards):
        source = lax.rem(shard - shift + shards, shards)
        coef_ref[pl.ds(source * base, base), :] = ins[shift][:base, :]
        aux = unpack_aux(ins[shift], base)
        for k in range(per_shard):
            row_ref[source * per_shard + k] = aux[per_shard : per_shard + 1, k * rows : (k + 1) * rows]
        loss_ref[pl.ds(source, 1), :] = aux[per_shard : per_shard + 1, base:]
        loss_low = loss_low + jnp.where(source == 0, aux, 0.0)
    per_row = cands // base
    for r in range(shards):
        low = loss_low[per_shard + 1 + r // per_row : per_shard + 2 + r // per_row, :]
        low = low[:, (r % per_row) * base : (r % per_row + 1) * base]
        loss_ref[r : r + 1, :] = (loss_ref[r : r + 1, :] + low) * loss_scale

    def run(spans, low):
        def step(block, carry):
            take_blocks(pool_ref, slot_ref, block, count, cand_ref)
            rows_here = jnp.broadcast_to(row_ref[block], (8, rows))
            if low:
                rows_here = rows_here + low_row_ref[block]
            row_cols = columns(rows_here)
            here = pl.ds(block * rows, rows)
            for level, (lo, hi) in enumerate(spans):
                coef = low_half_ref[level, here, :] if low else coef_ref[here, :]
                query = query_ref[here, lo:hi].astype(F32)
                cand = cand_ref[:, :, lo:hi].reshape(cands, hi - lo)
                grad = contract(coef, cand, 1, 0) - row_cols[:rows, level : level + 1] * query
                query_grad_ref[here, lo:hi] = grad.astype(BF16)
            return carry

        lax.fori_loop(0, blocks, step, 0)

    @pl.when(shard == 0)
    def _():
        copy.wait()
        run(bounds, True)

    @pl.when(shard != 0)
    def _():
        run([(0, width)], False)


def collect_kernel(target_ref, back_ref, out_ref):
    rows = out_ref.shape[0]
    here = lax.broadcasted_iota(jnp.int32, (rows, target_ref.shape[1]), 0)
    choose = jnp.where(here == target_ref[...], 1.0, 0.0).astype(BF16)
    out_ref[...] = contract(choose, back_ref[...], 1, 0).astype(BF16)


def per_device(queries, passages, neg_lists, positives):
    peers = lax.axis_size("dp")
    shards = lax.axis_size("tensor")
    total_rows, width = queries.shape
    blocks = neg_lists.shape[0] // peers
    count = neg_lists.shape[1]
    rows = total_rows // blocks
    local_blocks = passages.shape[0] // PBLK
    cands = count * PBLK
    per_shard = blocks // shards
    base = per_shard * rows
    slots = peers
    my_index = lax.axis_index("dp")
    shard = lax.axis_index("tensor")
    sizes = [MINP * 2**level for level in range(NPRE)]
    low_sizes = [size for size in sizes if size <= width]
    high_sizes = [size for size in sizes if size > width]
    assert high_sizes == [width * shards // 2, width * shards] and low_sizes[-1] == width
    assert shards == 4 and base == LANES and len(low_sizes) == FULL + 1
    bounds = list(zip([0] + low_sizes[:-1], low_sizes))
    levels = len(bounds)
    weight_total = sum(size / MINP for size in sizes)

    flat = neg_lists.reshape(peers, blocks * count)
    mine = (flat >= 0) & (flat // local_blocks == my_index)
    wanted = jnp.max(jnp.where(mine, flat % local_blocks, -1), axis=1)
    own = lax.dynamic_slice_in_dim(neg_lists, my_index * blocks, blocks, 0)
    valid = own >= 0
    slot = jnp.where(valid, own // local_blocks, 0).reshape(blocks * count)
    spare_slot = jnp.where(valid, own // local_blocks, slots).reshape(blocks * count)
    within = jnp.arange(PBLK, dtype=jnp.int32)
    ids = jnp.where(valid[:, :, None], own[:, :, None] * PBLK + within[None, None, :], -1)
    ids = ids.reshape(blocks, cands).astype(F32)
    target = jnp.where(wanted[:, None] >= 0, wanted[:, None] * PBLK + within[None, :], -1).reshape(1, slots * PBLK)
    pos = positives.reshape(blocks, rows).astype(F32)
    shard_arr = shard.reshape(1).astype(jnp.int32)
    pool_shape = (slots, PBLK, width)

    panels = pl.pallas_call(
        pack_kernel,
        out_shape=pltpu.HBM(pool_shape, BF16),
        in_specs=[smem(), hbm()],
        out_specs=hbm(),
        scratch_shapes=[pltpu.SemaphoreType.DMA(())],
        compiler_params=params(),
        name="pack",
    )(wanted, pltpu.with_memory_space_constraint(passages.reshape(local_blocks, PBLK, width), pltpu.HBM))
    pool = lax.all_to_all(panels, "dp", split_axis=0, concat_axis=0, tiled=True)

    def shift_by(part, s):
        return lax.ppermute(part, "tensor", [(i, (i + s) % shards) for i in range(shards)])

    cand_scratch = pltpu.VMEM((count, PBLK, width), BF16)
    message = jax.ShapeDtypeStruct((base + AUX, cands), F32)
    norms, far = pl.pallas_call(
        partial(first_dots_kernel, bounds, shards, per_shard, rows, (2,)),
        out_shape=[jax.ShapeDtypeStruct((slots, PBLK, LANES), F32), message],
        in_specs=[smem(), smem(), vmem(), vmem()],
        out_specs=[vmem()] * 2,
        scratch_shapes=[cand_scratch],
        compiler_params=params(),
        name="dots_far",
    )(slot, shard_arr, queries, pool)

    def more_dots(shifts, name):
        return pl.pallas_call(
            partial(dots_kernel, shards, per_shard, rows, shifts),
            out_shape=[message] * len(shifts),
            in_specs=[smem(), smem(), vmem(), vmem(), vmem()],
            out_specs=[vmem()] * len(shifts),
            scratch_shapes=[cand_scratch],
            compiler_params=params(),
            name=name,
        )(slot, shard_arr, queries, pool, norms)

    right, left = more_dots((1, 3), "dots_near")
    (here,) = more_dots((0,), "dots_own")
    arrived = [here, shift_by(right, 1), shift_by(far, 2), shift_by(left, 3)]
    low_coef, low_row, low_col, low_loss = pl.pallas_call(
        partial(low_kernel, bounds, rows),
        out_shape=[
            pltpu.HBM((levels, total_rows, cands), F32),
            jax.ShapeDtypeStruct((blocks, 8, rows), F32),
            jax.ShapeDtypeStruct((blocks, 8, cands), F32),
            jax.ShapeDtypeStruct((blocks, rows), F32),
        ],
        in_specs=[smem(), smem()] + [vmem()] * 5,
        out_specs=[hbm()] + [vmem()] * 3,
        scratch_shapes=[
            cand_scratch,
            pltpu.VMEM((levels, rows, cands), F32),
            pltpu.VMEM((levels, total_rows, cands), F32),
            pltpu.SemaphoreType.DMA(()),
        ],
        compiler_params=params(),
        name="low",
    )(slot, shard_arr, queries, pool, norms, ids, pos)

    coefs = pl.pallas_call(
        partial(high_kernel, shards, per_shard, rows, [size / MINP for size in high_sizes]),
        out_shape=[jax.ShapeDtypeStruct((base + COEF_AUX, cands), BF16)] * shards,
        in_specs=[smem()] + [vmem()] * (3 + shards),
        out_specs=[vmem()] * shards,
        compiler_params=params(),
        name="high",
    )(shard_arr, ids, pos, low_loss, *arrived)
    coefs = [coefs[0]] + [shift_by(coefs[s], s) for s in range(1, shards)]

    slot_grad, low_half = pl.pallas_call(
        partial(passage_kernel, bounds, shards, per_shard, rows),
        out_shape=[pltpu.HBM(pool_shape, BF16), pltpu.HBM((levels, total_rows, cands), BF16)],
        in_specs=[smem(), smem()] + [vmem()] * 3 + [hbm()] + [vmem()] * shards,
        out_specs=[hbm()] * 2,
        scratch_shapes=[
            pltpu.VMEM((total_rows, cands), BF16),
            pltpu.VMEM((blocks, 1, cands), F32),
            pltpu.VMEM((slots + 1, PBLK, total_rows), BF16),
            pltpu.VMEM((slots + 1, PBLK, LANES), F32),
            pltpu.VMEM(pool_shape, BF16),
            pltpu.VMEM((levels, total_rows, cands), BF16),
            pltpu.VMEM((levels, total_rows, cands), F32),
            pltpu.SemaphoreType.DMA(()),
            pltpu.SemaphoreType.DMA(()),
            pltpu.SemaphoreType.DMA(()),
        ],
        compiler_params=params(),
        name="passage",
    )(
        spare_slot, shard_arr, queries, pool, low_col,
        pltpu.with_memory_space_constraint(low_coef, pltpu.HBM), *coefs,
    )
    back = lax.all_to_all(slot_grad, "dp", split_axis=0, concat_axis=0, tiled=True)

    query_grad, loss = pl.pallas_call(
        partial(query_kernel, bounds, shards, per_shard, rows, 1.0 / weight_total),
        out_shape=[
            jax.ShapeDtypeStruct((total_rows, width), BF16),
            jax.ShapeDtypeStruct((shards, base), F32),
        ],
        in_specs=[smem(), smem()] + [vmem()] * 3 + [hbm()] + [vmem()] * shards,
        out_specs=[vmem()] * 2,
        scratch_shapes=[
            cand_scratch,
            pltpu.VMEM((total_rows, cands), BF16),
            pltpu.VMEM((blocks, 1, rows), F32),
            pltpu.VMEM((levels, total_rows, cands), BF16),
            pltpu.SemaphoreType.DMA(()),
        ],
        compiler_params=params(),
        name="query",
    )(
        slot, shard_arr, queries, pool, low_row,
        pltpu.with_memory_space_constraint(low_half, pltpu.HBM), *coefs,
    )

    passage_grad = pl.pallas_call(
        collect_kernel,
        out_shape=jax.ShapeDtypeStruct((local_blocks * PBLK, width), BF16),
        in_specs=[vmem(), vmem()],
        out_specs=vmem(),
        compiler_params=params(),
        name="collect",
    )(target, back.reshape(slots * PBLK, width))
    return (
        query_grad,
        passage_grad,
        loss.reshape(total_rows),
    )


def solution(mesh):
    return jax.shard_map(
        per_device,
        mesh=mesh,
        in_specs=(P("dp", "tensor"), P("dp", "tensor"), P(), P("dp")),
        out_specs=(P("dp", "tensor"), P("dp", "tensor"), P("dp")),
        check_vma=False,
    )
```

time: 165 us -> 226 us (1.37)
  Pallas kernels: 25.6 us -> 94.1 us
  blocking collectives: 58.8 us -> 0 us
  waiting for transfers between devices: 53.3 us -> 98.6 us
  starting transfers between devices: 20.9 us -> 28.9 us
    pallas_call x5 -> x8, Pallas kernels: 25.1 us -> 92.9 us  [the longest x1 65.2 us: per_device(): pl.pallas_call(pack_kernel, out_shape=pltpu.HBM(pool_shape, BF16), in_spe...]
    all_to_all x1 -> x0, blocking collectives: 58.8 us -> none  [per_device(): lax.all_to_all(slot_grad.reshape(slots, PBLK, width), 'dp', split_axis=0,...]
    all_to_all x0 -> x1, waiting for transfers between devices: none -> 45.1 us  [per_device(): lax.all_to_all(slot_grad, 'dp', split_axis=0, concat_axis=0, tiled=True)]
    all_to_all x0 -> x1, starting transfers between devices: none -> 8 us  [per_device(): lax.all_to_all(slot_grad, 'dp', split_axis=0, concat_axis=0, tiled=True)]
  transfers between devices with their start and end apart: 7 -> 8, of which waited for: 3 -> 4; matrix products, arithmetic and copies ran while one was open for 1% -> 1% of each run, Pallas kernels for 5% -> 6%
where the time goes in v1:
time: 226 us
  waiting for transfers between devices  98.6 us (44%)
  Pallas kernels  94.1 us (42%)
  starting transfers between devices  28.9 us (13%)
  local copies, waits for them, and re-layouts  2.31 us (1%)
    pallas_call x1, Pallas kernels, per_device(): pl.pallas_call(pack_kernel, out_shape=pltpu.HBM(pool_shape, BF16), in_spe...  65.2 us
    all_to_all x1, waiting for transfers between devices, per_device(): pool = lax.all_to_all(panels, 'dp', split_axis=0, concat_axis=0, tiled=True)  49.7 us
    all_to_all x1, waiting for transfers between devices, per_device(): lax.all_to_all(slot_grad, 'dp', split_axis=0, concat_axis=0, tiled=True)  45.1 us
    all_to_all x1, starting transfers between devices, per_device(): pool = lax.all_to_all(panels, 'dp', split_axis=0, concat_axis=0, tiled=True)  13.3 us
    all_to_all x1, starting transfers between devices, per_device(): lax.all_to_all(slot_grad, 'dp', split_axis=0, concat_axis=0, tiled=True)  8 us
    ppermute x6, starting transfers between devices, shift_by(): lax.ppermute(part, 'tensor', [(i, (i + s) % shards) for i in range(shards)])  7.57 us
    pallas_call x1, Pallas kernels, per_device(): pl.pallas_call(partial(passage_kernel, bounds, shards, per_shard, rows),...  7.42 us
    pallas_call x1, Pallas kernels, per_device(): pl.pallas_call(partial(low_kernel, bounds, rows), out_shape=[pltpu.HBM((l...  6.04 us
  transfers between devices with their start and end apart: 8, of which 4 were waited for; matrix products, arithmetic and copies ran while one was open for 1% of the time, Pallas kernels for 6%

profile of v1, /device:TPU:1, one launch (start us, length us, event | category | flops | bytes accessed | tf_op | source)
XLA Modules:
  0.0 225.7 jit_solution(17103119102385352023)
XLA Ops:
  0.6 0.8 fusion.2
  1.4 0.1 reduce_max.14
  1.5 0.1 reduce_max.18.wanted_ref
  1.7 65.2 %pack.1 = bf16[64,16,1024]{2,1,0:T(8,128)(2,1)} custom-call(s32[64]{0:T(128)S(1)} %reduce_max.18.wanted_ref, bf16[16,16,1024]{2,1,0:T(8,128)(2,1)} %bitcast.4), custom_call_target="tpu_custom_call" | custom-call | tf_op jit(solution)/shard_map/pack/pallas_call | solution.py:465
  66.9 0.0 copy-start.3
  66.9 0.0 copy-start
  66.9 13.3 %all-to-all-start = ((bf16[64,16,1024]{2,1,0:T(8,128)(2,1)}), bf16[64,16,1024]{2,1,0:T(8,128)(2,1)S(1)}, u32[]{:S(2)}, u32[]{:S(2)}) async-start(bf16[64,16,1024]{2,1,0:T(8,128)(2,1)} %pack.1), calls=%async_computation | async-start | bytes 4194304 | tf_op jit(solution)/shard_map/all_to_all | solution.py:474
  80.2 0.8 constant_dynamic-slice_fusion
  81.0 0.1 copy.16
  81.1 0.1 reshape.80.slot_ref
  81.1 0.1 broadcast_in_dim.39
  81.2 0.1 broadcast_in_dim.40
  81.3 0.1 add.56
  81.4 0.1 add.57
  81.5 0.1 add.59
  81.6 0.0 copy-done.3
  81.6 0.1 convert_element_type.10.pos_ref
  81.7 49.7 %all-to-all-done.pool_ref = bf16[64,16,1024]{2,1,0:T(8,128)(2,1)S(1)} async-done(((bf16[64,16,1024]{2,1,0:T(8,128)(2,1)}), bf16[64,16,1024]{2,1,0:T(8,128)(2,1)S(1)}, u32[]{:S(2)}, u32[]{:S(2)}) %all-to-all-start) | async-done | bytes 2097184 | tf_op jit(solution)/shard_map/all_to_all | solution.py:474
  131.4 0.0 copy-done
  131.4 2.9 %dots_far.1 = (f32[64,16,128]{2,1,0:T(8,128)S(1)}, f32[136,256]{1,0:T(8,128)S(1)}) custom-call(s32[128]{0:T(128)S(1)} %reshape.80.slot_ref, s32[1]{0:T(128)} %bitcast.shard_ref, bf16[512,1024]{1,0:T(8,128)(2,1)S(1)} %copy-done, bf16[64,16,1024]{2,1,0:T(8,128)(2,1)S(1)} %all-to-all-done.pool_ref), custom_call_target="tpu_custom_call" | custom-call | tf_op jit(solution)/shard_map/dots_far/pallas_call | solution.py:481
  134.4 1.3 dots_near.1
  135.7 1.3 collective-permute-start
  137.0 2.5 %collective-permute-start.1 = (f32[136,256]{1,0:T(8,128)S(1)}, f32[136,256]{1,0:T(8,128)S(1)}, u32[]{:S(2)}, u32[]{:S(2)}) collective-permute-start(f32[136,256]{1,0:T(8,128)S(1)} %get-tuple-element.25), channel_id=1, source_target_pairs={{0,2},{1,3},{2,0},{3,1},{4,6},{5,7},{6,4},{7,5},{8,10},{9,11},{10,... | collective-permute-start | bytes 417800 | tf_op jit(solution)/shard_map/ppermute | solution.py:477
  139.4 1.2 collective-permute-start.2
  140.6 1.0 dots_own.1.refs_0_
  141.6 6.0 %low.1 = (f32[5,512,256]{2,1,0:T(8,128)}, f32[8,8,64]{2,1,0:T(8,128)S(1)}, f32[8,8,256]{2,1,0:T(8,128)S(1)}, f32[8,64]{1,0:T(8,128)S(1)}) custom-call(s32[128]{0:T(128)S(1)} %reshape.80.slot_ref, s32[1]{0:T(128)} %bitcast.shard_ref, bf16[512,1024]{1,0:T(8,128)(2,1)S(1)} %copy-done, bf16[64,16,1024]{2,1,0:T(8,128)(2,1)S(1)} %all-to-all-done.pool_ref, ...), custom_call_target="tpu_custom_call" | custom-call | tf_op jit(solution)/shard_map/low/pallas_call | solution.py:505
  147.6 0.0 copy-start.1
  147.7 0.6 copy-done.1
  148.3 0.0 collective-permute-done.refs_1_
  148.3 0.0 collective-permute-done.1.refs_2_
  148.3 0.0 collective-permute-done.2.refs_3_
  148.3 1.2 high.1
  149.5 0.0 collective-permute-start.3
  149.5 0.8 collective-permute-start.4
  150.3 1.9 collective-permute-start.5
  152.2 0.1 reshape.83.slot_ref
  152.3 2.8 %collective-permute-done.3.refs_1_ = bf16[160,256]{1,0:T(8,128)(2,1)S(1)} collective-permute-done((bf16[160,256]{1,0:T(8,128)(2,1)}, bf16[160,256]{1,0:T(8,128)(2,1)S(1)}, u32[]{:S(2)}, u32[]{:S(2)}) %collective-permute-start.3) | collective-permute-done | bytes 81952 | tf_op jit(solution)/shard_map/ppermute | solution.py:477
  155.1 0.0 collective-permute-done.4.refs_2_
  155.1 0.9 collective-permute-done.5.refs_3_
  156.0 7.4 %passage.1 = (bf16[64,16,1024]{2,1,0:T(8,128)(2,1)}, bf16[5,512,256]{2,1,0:T(8,128)(2,1)}) custom-call(s32[128]{0:T(128)S(1)} %reshape.83.slot_ref, s32[1]{0:T(128)} %bitcast.shard_ref, bf16[512,1024]{1,0:T(8,128)(2,1)S(1)} %copy-done, bf16[64,16,1024]{2,1,0:T(8,128)(2,1)S(1)} %all-to-all-done.pool_ref, f32[8,8,256]{2,1,0:T(8,128)S(1)} %get-tuple-element.21.low_col_ref, ...), custom_call_target="tpu_custom_call" | custom-call | tf_op jit(solution)/shard_map/passage/pallas_call | solution.py:535
  163.4 0.0 copy-start.2
  163.4 8.0 %all-to-all-start.1 = ((bf16[64,16,1024]{2,1,0:T(8,128)(2,1)}), bf16[64,16,1024]{2,1,0:T(8,128)(2,1)}, u32[]{:S(2)}, u32[]{:S(2)}) async-start(bf16[64,16,1024]{2,1,0:T(8,128)(2,1)} %get-tuple-element.33), calls=%async_computation.1 | async-start | bytes 4194304 | tf_op jit(solution)/shard_map/all_to_all | solution.py:558
  171.4 0.1 add_select_fusion.2
  171.5 0.1 select_n.63.target_ref
  171.6 0.0 copy-done.2
  171.6 5.9 %query.1 = (bf16[512,1024]{1,0:T(8,128)(2,1)}, f32[4,128]{1,0:T(4,128)}) custom-call(s32[128]{0:T(128)S(1)} %reshape.80.slot_ref, s32[1]{0:T(128)} %bitcast.shard_ref, bf16[512,1024]{1,0:T(8,128)(2,1)S(1)} %copy-done, bf16[64,16,1024]{2,1,0:T(8,128)(2,1)S(1)} %all-to-all-done.pool_ref, f32[8,8,64]{2,1,0:T(8,128)S(1)} %copy-done.2, ...), custom_call_target="tpu_custom_call" | custom-call | tf_op jit(solution)/shard_map/query/pallas_call | solution.py:560
  177.5 45.1 %all-to-all-done.1 = bf16[64,16,1024]{2,1,0:T(8,128)(2,1)} async-done(((bf16[64,16,1024]{2,1,0:T(8,128)(2,1)}), bf16[64,16,1024]{2,1,0:T(8,128)(2,1)}, u32[]{:S(2)}, u32[]{:S(2)}) %all-to-all-start.1) | async-done | bytes 2097184 | tf_op jit(solution)/shard_map/all_to_all | solution.py:558
  222.6 3.1 %collect.1 = bf16[256,1024]{1,0:T(8,128)(2,1)} custom-call(s32[1,1024]{1,0:T(1,128)S(1)} %select_n.63.target_ref, bf16[1024,1024]{1,0:T(8,128)(2,1)} %bitcast.2.back_ref), custom_call_target="tpu_custom_call" | custom-call | tf_op jit(solution)/shard_map/collect/pallas_call | solution.py:582
  (7 shorter events, 0.0 us)
Async XLA Ops:
  66.9 14.8 %copy-start.3 = (s32[512]{0:T(512)S(1)}, s32[512]{0:T(512)}, u32[]{:S(2)}) copy-start(s32[512]{0:T(512)} %param.7) | copy-start | bytes 6148
  66.9 64.6 %copy-start = (bf16[512,1024]{1,0:T(8,128)(2,1)S(1)}, bf16[512,1024]{1,0:T(8,128)(2,1)}, u32[]{:S(2)}) copy-start(bf16[512,1024]{1,0:T(8,128)(2,1)} %query_ref.11) | copy-start | bytes 3145732
  66.9 64.6 %all-to-all-start = ((bf16[64,16,1024]{2,1,0:T(8,128)(2,1)}), bf16[64,16,1024]{2,1,0:T(8,128)(2,1)S(1)}, u32[]{:S(2)}, u32[]{:S(2)}) async-start(bf16[64,16,1024]{2,1,0:T(8,128)(2,1)} %pack.1), calls=%async_computation | async-start | bytes 4194304 | tf_op jit(solution)/shard_map/all_to_all | solution.py:474
  135.7 12.6 %collective-permute-start = (f32[136,256]{1,0:T(8,128)S(1)}, f32[136,256]{1,0:T(8,128)S(1)}, u32[]{:S(2)}, u32[]{:S(2)}) collective-permute-start(f32[136,256]{1,0:T(8,128)S(1)} %get-tuple-element.24), channel_id=1, source_target_pairs={{0,1},{1,2},{2,3},{3,0},{4,5},{5,6},{6,7},{7,4},{8,9},{9,10},{10,1... | collective-permute-start | bytes 417800 | tf_op jit(solution)/shard_map/ppermute | solution.py:477
  137.0 11.3 %collective-permute-start.1 = (f32[136,256]{1,0:T(8,128)S(1)}, f32[136,256]{1,0:T(8,128)S(1)}, u32[]{:S(2)}, u32[]{:S(2)}) collective-permute-start(f32[136,256]{1,0:T(8,128)S(1)} %get-tuple-element.25), channel_id=1, source_target_pairs={{0,2},{1,3},{2,0},{3,1},{4,6},{5,7},{6,4},{7,5},{8,10},{9,11},{10,... | collective-permute-start | bytes 417800 | tf_op jit(solution)/shard_map/ppermute | solution.py:477
  139.4 8.8 %collective-permute-start.2 = (f32[136,256]{1,0:T(8,128)S(1)}, f32[136,256]{1,0:T(8,128)S(1)}, u32[]{:S(2)}, u32[]{:S(2)}) collective-permute-start(f32[136,256]{1,0:T(8,128)S(1)} %get-tuple-element.26), channel_id=1, source_target_pairs={{0,3},{1,0},{2,1},{3,2},{4,7},{5,4},{6,5},{7,6},{8,11},{9,8},{10,9... | collective-permute-start | bytes 417800 | tf_op jit(solution)/shard_map/ppermute | solution.py:477
  147.6 0.6 copy-start.1
  149.5 5.6 %collective-permute-start.3 = (bf16[160,256]{1,0:T(8,128)(2,1)}, bf16[160,256]{1,0:T(8,128)(2,1)S(1)}, u32[]{:S(2)}, u32[]{:S(2)}) collective-permute-start(bf16[160,256]{1,0:T(8,128)(2,1)} %get-tuple-element.28), channel_id=1, source_target_pairs={{0,1},{1,2},{2,3},{3,0},{4,5},{5,6},{6,7},{7,4},{8,9},{9,10},{10,1... | collective-permute-start | bytes 245768 | tf_op jit(solution)/shard_map/ppermute | solution.py:477
  149.5 5.6 %collective-permute-start.4 = (bf16[160,256]{1,0:T(8,128)(2,1)}, bf16[160,256]{1,0:T(8,128)(2,1)S(1)}, u32[]{:S(2)}, u32[]{:S(2)}) collective-permute-start(bf16[160,256]{1,0:T(8,128)(2,1)} %get-tuple-element.29), channel_id=1, source_target_pairs={{0,2},{1,3},{2,0},{3,1},{4,6},{5,7},{6,4},{7,5},{8,10},{9,11},{10,... | collective-permute-start | bytes 245768 | tf_op jit(solution)/shard_map/ppermute | solution.py:477
  150.3 5.7 %collective-permute-start.5 = (bf16[160,256]{1,0:T(8,128)(2,1)}, bf16[160,256]{1,0:T(8,128)(2,1)S(1)}, u32[]{:S(2)}, u32[]{:S(2)}) collective-permute-start(bf16[160,256]{1,0:T(8,128)(2,1)} %get-tuple-element.30), channel_id=1, source_target_pairs={{0,3},{1,0},{2,1},{3,2},{4,7},{5,4},{6,5},{7,6},{8,11},{9,8},{10,9... | collective-permute-start | bytes 245768 | tf_op jit(solution)/shard_map/ppermute | solution.py:477
  163.4 8.2 %copy-start.2 = (f32[8,8,64]{2,1,0:T(8,128)S(1)}, f32[8,8,64]{2,1,0:T(8,128)}, u32[]{:S(2)}) copy-start(f32[8,8,64]{2,1,0:T(8,128)} %copy-done.1) | copy-start | bytes 49156
  163.4 59.2 %all-to-all-start.1 = ((bf16[64,16,1024]{2,1,0:T(8,128)(2,1)}), bf16[64,16,1024]{2,1,0:T(8,128)(2,1)}, u32[]{:S(2)}, u32[]{:S(2)}) async-start(bf16[64,16,1024]{2,1,0:T(8,128)(2,1)} %get-tuple-element.33), calls=%async_computation.1 | async-start | bytes 4194304 | tf_op jit(solution)/shard_map/all_to_all | solution.py:558

commit v2 on v1

v2 whole, which is shorter than its diff:
```python
from functools import partial

import jax
import jax.numpy as jnp
from jax import lax
from jax.experimental import pallas as pl
from jax.experimental.pallas import tpu as pltpu
from jax.sharding import PartitionSpec as P

MINP = 64
NPRE = 7
PBLK = 16

EPS = 1e-06
INV_TEMP = 20.0

F32 = jnp.float32
BF16 = jnp.bfloat16

AUX = 8
COEF_AUX = 32
LANES = 128
PIECE = 256


def vmem():
    return pl.BlockSpec(memory_space=pltpu.VMEM)


def smem():
    return pl.BlockSpec(memory_space=pltpu.SMEM)


def hbm():
    return pl.BlockSpec(memory_space=pltpu.HBM)


def params():
    return pltpu.CompilerParams(vmem_limit_bytes=20 * 2**20)


def contract(a, b, da, db):
    return lax.dot_general(a, b, (((da,), (db,)), ((), ())), preferred_element_type=F32)


def eye(n):
    return lax.broadcasted_iota(jnp.int32, (n, n), 0) == lax.broadcasted_iota(jnp.int32, (n, n), 1)


def to_col(row):
    return jnp.sum(jnp.where(eye(row.shape[1]), row, 0.0), axis=1, keepdims=True)


def to_row(col):
    return jnp.sum(jnp.where(eye(col.shape[0]), col, 0.0), axis=0, keepdims=True)


def square_sums(half):
    wide = half.astype(F32)
    return jnp.sum(wide * wide, axis=1, keepdims=True)


def columns(table):
    table = jnp.concatenate([table, jnp.zeros((8, LANES - table.shape[1]), F32)], axis=1) if table.shape[1] < LANES else table
    return jnp.concatenate([table, jnp.zeros((LANES - 8, table.shape[1]), F32)], axis=0).T


def terms(dots, qq_col, pp_row, live, labels, weight):
    a = lax.rsqrt(qq_col + EPS)
    b = jnp.where(live, lax.rsqrt(pp_row + EPS), 0.0)
    scale = (a * INV_TEMP) * b
    logits = dots * scale
    exponent = jnp.where(live, jnp.exp(logits), 0.0)
    total = jnp.sum(exponent, axis=1, keepdims=True)
    gradient = weight * (exponent * (1.0 / total) - labels)
    inner = gradient * logits
    row = (a * a) * jnp.sum(inner, axis=1, keepdims=True)
    col = (b * b) * jnp.sum(inner, axis=0, keepdims=True)
    return gradient * scale, row, col, weight * jnp.log(total), weight * logits


def take_blocks(pool_ref, slot_ref, block, count, out_ref):
    for n in range(count):
        out_ref[n] = pool_ref[slot_ref[block * count + n]]


def pool_norms(pool_ref, norm_ref, bounds):
    step_slots = 8
    lane = lax.broadcasted_iota(jnp.int32, (step_slots * PBLK, LANES), 1)

    def step(i, carry):
        here = pl.ds(i * step_slots, step_slots)
        block = pool_ref[here]
        wide = block.reshape(step_slots * PBLK, block.shape[2]).astype(F32)
        square = wide * wide
        total = jnp.zeros((step_slots * PBLK, 1), F32)
        result = jnp.zeros((step_slots * PBLK, LANES), F32)
        for level, (low, high) in enumerate(bounds):
            total = total + jnp.sum(square[:, low:high], axis=1, keepdims=True)
            result = jnp.where(lane == level, total, result)
        norm_ref[here] = result.reshape(step_slots, PBLK, LANES)
        return carry

    lax.fori_loop(0, pool_ref.shape[0] // step_slots, step, 0)


def norm_rows(norm_ref, slot_ref, block, count):
    table = jnp.concatenate([norm_ref[slot_ref[block * count + n]] for n in range(count)], axis=0)
    return table.T[:8, :]


def pack_kernel(wanted_ref, block_ref, out_ref, sem):
    def step(d, carry):
        source = block_ref.at[jnp.maximum(wanted_ref[d], 0)]
        pltpu.make_async_copy(source, out_ref.at[d], sem).start()
        return carry

    lax.fori_loop(0, out_ref.shape[0], step, 0, unroll=8)
    pltpu.make_async_copy(out_ref, out_ref, sem).wait()


def dots_kernel(shards, per_shard, rows, shifts, slot_ref, shard_ref, query_ref, pool_ref, norm_ref, *refs):
    outs, cand_ref = refs[:-1], refs[-1]
    count, _, width = cand_ref.shape
    shard = shard_ref[0]
    base = per_shard * rows
    for shift, out_ref in zip(shifts, outs):
        target = lax.rem(shard + shift, shards)
        for k in range(per_shard):
            block = target * per_shard + k
            take_blocks(pool_ref, slot_ref, block, count, cand_ref)
            query = query_ref[pl.ds(block * rows, rows), :]
            cand = cand_ref[...].reshape(count * PBLK, width)
            out_ref[k * rows : (k + 1) * rows, :] = contract(query, cand, 1, 1)
            out_ref[base + k : base + k + 1, :] = norm_rows(norm_ref, slot_ref, block, count)[0:1, :]
            out_ref[base + per_shard : base + per_shard + 1, k * rows : (k + 1) * rows] = to_row(square_sums(query))


def first_dots_kernel(shards, per_shard, rows, shifts, slot_ref, shard_ref, query_ref, pool_ref, norm_ref, *refs):
    pool_norms(pool_ref, norm_ref, [(0, pool_ref.shape[2])])
    dots_kernel(shards, per_shard, rows, shifts, slot_ref, shard_ref, query_ref, pool_ref, norm_ref, *refs)


def prefix_dots(bounds, rows, block, query_ref, cand_ref, count):
    dots = None
    for low, high in bounds:
        query = query_ref[pl.ds(block * rows, rows), low:high]
        cand = cand_ref[:, :, low:high]
        part = contract(query, cand.reshape(count * PBLK, high - low), 1, 1)
        dots = part if dots is None else dots + part
        yield dots


def low_kernel(
    bounds, rows, first, renorm, slot_ref, shard_ref, query_ref, pool_ref, ids_ref, pos_ref, norm_in_ref, after_ref,
    coef_hbm, row_ref, col_ref, loss_ref, norm_ref, cand_ref, term_ref, coef_ref, sem,
):
    del after_ref
    count = cand_ref.shape[0]
    levels, pairs, cands, _ = coef_ref.shape
    per_pair = LANES // rows

    @pl.when(shard_ref[0] == 0)
    def _():
        if renorm:
            pool_norms(pool_ref, norm_ref, bounds)
        norms = norm_ref if renorm else norm_in_ref
        row_ref[...] = jnp.zeros_like(row_ref)
        col_ref[...] = jnp.zeros_like(col_ref)

        def step(pair, carry):
            row_sums, col_sums = [], []
            for j in range(per_pair):
                local = pair * per_pair + j
                block = first + local
                take_blocks(pool_ref, slot_ref, block, count, cand_ref)
                pp = norm_rows(norms, slot_ref, block, count)
                ids = ids_ref[pl.ds(block, 1), :]
                live = ids >= 0.0
                labels = jnp.where(ids == to_col(pos_ref[pl.ds(block, 1), :]), 1.0, 0.0)
                here = pl.ds(block * rows, rows)
                qq = jnp.zeros((rows, 1), F32)
                entropy = jnp.zeros((rows, 1), F32)
                logit_sum = jnp.zeros((rows, cands), F32)
                sums = prefix_dots(bounds, rows, block, query_ref, cand_ref, count)
                for level, ((low, high), dots) in enumerate(zip(bounds, sums)):
                    qq = qq + square_sums(query_ref[here, low:high])
                    coef, row, col, part, logits = terms(
                        dots, qq, pp[level : level + 1, :], live, labels, float(high // MINP)
                    )
                    term_ref[level, j * rows : (j + 1) * rows, :] = coef
                    row_sums.append(row)
                    col_sums.append(col)
                    entropy = entropy + part
                    logit_sum = logit_sum + logits
                loss = entropy - jnp.sum(labels * logit_sum, axis=1, keepdims=True)
                loss_ref[pl.ds(local, 1), :] = to_row(loss)
                row = jnp.zeros((rows, 1), F32)
                col = jnp.zeros((1, cands), F32)
                for level in reversed(range(levels)):
                    row = row + row_sums[level]
                    col = col + col_sums[level]
                    row_ref[local, level : level + 1, :] = to_row(row)
                    col_ref[local, level : level + 1, :] = col
                row_sums, col_sums = [], []
            coef = jnp.zeros((LANES, cands), F32)
            for level in reversed(range(levels)):
                coef = coef + term_ref[level]
                coef_ref[level, pair] = coef.T
            pltpu.make_async_copy(coef_ref.at[:, pair], coef_hbm.at[:, pair], sem).start()
            return carry

        lax.fori_loop(0, pairs, step, 0)
        pltpu.make_async_copy(coef_ref, coef_hbm, sem).wait()

    @pl.when(shard_ref[0] != 0)
    def _():
        loss_ref[...] = jnp.zeros_like(loss_ref)


def high_kernel(shards, per_shard, rows, weights, shard_ref, ids_ref, pos_ref, after_ref, *refs):
    del after_ref
    ins, outs, loss_ref = refs[:shards], refs[shards:-1], refs[-1]
    shard = shard_ref[0]
    base = per_shard * rows
    width = ids_ref.shape[1]
    in_half = [
        jnp.where(lax.rem(shard - shift + shards, shards) < shards // 2, 1.0, 0.0)
        for shift in range(shards)
    ]

    def total(span, keep):
        pieces = [ref[span, :] * scale if keep else ref[span, :] for ref, scale in zip(ins, in_half)]
        return (pieces[0] + pieces[1]) + (pieces[2] + pieces[3])

    below = slice(base, base + AUX)
    half_rows, half_cols, full_rows, full_cols, losses, coefs = [], [], [], [], [], []
    aux_half, aux_full = total(below, True), total(below, False)
    for k in range(per_shard):
        block = shard * per_shard + k
        ids = ids_ref[pl.ds(block, 1), :]
        live = ids >= 0.0
        labels = jnp.where(ids == to_col(pos_ref[pl.ds(block, 1), :]), 1.0, 0.0)
        span = slice(k * rows, (k + 1) * rows)
        results = []
        for keep, aux, weight in ((True, aux_half, weights[0]), (False, aux_full, weights[1])):
            qq = to_col(aux[per_shard : per_shard + 1, span])
            results.append(terms(total(span, keep), qq, aux[k : k + 1, :], live, labels, weight))
        (coef_h, row_h, col_h, part_h, logit_h), (coef_f, row_f, col_f, part_f, logit_f) = results
        loss = part_h + part_f - jnp.sum(labels * (logit_h + logit_f), axis=1, keepdims=True)
        coefs.append(((coef_h + coef_f).astype(BF16), coef_f.astype(BF16)))
        half_rows.append(to_row(row_h + row_f))
        full_rows.append(to_row(row_f))
        half_cols.append(col_h + col_f)
        full_cols.append(col_f)
        losses.append(to_row(loss))
    loss_ref[...] = jnp.concatenate(losses, axis=1)

    def aux_rows(rows_list, cols_list):
        line = jnp.concatenate(rows_list + [jnp.zeros((1, width - base), F32)], axis=1)
        table = jnp.concatenate(cols_list + [line], axis=0)
        table = jnp.concatenate([table, jnp.zeros((AUX - table.shape[0], width), F32)], axis=0)
        first = table.astype(BF16).astype(F32)
        second = (table - first).astype(BF16).astype(F32)
        third = table - first - second
        return jnp.concatenate([first, second, third, jnp.zeros_like(table)], axis=0).astype(BF16)

    aux = (aux_rows(half_rows, half_cols), aux_rows(full_rows, full_cols))
    for shift in range(shards):
        out_ref = outs[shift]
        high_target = lax.rem(shard + shift, shards) >= shards // 2
        for which, chosen in ((1, high_target), (0, jnp.logical_not(high_target))):

            @pl.when(chosen)
            def _():
                for k in range(per_shard):
                    out_ref[k * rows : (k + 1) * rows, :] = coefs[k][which]
                out_ref[base : base + COEF_AUX, :] = aux[which]


def unpack_aux(ref, base):
    packed = ref[base : base + COEF_AUX, :].astype(F32)
    return packed[:AUX] + packed[AUX : 2 * AUX] + packed[2 * AUX : 3 * AUX]


def passage_kernel(
    bounds, shards, per_shard, rows, slot_ref, shard_ref, query_ref, pool_ref, low_col_a_ref, low_col_b_ref,
    low_coef_a_hbm, low_coef_b_hbm, *refs
):
    ins = refs[:shards]
    out_hbm, half_hbm, turned_ref, col_ref, spread_ref, scale_ref, out_ref, half_ref, low_coef_ref = refs[shards:-3]
    out_sem, half_sem, low_sem = refs[-3:]
    shard = shard_ref[0]
    base = per_shard * rows
    blocks = shards * per_shard
    slots, _, width = pool_ref.shape
    pairs, cands, _ = turned_ref.shape
    per_pair = LANES // rows
    count = cands // PBLK
    split = low_coef_a_hbm.shape[1]
    loads = [
        pltpu.make_async_copy(low_coef_a_hbm, low_coef_ref.at[:, pl.ds(0, split)], low_sem.at[0]),
        pltpu.make_async_copy(low_coef_b_hbm, low_coef_ref.at[:, pl.ds(split, pairs - split)], low_sem.at[1]),
    ]

    @pl.when(shard == 0)
    def _():
        for load in loads:
            load.start()

    spread_ref[...] = jnp.zeros_like(spread_ref)
    scale_ref[...] = jnp.zeros_like(scale_ref)
    for shift in range(shards):
        source = lax.rem(shard - shift + shards, shards)
        turned_ref[source] = ins[shift][:base, :].astype(F32).T
        aux = unpack_aux(ins[shift], base)
        for k in range(per_shard):
            col_ref[source * per_shard + k] = aux[k : k + 1, :]

    def run(spans, low):
        for block in range(blocks):
            cols = jnp.broadcast_to(col_ref[block], (8, cands))
            if low:
                half = blocks // 2
                cols = cols + (low_col_a_ref[block] if block < half else low_col_b_ref[block - half])
            col_cols = columns(cols)
            for n in range(count):
                slot = slot_ref[block * count + n]
                scale_ref[slot] = scale_ref[slot] + col_cols[n * PBLK : (n + 1) * PBLK, :]
        for level, (lo, hi) in enumerate(spans):
            for pair in range(pairs):
                coef = turned_ref[pair]
                if low:
                    coef = coef + low_coef_ref[level, pair]
                coef = coef.astype(BF16)
                if low:
                    half_ref[level, pair] = coef
                for j in range(per_pair):
                    block = pair * per_pair + j
                    lanes = slice(j * rows, (j + 1) * rows)
                    for n in range(count):
                        spread_ref[slot_ref[block * count + n], :, block * rows : (block + 1) * rows] = coef[
                            n * PBLK : (n + 1) * PBLK, lanes
                        ]
            if low:
                pltpu.make_async_copy(half_ref.at[level], half_hbm.at[level], half_sem).start()
            spread = spread_ref[0:slots].reshape(slots * PBLK, blocks * rows)
            scale = scale_ref[0:slots].reshape(slots * PBLK, LANES)[:, level : level + 1]
            for start in range(lo, hi, PIECE):
                end = min(start + PIECE, hi)
                grad = contract(spread, query_ref[:, start:end], 1, 0)
                pool = pool_ref[:, :, start:end].reshape(slots * PBLK, end - start).astype(F32)
                out_ref[:, :, start:end] = (grad - scale * pool).astype(BF16).reshape(slots, PBLK, end - start)
                if end % LANES == 0:
                    done = pl.ds(start // LANES * LANES, end - start // LANES * LANES)
                    pltpu.make_async_copy(out_ref.at[:, :, done], out_hbm.at[:, :, done], out_sem).start()
        if low:
            pltpu.make_async_copy(half_ref, half_hbm, half_sem).wait()
        pltpu.make_async_copy(out_ref, out_hbm, out_sem).wait()

    @pl.when(shard == 0)
    def _():
        for load in loads:
            load.wait()
        run(bounds, True)

    @pl.when(shard != 0)
    def _():
        run([(0, width)], False)


def query_kernel(
    bounds, shards, per_shard, rows, loss_scale, slot_ref, shard_ref, query_ref, pool_ref, low_row_a_ref, low_row_b_ref,
    low_loss_a_ref, low_loss_b_ref, high_loss_ref, low_half_hbm, *refs
):
    ins = refs[:shards]
    query_grad_ref, loss_ref = refs[shards : shards + 2]
    cand_ref, coef_ref, row_ref, low_half_ref, sem = refs[shards + 2 :]
    shard = shard_ref[0]
    base = per_shard * rows
    blocks = shards * per_shard
    count = cand_ref.shape[0]
    width = query_ref.shape[1]
    cands = coef_ref.shape[1]
    per_pair = LANES // rows
    copy = pltpu.make_async_copy(low_half_hbm, low_half_ref, sem)

    @pl.when(shard == 0)
    def _():
        copy.start()

    for shift in range(shards):
        source = lax.rem(shard - shift + shards, shards)
        coef_ref[pl.ds(source * base, base), :] = ins[shift][:base, :]
        aux = unpack_aux(ins[shift], base)
        for k in range(per_shard):
            row_ref[source * per_shard + k] = aux[per_shard : per_shard + 1, k * rows : (k + 1) * rows]
    half = blocks // 2
    for block in range(blocks):
        line = low_loss_a_ref[block : block + 1, :] if block < half else low_loss_b_ref[block - half : block - half + 1, :]
        loss_ref[block // per_pair : block // per_pair + 1, block % per_pair * rows : (block % per_pair + 1) * rows] = line
    loss_ref[pl.ds(shard, 1), :] = loss_ref[pl.ds(shard, 1), :] + high_loss_ref[...]
    loss_ref[...] = loss_ref[...] * loss_scale

    def run(spans, low):
        def one(pair, low_row_ref, first):
            for j in range(per_pair):
                local = pair * per_pair + j
                block = first * per_pair + local
                take_blocks(pool_ref, slot_ref, block, count, cand_ref)
                rows_here = jnp.broadcast_to(row_ref[block], (8, rows))
                if low:
                    rows_here = rows_here + low_row_ref[local]
                row_cols = columns(rows_here)
                here = pl.ds(block * rows, rows)
                for level, (lo, hi) in enumerate(spans):
                    query = query_ref[here, lo:hi].astype(F32)
                    cand = cand_ref[:, :, lo:hi].reshape(cands, hi - lo)
                    if low:
                        coef = low_half_ref[level, first + pair][:, j * rows : (j + 1) * rows]
                        grad = contract(coef, cand, 0, 0)
                    else:
                        grad = contract(coef_ref[here, :], cand, 1, 0)
                    grad = grad - row_cols[:rows, level : level + 1] * query
                    query_grad_ref[here, lo:hi] = grad.astype(BF16)

        def step(pair, carry):
            one(pair, low_row_a_ref, 0)
            one(pair, low_row_b_ref, half // per_pair)
            return carry

        lax.fori_loop(0, half // per_pair, step, 0)

    @pl.when(shard == 0)
    def _():
        copy.wait()
        run(bounds, True)

    @pl.when(shard != 0)
    def _():
        run([(0, width)], False)


def collect_kernel(target_ref, back_ref, out_ref, choose_ref):
    rows, count = choose_ref.shape

    @pl.when(pl.program_id(0) == 0)
    def _():
        here = lax.broadcasted_iota(jnp.int32, (rows, count), 0)
        choose_ref[...] = jnp.where(here == target_ref[...], 1.0, 0.0).astype(BF16)

    out_ref[...] = contract(choose_ref[...], back_ref[...], 1, 0).astype(BF16)


def per_device(queries, passages, neg_lists, positives):
    peers = lax.axis_size("dp")
    shards = lax.axis_size("tensor")
    total_rows, width = queries.shape
    blocks = neg_lists.shape[0] // peers
    count = neg_lists.shape[1]
    rows = total_rows // blocks
    local_blocks = passages.shape[0] // PBLK
    cands = count * PBLK
    per_shard = blocks // shards
    base = per_shard * rows
    slots = peers
    my_index = lax.axis_index("dp")
    shard = lax.axis_index("tensor")
    sizes = [MINP * 2**level for level in range(NPRE)]
    low_sizes = [size for size in sizes if size <= width]
    high_sizes = [size for size in sizes if size > width]
    assert high_sizes == [width * shards // 2, width * shards] and low_sizes[-1] == width
    assert shards == 4 and base == LANES and blocks % 4 == 0
    bounds = list(zip([0] + low_sizes[:-1], low_sizes))
    levels = len(bounds)
    weight_total = sum(size / MINP for size in sizes)

    flat = neg_lists.reshape(peers, blocks * count)
    mine = (flat >= 0) & (flat // local_blocks == my_index)
    wanted = jnp.max(jnp.where(mine, flat % local_blocks, -1), axis=1)
    own = lax.dynamic_slice_in_dim(neg_lists, my_index * blocks, blocks, 0)
    valid = own >= 0
    slot = jnp.where(valid, own // local_blocks, 0).reshape(blocks * count)
    spare_slot = jnp.where(valid, own // local_blocks, slots).reshape(blocks * count)
    within = jnp.arange(PBLK, dtype=jnp.int32)
    ids = jnp.where(valid[:, :, None], own[:, :, None] * PBLK + within[None, None, :], -1)
    ids = ids.reshape(blocks, cands).astype(F32)
    target = jnp.where(wanted[:, None] >= 0, wanted[:, None] * PBLK + within[None, :], -1).reshape(1, slots * PBLK)
    pos = positives.reshape(blocks, rows).astype(F32)
    shard_arr = shard.reshape(1).astype(jnp.int32)
    pool_shape = (slots, PBLK, width)

    panels = pl.pallas_call(
        pack_kernel,
        out_shape=pltpu.HBM(pool_shape, BF16),
        in_specs=[smem(), vmem()],
        out_specs=hbm(),
        scratch_shapes=[pltpu.SemaphoreType.DMA(())],
        compiler_params=params(),
        name="pack",
    )(wanted, passages.reshape(local_blocks, PBLK, width))
    pool = lax.all_to_all(panels, "dp", split_axis=0, concat_axis=0, tiled=True)

    def shift_by(part, s):
        return lax.ppermute(part, "tensor", [(i, (i + s) % shards) for i in range(shards)])

    cand_scratch = pltpu.VMEM((count, PBLK, width), BF16)
    message = jax.ShapeDtypeStruct((base + AUX, cands), F32)
    norm_shape = (slots, PBLK, LANES)
    norms, far, right, left = pl.pallas_call(
        partial(first_dots_kernel, shards, per_shard, rows, (2, 1, 3)),
        out_shape=[jax.ShapeDtypeStruct(norm_shape, F32)] + [message] * 3,
        in_specs=[smem(), smem(), vmem(), vmem()],
        out_specs=[vmem()] * 4,
        scratch_shapes=[cand_scratch],
        compiler_params=params(),
        name="dots",
    )(slot, shard_arr, queries, pool)
    (here,) = pl.pallas_call(
        partial(dots_kernel, shards, per_shard, rows, (0,)),
        out_shape=[message],
        in_specs=[smem(), smem(), vmem(), vmem(), vmem()],
        out_specs=[vmem()],
        scratch_shapes=[cand_scratch],
        compiler_params=params(),
        name="dots_own",
    )(slot, shard_arr, queries, pool, norms)
    arrived = [here, shift_by(right, 1), shift_by(far, 2), shift_by(left, 3)]

    pairs = total_rows // LANES
    half_pairs, half_blocks = pairs // 2, blocks // 2

    def low_terms(first, renorm, norm_table, after, name):
        return pl.pallas_call(
            partial(low_kernel, bounds, rows, first, renorm),
            out_shape=[
                pltpu.HBM((levels, half_pairs, cands, LANES), F32),
                jax.ShapeDtypeStruct((half_blocks, 8, rows), F32),
                jax.ShapeDtypeStruct((half_blocks, 8, cands), F32),
                jax.ShapeDtypeStruct((half_blocks, rows), F32),
                jax.ShapeDtypeStruct(norm_shape if renorm else (8, LANES), F32),
            ],
            in_specs=[smem(), smem()] + [vmem()] * 5 + [pl.BlockSpec(memory_space=pl.ANY)],
            out_specs=[hbm()] + [vmem()] * 4,
            scratch_shapes=[
                cand_scratch,
                pltpu.VMEM((levels, LANES, cands), F32),
                pltpu.VMEM((levels, half_pairs, cands, LANES), F32),
                pltpu.SemaphoreType.DMA(()),
            ],
            compiler_params=params(),
            name=name,
        )(slot, shard_arr, queries, pool, ids, pos, norm_table, after)

    coef_a, row_a, col_a, loss_a, level_norms = low_terms(0, True, ids, here, "low_a")
    *coefs, high_loss = pl.pallas_call(
        partial(high_kernel, shards, per_shard, rows, [size / MINP for size in high_sizes]),
        out_shape=[jax.ShapeDtypeStruct((base + COEF_AUX, cands), BF16)] * shards
        + [jax.ShapeDtypeStruct((1, base), F32)],
        in_specs=[smem()] + [vmem()] * 2 + [pl.BlockSpec(memory_space=pl.ANY)] + [vmem()] * shards,
        out_specs=[vmem()] * (shards + 1),
        compiler_params=params(),
        name="high",
    )(shard_arr, ids, pos, loss_a, *arrived)
    coef_b, row_b, col_b, loss_b, _ = low_terms(half_blocks, False, level_norms, high_loss, "low_b")
    coefs = [coefs[0]] + [shift_by(coefs[s], s) for s in range(1, shards)]

    pinned = partial(pltpu.with_memory_space_constraint, memory_space=pltpu.HBM)
    half_shape = (levels, pairs, cands, LANES)
    slot_grad, low_half = pl.pallas_call(
        partial(passage_kernel, bounds, shards, per_shard, rows),
        out_shape=[pltpu.HBM(pool_shape, BF16), pltpu.HBM(half_shape, BF16)],
        in_specs=[smem(), smem()] + [vmem()] * 4 + [hbm()] * 2 + [vmem()] * shards,
        out_specs=[hbm()] * 2,
        scratch_shapes=[
            pltpu.VMEM((pairs, cands, LANES), F32),
            pltpu.VMEM((blocks, 1, cands), F32),
            pltpu.VMEM((slots + 1, PBLK, total_rows), BF16),
            pltpu.VMEM((slots + 1, PBLK, LANES), F32),
            pltpu.VMEM(pool_shape, BF16),
            pltpu.VMEM(half_shape, BF16),
            pltpu.VMEM(half_shape, F32),
            pltpu.SemaphoreType.DMA(()),
            pltpu.SemaphoreType.DMA(()),
            pltpu.SemaphoreType.DMA((2,)),
        ],
        compiler_params=params(),
        name="passage",
    )(spare_slot, shard_arr, queries, pool, col_a, col_b, pinned(coef_a), pinned(coef_b), *coefs)
    back = lax.all_to_all(slot_grad, "dp", split_axis=0, concat_axis=0, tiled=True)

    query_grad, loss = pl.pallas_call(
        partial(query_kernel, bounds, shards, per_shard, rows, 1.0 / weight_total),
        out_shape=[
            jax.ShapeDtypeStruct((total_rows, width), BF16),
            jax.ShapeDtypeStruct((shards, base), F32),
        ],
        in_specs=[smem(), smem()] + [vmem()] * 7 + [hbm()] + [vmem()] * shards,
        out_specs=[vmem()] * 2,
        scratch_shapes=[
            cand_scratch,
            pltpu.VMEM((total_rows, cands), BF16),
            pltpu.VMEM((blocks, 1, rows), F32),
            pltpu.VMEM(half_shape, BF16),
            pltpu.SemaphoreType.DMA(()),
        ],
        compiler_params=params(),
        name="query",
    )(slot, shard_arr, queries, pool, row_a, row_b, loss_a, loss_b, high_loss, pinned(low_half), *coefs)
    loss = lax.psum(loss, "tensor")

    piece = width // 4
    passage_grad = pl.pallas_call(
        collect_kernel,
        grid=(width // piece,),
        out_shape=jax.ShapeDtypeStruct((local_blocks * PBLK, width), BF16),
        in_specs=[
            pl.BlockSpec((1, slots * PBLK), lambda i: (0, 0)),
            pl.BlockSpec((slots * PBLK, piece), lambda i: (0, i)),
        ],
        out_specs=pl.BlockSpec((local_blocks * PBLK, piece), lambda i: (0, i)),
        scratch_shapes=[pltpu.VMEM((local_blocks * PBLK, slots * PBLK), BF16)],
        compiler_params=params(),
        name="collect",
    )(target, back.reshape(slots * PBLK, width))
    return (
        query_grad,
        passage_grad,
        loss.reshape(total_rows),
    )


def solution(mesh):
    return jax.shard_map(
        per_device,
        mesh=mesh,
        in_specs=(P("dp", "tensor"), P("dp", "tensor"), P(), P("dp")),
        out_specs=(P("dp", "tensor"), P("dp", "tensor"), P("dp")),
        check_vma=False,
    )
```

time: 226 us -> 168 us (0.74)
  Pallas kernels: 94.1 us -> 37.5 us
  waiting for transfers between devices: 98.6 us -> 84.6 us
  blocking collectives: 0 us -> 7.38 us
  local copies, waits for them, and re-layouts: 2.31 us -> 7.61 us
    pallas_call x1, Pallas kernels: 65.2 us -> 1.89 us  [per_device(): pl.pallas_call(pack_kernel, out_shape=pltpu.HBM(pool_shape, BF16), in_spe...]
    all_to_all x1, waiting for transfers between devices: 45.1 us -> 34.8 us  [per_device(): lax.all_to_all(slot_grad, 'dp', split_axis=0, concat_axis=0, tiled=True)]
    psum x0 -> x1, blocking collectives: none -> 7.38 us  [per_device(): loss = lax.psum(loss, 'tensor')]
    pallas_call x5, Pallas kernels: 14.4 us -> 20.8 us  [the longest x2 13 us: low_terms(): pl.pallas_call(partial(low_kernel, bounds, rows, first, renorm), out_shap...]
    unnamed x9 -> x31, local copies, waits for them, and re-layouts: 0.69 us -> 4.69 us
    ppermute x6, waiting for transfers between devices: 3.71 us -> 0.02 us  [shift_by(): lax.ppermute(part, 'tensor', [(i, (i + s) % shards) for i in range(shards)])]
  transfers between devices with their start and end apart: 8 -> 8, of which waited for: 4 -> 2; matrix products, arithmetic and copies ran while one was open for 1% -> 2% of each run, Pallas kernels for 6% -> 13%
where the time goes in v2:
time: 168 us; the launch traced here: 167 us
  waiting for transfers between devices  84.6 us (50%)
  Pallas kernels  37.5 us (22%)
  starting transfers between devices  27.9 us (17%)
  local copies, waits for them, and re-layouts  7.61 us (5%)
  blocking collectives  7.38 us (4%)
    all_to_all x1, waiting for transfers between devices, per_device(): pool = lax.all_to_all(panels, 'dp', split_axis=0, concat_axis=0, tiled=True)  49.7 us
    all_to_all x1, waiting for transfers between devices, per_device(): lax.all_to_all(slot_grad, 'dp', split_axis=0, concat_axis=0, tiled=True)  34.8 us
    all_to_all x1, starting transfers between devices, per_device(): pool = lax.all_to_all(panels, 'dp', split_axis=0, concat_axis=0, tiled=True)  13.3 us
    pallas_call x2, Pallas kernels, low_terms(): pl.pallas_call(partial(low_kernel, bounds, rows, first, renorm), out_shap...  13 us
    all_to_all x1, starting transfers between devices, per_device(): lax.all_to_all(slot_grad, 'dp', split_axis=0, concat_axis=0, tiled=True)  7.38 us
    psum x1, blocking collectives, per_device(): loss = lax.psum(loss, 'tensor')  7.38 us
    pallas_call x1, Pallas kernels, per_device(): pl.pallas_call(partial(query_kernel, bounds, shards, per_shard, rows, 1.0...  7.34 us
    ppermute x6, starting transfers between devices, shift_by(): lax.ppermute(part, 'tensor', [(i, (i + s) % shards) for i in range(shards)])  7.18 us
  transfers between devices with their start and end apart: 8, of which 2 were waited for; matrix products, arithmetic and copies ran while one was open for 2% of the time, Pallas kernels for 13%

profile of v2, /device:TPU:1, one launch (start us, length us, event | category | flops | bytes accessed | tf_op | source)
XLA Modules:
  0.0 167.5 jit_solution(7810351188119679930)
XLA Ops:
  0.6 0.8 fusion.2
  1.4 0.1 reduce_max.14
  1.5 0.1 reduce_max.18.wanted_ref
  1.7 0.0 copy-start.12
  1.7 0.0 copy-start.3
  1.7 1.0 copy-done.3
  2.7 1.9 %pack.1 = bf16[64,16,1024]{2,1,0:T(8,128)(2,1)} custom-call(s32[64]{0:T(128)S(1)} %reduce_max.18.wanted_ref, bf16[16,16,1024]{2,1,0:T(8,128)(2,1)S(1)} %bitcast.4), custom_call_target="tpu_custom_call" | custom-call | tf_op jit(solution)/shard_map/pack/pallas_call | solution.py:493
  4.6 0.0 copy-start.14
  4.6 0.0 copy-start
  4.6 0.0 copy-done.12
  4.6 13.3 %all-to-all-start = ((bf16[64,16,1024]{2,1,0:T(8,128)(2,1)}), bf16[64,16,1024]{2,1,0:T(8,128)(2,1)S(1)}, u32[]{:S(2)}, u32[]{:S(2)}) async-start(bf16[64,16,1024]{2,1,0:T(8,128)(2,1)} %pack.1), calls=%async_computation | async-start | bytes 4194304 | tf_op jit(solution)/shard_map/all_to_all | solution.py:502
  18.0 0.8 constant_dynamic-slice_fusion
  18.7 0.1 copy.16
  18.8 0.1 reshape.80.slot_ref
  18.9 0.1 broadcast_in_dim.39
  19.0 0.1 broadcast_in_dim.40
  19.1 0.1 add.58
  19.2 0.1 add.59
  19.3 0.1 add.61
  19.4 0.0 copy-done.14
  19.4 0.1 convert_element_type.10.pos_ref
  19.5 49.7 %all-to-all-done.pool_ref = bf16[64,16,1024]{2,1,0:T(8,128)(2,1)S(1)} async-done(((bf16[64,16,1024]{2,1,0:T(8,128)(2,1)}), bf16[64,16,1024]{2,1,0:T(8,128)(2,1)S(1)}, u32[]{:S(2)}, u32[]{:S(2)}) %all-to-all-start) | async-done | bytes 2097184 | tf_op jit(solution)/shard_map/all_to_all | solution.py:502
  69.2 0.0 copy-done
  69.2 2.7 %dots.1 = (f32[64,16,128]{2,1,0:T(8,128)S(1)}, f32[136,256]{1,0:T(8,128)S(1)}, f32[136,256]{1,0:T(8,128)S(1)}, f32[136,256]{1,0:T(8,128)S(1)}) custom-call(s32[128]{0:T(128)S(1)} %reshape.80.slot_ref, s32[1]{0:T(128)} %bitcast.shard_ref, bf16[512,1024]{1,0:T(8,128)(2,1)S(1)} %copy-done, bf16[64,16,1024]{2,1,0:T(8,128)(2,1)S(1)} %all-to-all-done.pool_ref), custom_call_target="tpu_custom_call" | custom-call | tf_op jit(solution)/shard_map/dots/pallas_call | solution.py:510
  71.9 1.3 collective-permute-start
  73.2 2.5 %collective-permute-start.1 = (f32[136,256]{1,0:T(8,128)S(1)}, f32[136,256]{1,0:T(8,128)S(1)}, u32[]{:S(2)}, u32[]{:S(2)}) collective-permute-start(f32[136,256]{1,0:T(8,128)S(1)} %get-tuple-element.30), channel_id=1, source_target_pairs={{0,2},{1,3},{2,0},{3,1},{4,6},{5,7},{6,4},{7,5},{8,10},{9,11},{10,... | collective-permute-start | bytes 417800 | tf_op jit(solution)/shard_map/ppermute | solution.py:505
  75.6 1.1 collective-permute-start.2
  76.8 1.0 dots_own.1.after_ref.refs_0_
  77.8 7.1 %low_a.1 = (f32[5,2,256,128]{3,2,1,0:T(8,128)}, f32[4,8,64]{2,1,0:T(8,128)S(1)}, f32[4,8,256]{2,1,0:T(8,128)S(1)}, f32[4,64]{1,0:T(4,128)S(1)}, f32[64,16,128]{2,1,0:T(8,128)S(1)}) custom-call(s32[128]{0:T(128)S(1)} %reshape.80.slot_ref, s32[1]{0:T(128)} %bitcast.shard_ref, bf16[512,1024]{1,0:T(8,128)(2,1)S(1)} %copy-done, ...), custom_call_target="tpu_custom_call" | custom-call | tf_op jit(solution)/shard_map/low_a/pallas_call | solution.py:534
  84.9 0.0 copy-start.1
  84.9 0.8 copy-done.1
  85.7 0.0 collective-permute-done.refs_1_
  85.7 0.0 collective-permute-done.1.refs_2_
  85.7 0.0 collective-permute-done.2.refs_3_
  85.7 1.3 high.1
  87.0 0.0 collective-permute-start.3
  87.0 0.0 copy-done.4
  87.0 0.1 collective-permute-start.4
  87.1 0.5 copy-done.8
  87.6 2.2 %collective-permute-start.5 = (bf16[160,256]{1,0:T(8,128)(2,1)}, bf16[160,256]{1,0:T(8,128)(2,1)S(1)}, u32[]{:S(2)}, u32[]{:S(2)}) collective-permute-start(bf16[160,256]{1,0:T(8,128)(2,1)} %get-tuple-element.42), channel_id=1, source_target_pairs={{0,3},{1,0},{2,1},{3,2},{4,7},{5,4},{6,5},{7,6},{8,11},{9,8},{10,9... | collective-permute-start | bytes 245768 | tf_op jit(solution)/shard_map/ppermute | solution.py:505
  89.8 0.6 reshape.83.slot_ref
  90.4 1.0 copy-done.2
  91.4 0.7 copy-done.9
  92.1 5.8 %low_b.1 = (f32[5,2,256,128]{3,2,1,0:T(8,128)}, f32[4,8,64]{2,1,0:T(8,128)S(1)}, f32[4,8,256]{2,1,0:T(8,128)S(1)}, f32[4,64]{1,0:T(4,128)S(1)}, f32[8,128]{1,0:T(8,128)}) custom-call(s32[128]{0:T(128)S(1)} %reshape.80.slot_ref, s32[1]{0:T(128)} %bitcast.shard_ref, bf16[512,1024]{1,0:T(8,128)(2,1)S(1)} %copy-done, ...), custom_call_target="tpu_custom_call" | custom-call | tf_op jit(solution)/shard_map/low_b/pallas_call | solution.py:534
  97.9 0.0 copy-start.6
  97.9 0.6 copy-done.6
  98.5 0.0 collective-permute-done.3.refs_1_
  98.5 0.0 collective-permute-done.4.refs_2_
  98.5 0.0 collective-permute-done.5.refs_3_
  98.5 0.0 copy-done.11
  98.5 6.2 %passage.1 = (bf16[64,16,1024]{2,1,0:T(8,128)(2,1)}, bf16[5,4,256,128]{3,2,1,0:T(8,128)(2,1)}) custom-call(s32[128]{0:T(128)S(1)} %copy-done.11, s32[1]{0:T(128)} %bitcast.shard_ref, bf16[512,1024]{1,0:T(8,128)(2,1)S(1)} %copy-done, bf16[64,16,1024]{2,1,0:T(8,128)(2,1)S(1)} %all-to-all-done.pool_ref, f32[4,8,256]{2,1,0:T(8,128)S(1)} %get-tuple-element.35.low_col_a_ref, ...), custom_call_target="tpu_custom_call" | custom-call | tf_op jit(solution)/shard_map/passage/pallas_call | solution.py:570
  104.8 0.0 copy-start.13
  104.8 0.0 copy-start.5
  104.8 0.0 copy-start.7
  104.8 0.0 copy-start.10
  104.8 7.4 %all-to-all-start.1 = ((bf16[64,16,1024]{2,1,0:T(8,128)(2,1)}), bf16[64,16,1024]{2,1,0:T(8,128)(2,1)}, u32[]{:S(2)}, u32[]{:S(2)}) async-start(bf16[64,16,1024]{2,1,0:T(8,128)(2,1)} %get-tuple-element.45), calls=%async_computation.1 | async-start | bytes 4194304 | tf_op jit(solution)/shard_map/all_to_all | solution.py:590
  112.2 0.0 copy-done.13
  112.2 0.7 add_select_fusion.2
  112.9 0.8 select_n.63.target_ref
  113.8 0.0 copy-done.5
  113.8 7.3 %query.1 = (bf16[512,1024]{1,0:T(8,128)(2,1)}, f32[4,128]{1,0:T(4,128)S(1)}) custom-call(s32[128]{0:T(128)S(1)} %reshape.80.slot_ref, s32[1]{0:T(128)} %bitcast.shard_ref, bf16[512,1024]{1,0:T(8,128)(2,1)S(1)} %copy-done, bf16[64,16,1024]{2,1,0:T(8,128)(2,1)S(1)} %all-to-all-done.pool_ref, f32[4,8,64]{2,1,0:T(8,128)S(1)} %get-tuple-element.26.low_row_a_ref, ...), custom_call_target="tpu_custom_call" | custom-call | tf_op jit(solution)/shard_map/query/pallas_call | solution.py:592
  121.1 7.4 %psum.7 = f32[512]{0:T(512)} all-reduce(f32[512]{0:T(512)S(1)} %bitcast.5), channel_id=1, replica_groups=mesh['dp'=64,'tensor'=4] {'tensor'}, use_global_device_ids=true, to_apply=%region_2.3 | all-reduce | flops 512 | bytes 4096 | tf_op jit(solution)/shard_map/psum | solution.py:610
  128.5 34.8 %all-to-all-done.1 = bf16[64,16,1024]{2,1,0:T(8,128)(2,1)} async-done(((bf16[64,16,1024]{2,1,0:T(8,128)(2,1)}), bf16[64,16,1024]{2,1,0:T(8,128)(2,1)}, u32[]{:S(2)}, u32[]{:S(2)}) %all-to-all-start.1) | async-done | bytes 2097184 | tf_op jit(solution)/shard_map/all_to_all | solution.py:590
  163.4 4.1 %collect.1 = bf16[256,1024]{1,0:T(8,128)(2,1)} custom-call(s32[1,1024]{1,0:T(1,128)S(1)} %select_n.63.target_ref, bf16[1024,1024]{1,0:T(8,128)(2,1)} %bitcast.2.back_ref), custom_call_target="tpu_custom_call" | custom-call | tf_op jit(solution)/shard_map/collect/pallas_call | solution.py:613
  (14 shorter events, 0.1 us)
Async XLA Ops:
  1.7 3.0 %copy-start.12 = (s32[64]{0:T(128)}, s32[64]{0:T(128)S(1)}, u32[]{:S(2)}) copy-start(s32[64]{0:T(128)S(1)} %reduce_max.18.wanted_ref) | copy-start | bytes 772
  1.7 1.0 copy-start.3
  4.6 14.8 %copy-start.14 = (s32[512]{0:T(512)S(1)}, s32[512]{0:T(512)}, u32[]{:S(2)}) copy-start(s32[512]{0:T(512)} %param.7) | copy-start | bytes 6148
  4.6 64.6 %copy-start = (bf16[512,1024]{1,0:T(8,128)(2,1)S(1)}, bf16[512,1024]{1,0:T(8,128)(2,1)}, u32[]{:S(2)}) copy-start(bf16[512,1024]{1,0:T(8,128)(2,1)} %query_ref.11) | copy-start | bytes 3145732
  4.6 64.6 %all-to-all-start = ((bf16[64,16,1024]{2,1,0:T(8,128)(2,1)}), bf16[64,16,1024]{2,1,0:T(8,128)(2,1)S(1)}, u32[]{:S(2)}, u32[]{:S(2)}) async-start(bf16[64,16,1024]{2,1,0:T(8,128)(2,1)} %pack.1), calls=%async_computation | async-start | bytes 4194304 | tf_op jit(solution)/shard_map/all_to_all | solution.py:502
  71.9 13.8 %collective-permute-start = (f32[136,256]{1,0:T(8,128)S(1)}, f32[136,256]{1,0:T(8,128)S(1)}, u32[]{:S(2)}, u32[]{:S(2)}) collective-permute-start(f32[136,256]{1,0:T(8,128)S(1)} %get-tuple-element.29), channel_id=1, source_target_pairs={{0,1},{1,2},{2,3},{3,0},{4,5},{5,6},{6,7},{7,4},{8,9},{9,10},{10,1... | collective-permute-start | bytes 417800 | tf_op jit(solution)/shard_map/ppermute | solution.py:505
  73.2 12.5 %collective-permute-start.1 = (f32[136,256]{1,0:T(8,128)S(1)}, f32[136,256]{1,0:T(8,128)S(1)}, u32[]{:S(2)}, u32[]{:S(2)}) collective-permute-start(f32[136,256]{1,0:T(8,128)S(1)} %get-tuple-element.30), channel_id=1, source_target_pairs={{0,2},{1,3},{2,0},{3,1},{4,6},{5,7},{6,4},{7,5},{8,10},{9,11},{10,... | collective-permute-start | bytes 417800 | tf_op jit(solution)/shard_map/ppermute | solution.py:505
  75.6 10.1 %collective-permute-start.2 = (f32[136,256]{1,0:T(8,128)S(1)}, f32[136,256]{1,0:T(8,128)S(1)}, u32[]{:S(2)}, u32[]{:S(2)}) collective-permute-start(f32[136,256]{1,0:T(8,128)S(1)} %get-tuple-element.31), channel_id=1, source_target_pairs={{0,3},{1,0},{2,1},{3,2},{4,7},{5,4},{6,5},{7,6},{8,11},{9,8},{10,9... | collective-permute-start | bytes 417800 | tf_op jit(solution)/shard_map/ppermute | solution.py:505
  84.9 0.8 copy-start.1
  85.7 1.3 copy-start.4
  87.0 0.6 copy-start.8
  87.0 11.5 %collective-permute-start.3 = (bf16[160,256]{1,0:T(8,128)(2,1)}, bf16[160,256]{1,0:T(8,128)(2,1)S(1)}, u32[]{:S(2)}, u32[]{:S(2)}) collective-permute-start(bf16[160,256]{1,0:T(8,128)(2,1)} %get-tuple-element.40), channel_id=1, source_target_pairs={{0,1},{1,2},{2,3},{3,0},{4,5},{5,6},{6,7},{7,4},{8,9},{9,10},{10,1... | collective-permute-start | bytes 245768 | tf_op jit(solution)/shard_map/ppermute | solution.py:505
  87.0 11.5 %collective-permute-start.4 = (bf16[160,256]{1,0:T(8,128)(2,1)}, bf16[160,256]{1,0:T(8,128)(2,1)S(1)}, u32[]{:S(2)}, u32[]{:S(2)}) collective-permute-start(bf16[160,256]{1,0:T(8,128)(2,1)} %get-tuple-element.41), channel_id=1, source_target_pairs={{0,2},{1,3},{2,0},{3,1},{4,6},{5,7},{6,4},{7,5},{8,10},{9,11},{10,... | collective-permute-start | bytes 245768 | tf_op jit(solution)/shard_map/ppermute | solution.py:505
  87.6 11.0 %collective-permute-start.5 = (bf16[160,256]{1,0:T(8,128)(2,1)}, bf16[160,256]{1,0:T(8,128)(2,1)S(1)}, u32[]{:S(2)}, u32[]{:S(2)}) collective-permute-start(bf16[160,256]{1,0:T(8,128)(2,1)} %get-tuple-element.42), channel_id=1, source_target_pairs={{0,3},{1,0},{2,1},{3,2},{4,7},{5,4},{6,5},{7,6},{8,11},{9,8},{10,9... | collective-permute-start | bytes 245768 | tf_op jit(solution)/shard_map/ppermute | solution.py:505
  90.4 8.2 %copy-start.11 = (s32[128]{0:T(128)S(1)}, s32[128]{0:T(128)}, u32[]{:S(2)}) copy-start(s32[128]{0:T(128)} %reshape.83.slot_ref) | copy-start | bytes 1540
  90.4 1.0 copy-start.2
  91.4 0.7 copy-start.9
  97.9 0.6 copy-start.6
  104.8 7.4 %copy-start.13 = (s32[64]{0:T(128)S(1)}, s32[64]{0:T(128)}, u32[]{:S(2)}) copy-start(s32[64]{0:T(128)} %copy-done.12) | copy-start | bytes 772
  104.8 9.0 %copy-start.5 = (f32[4,64]{1,0:T(4,128)S(1)}, f32[4,64]{1,0:T(4,128)}, u32[]{:S(2)}) copy-start(f32[4,64]{1,0:T(4,128)} %copy-done.4) | copy-start | bytes 3076
  104.8 9.0 %copy-start.7 = (f32[4,64]{1,0:T(4,128)S(1)}, f32[4,64]{1,0:T(4,128)}, u32[]{:S(2)}) copy-start(f32[4,64]{1,0:T(4,128)} %copy-done.6) | copy-start | bytes 3076
  104.8 9.0 %copy-start.10 = (f32[1,128]{1,0:T(1,128)S(1)}, f32[1,128]{1,0:T(1,128)}, u32[]{:S(2)}) copy-start(f32[1,128]{1,0:T(1,128)} %copy-done.8) | copy-start | bytes 1540
  104.8 58.5 %all-to-all-start.1 = ((bf16[64,16,1024]{2,1,0:T(8,128)(2,1)}), bf16[64,16,1024]{2,1,0:T(8,128)(2,1)}, u32[]{:S(2)}, u32[]{:S(2)}) async-start(bf16[64,16,1024]{2,1,0:T(8,128)(2,1)} %get-tuple-element.45), calls=%async_computation.1 | async-start | bytes 4194304 | tf_op jit(solution)/shard_map/all_to_all | solution.py:590

commit v3 on v1

v3 whole, which is shorter than its diff:
```python
from functools import partial

import jax
import jax.numpy as jnp
from jax import lax
from jax.experimental import pallas as pl
from jax.experimental.pallas import tpu as pltpu
from jax.sharding import PartitionSpec as P

MINP = 64
NPRE = 7
PBLK = 16

EPS = 1e-06
INV_TEMP = 20.0

F32 = jnp.float32
BF16 = jnp.bfloat16

AUX = 8
COEF_AUX = 32
LANES = 128
PIECE = 256
CHUNKS = 4


def vmem():
    return pl.BlockSpec(memory_space=pltpu.VMEM)


def smem():
    return pl.BlockSpec(memory_space=pltpu.SMEM)


def hbm():
    return pl.BlockSpec(memory_space=pltpu.HBM)


def params():
    return pltpu.CompilerParams(vmem_limit_bytes=20 * 2**20)


def contract(a, b, da, db):
    return lax.dot_general(a, b, (((da,), (db,)), ((), ())), preferred_element_type=F32)


def eye(n):
    return lax.broadcasted_iota(jnp.int32, (n, n), 0) == lax.broadcasted_iota(jnp.int32, (n, n), 1)


def to_col(row):
    return jnp.sum(jnp.where(eye(row.shape[1]), row, 0.0), axis=1, keepdims=True)


def to_row(col):
    return jnp.sum(jnp.where(eye(col.shape[0]), col, 0.0), axis=0, keepdims=True)


def square_sums(half):
    wide = half.astype(F32)
    return jnp.sum(wide * wide, axis=1, keepdims=True)


def columns(table):
    table = jnp.concatenate([table, jnp.zeros((8, LANES - table.shape[1]), F32)], axis=1) if table.shape[1] < LANES else table
    return jnp.concatenate([table, jnp.zeros((LANES - 8, table.shape[1]), F32)], axis=0).T


def terms(dots, a, pp_row, live, labels, weight):
    b = jnp.where(live, lax.rsqrt(pp_row + EPS), 0.0)
    scale = (a * INV_TEMP) * b
    logits = dots * scale
    exponent = jnp.where(live, jnp.exp(logits), 0.0)
    total = jnp.sum(exponent, axis=1, keepdims=True)
    gradient = weight * (exponent * (1.0 / total) - labels)
    inner = gradient * logits
    row = jnp.square(a[:, :1]) * jnp.sum(inner, axis=1, keepdims=True)
    col = (b * b) * jnp.sum(inner, axis=0, keepdims=True)
    return gradient * scale, row, col, weight * jnp.log(total), weight * logits


def take_blocks(pool_ref, slot_ref, block, count, out_ref):
    for n in range(count):
        out_ref[n] = pool_ref[slot_ref[block * count + n]]


def pool_norms(pool_ref, norm_ref, bounds):
    step_slots = 4
    rows = step_slots * PBLK
    lane = lax.broadcasted_iota(jnp.int32, (rows, LANES), 1)

    def lane_sum(part):
        return jnp.sum(part, axis=1, keepdims=True)

    def step(i, carry):
        here = pl.ds(i * step_slots, step_slots)
        wide = pool_ref[here].reshape(rows, pool_ref.shape[2]).astype(F32)
        square = wide * wide
        result, before, inside = None, None, None
        for level, (low, high) in enumerate(bounds):
            if high < LANES:
                total = lane_sum(jnp.where(lane < high, square[:, :LANES], 0.0))
            else:
                start = low // LANES * LANES
                parts = [square[:, j : j + LANES] for j in range(start, high, LANES)]
                while len(parts) > 1:
                    parts = [x + y for x, y in zip(parts[::2], parts[1::2])]
                total = lane_sum(parts[0])
                if start:
                    total = total + before
            before = total
            result = jnp.broadcast_to(total, (rows, LANES)) if result is None else jnp.where(lane == level, total, result)
        norm_ref[here] = result.reshape(step_slots, PBLK, LANES)
        return carry

    lax.fori_loop(0, pool_ref.shape[0] // step_slots, step, 0, unroll=4)


def norm_rows(norm_ref, slot_ref, block, count):
    table = jnp.concatenate([norm_ref[slot_ref[block * count + n]] for n in range(count)], axis=0)
    return table.T[:8, :]


def pack_kernel(wanted_ref, block_hbm, out_hbm, block_ref, out_ref, in_sem, out_sem):
    load = pltpu.make_async_copy(block_hbm, block_ref, in_sem)
    load.start()
    load.wait()
    size = out_ref.shape[0] // CHUNKS
    for chunk in range(CHUNKS):

        def step(i, carry):
            d = chunk * size + i
            out_ref[d] = block_ref[jnp.maximum(wanted_ref[d], 0)]
            return carry

        lax.fori_loop(0, size, step, 0, unroll=8)
        part = pl.ds(chunk * size, size)
        pltpu.make_async_copy(out_ref.at[part], out_hbm.at[part], out_sem).start()
    pltpu.make_async_copy(out_ref, out_hbm, out_sem).wait()


def prep_kernel(bounds, rows, query_ref, ids_ref, pos_ref, scale_ref, full_ref, label_ref, mask_ref):
    blocks, cands = ids_ref.shape
    lane = lax.broadcasted_iota(jnp.int32, (rows, LANES), 1)

    def step(block, carry):
        here = pl.ds(block * rows, rows)
        total = jnp.zeros((rows, 1), F32)
        for level, (low, high) in enumerate(bounds):
            total = total + square_sums(query_ref[here, low:high])
            scale_ref[level, here, :] = jnp.broadcast_to(lax.rsqrt(total + EPS), (rows, LANES))
        full_ref[block] = to_row(total)
        first = query_ref[here, :LANES].astype(F32)
        split = bounds[0][1]
        mask_ref[0, here, :] = jnp.where(lane < split, first, 0.0).astype(BF16)
        mask_ref[1, here, :] = jnp.where(lane < split, 0.0, first).astype(BF16)
        label_ref[here, :] = jnp.where(ids_ref[pl.ds(block, 1), :] == to_col(pos_ref[pl.ds(block, 1), :]), 1.0, 0.0)
        return carry

    lax.fori_loop(0, blocks, step, 0)


def dots_kernel(
    shards, per_shard, rows, level, shifts, slot_ref, shard_ref, query_ref, pool_ref, full_ref, norm_ref, *refs
):
    outs, cand_ref = refs[:-1], refs[-1]
    count, _, width = cand_ref.shape
    shard = shard_ref[0]
    base = per_shard * rows
    for shift, out_ref in zip(shifts, outs):
        target = lax.rem(shard + shift, shards)
        for k in range(per_shard):
            block = target * per_shard + k
            take_blocks(pool_ref, slot_ref, block, count, cand_ref)
            query = query_ref[pl.ds(block * rows, rows), :]
            cand = cand_ref[...].reshape(count * PBLK, width)
            out_ref[k * rows : (k + 1) * rows, :] = contract(query, cand, 1, 1)
            out_ref[base + k : base + k + 1, :] = norm_rows(norm_ref, slot_ref, block, count)[level : level + 1, :]
            out_ref[base + per_shard : base + per_shard + 1, k * rows : (k + 1) * rows] = full_ref[block]


def first_dots_kernel(
    bounds, shards, per_shard, rows, shifts, slot_ref, shard_ref, query_ref, pool_ref, full_ref, norm_ref, *refs
):
    pool_norms(pool_ref, norm_ref, bounds)
    dots_kernel(
        shards, per_shard, rows, len(bounds) - 1, shifts, slot_ref, shard_ref, query_ref, pool_ref, full_ref, norm_ref, *refs
    )


def prefix_dots(bounds, rows, block, query_ref, mask_ref, cand_ref):
    here = pl.ds(block * rows, rows)
    cands = cand_ref.shape[0] * PBLK
    first = jnp.concatenate([mask_ref[0, here, :], query_ref[here, :LANES]], axis=0)
    both = contract(first, cand_ref[:, :, :LANES].reshape(cands, LANES), 1, 1)
    yield both[:rows]
    dots = both[rows:]
    yield dots
    for low, high in bounds[2:]:
        dots = dots + contract(query_ref[here, low:high], cand_ref[:, :, low:high].reshape(cands, high - low), 1, 1)
        yield dots


def low_kernel(
    bounds, rows, slot_ref, shard_ref, query_ref, pool_ref, norm_ref, ids_ref, scale_ref, label_ref, mask_ref, after_ref,
    coef_ref, row_ref, col_ref, loss_ref, cand_ref, term_ref,
):
    del after_ref
    count = cand_ref.shape[0]
    levels, _, cands = coef_ref.shape
    blocks = loss_ref.shape[0]

    @pl.when(shard_ref[0] == 0)
    def _():
        row_ref[...] = jnp.zeros_like(row_ref)
        col_ref[...] = jnp.zeros_like(col_ref)

        def step(block, carry):
            here = pl.ds(block * rows, rows)
            take_blocks(pool_ref, slot_ref, block, count, cand_ref)
            pp = norm_rows(norm_ref, slot_ref, block, count)
            live = ids_ref[pl.ds(block, 1), :] >= 0.0
            labels = label_ref[here, :]
            entropy = jnp.zeros((rows, 1), F32)
            logit_sum = jnp.zeros((rows, cands), F32)
            row_terms, col_terms = [], []
            sums = prefix_dots(bounds, rows, block, query_ref, mask_ref, cand_ref)
            for level, ((low, high), dots) in enumerate(zip(bounds, sums)):
                scale = scale_ref[level, here, :]
                scale = jnp.concatenate([scale] * (cands // LANES), axis=1)
                coef, row, col, part, logits = terms(
                    dots, scale, pp[level : level + 1, :], live, labels, float(high // MINP)
                )
                term_ref[level] = coef
                row_terms.append(row)
                col_terms.append(col)
                entropy = entropy + part
                logit_sum = logit_sum + logits
            loss = entropy - jnp.sum(labels * logit_sum, axis=1, keepdims=True)
            coef = jnp.zeros((rows, cands), F32)
            row = jnp.zeros((rows, 1), F32)
            col = jnp.zeros((1, cands), F32)
            for level in reversed(range(levels)):
                coef = coef + term_ref[level]
                row = row + row_terms[level]
                col = col + col_terms[level]
                coef_ref[level, here, :] = coef
                row_ref[block, level : level + 1, :] = to_row(row)
                col_ref[block, level : level + 1, :] = col
            loss_ref[pl.ds(block, 1), :] = to_row(loss)
            return carry

        lax.fori_loop(0, blocks, step, 0)

    @pl.when(shard_ref[0] != 0)
    def _():
        loss_ref[...] = jnp.zeros_like(loss_ref)


def high_kernel(shards, per_shard, rows, weights, shard_ref, ids_ref, label_ref, *refs):
    ins, outs, loss_ref = refs[:shards], refs[shards:-1], refs[-1]
    shard = shard_ref[0]
    base = per_shard * rows
    width = ids_ref.shape[1]
    in_half = [
        jnp.where(lax.rem(shard - shift + shards, shards) < shards // 2, 1.0, 0.0)
        for shift in range(shards)
    ]

    def total(span, keep):
        pieces = [ref[span, :] * scale if keep else ref[span, :] for ref, scale in zip(ins, in_half)]
        return (pieces[0] + pieces[1]) + (pieces[2] + pieces[3])

    below = slice(base, base + AUX)
    half_rows, half_cols, full_rows, full_cols, losses, coefs = [], [], [], [], [], []
    aux_half, aux_full = total(below, True), total(below, False)
    for k in range(per_shard):
        block = shard * per_shard + k
        ids = ids_ref[pl.ds(block, 1), :]
        live = ids >= 0.0
        labels = label_ref[pl.ds(block * rows, rows), :]
        span = slice(k * rows, (k + 1) * rows)
        results = []
        for keep, aux, weight in ((True, aux_half, weights[0]), (False, aux_full, weights[1])):
            scale = to_col(lax.rsqrt(aux[per_shard : per_shard + 1, span] + EPS))
            results.append(terms(total(span, keep), scale, aux[k : k + 1, :], live, labels, weight))
        (coef_h, row_h, col_h, part_h, logit_h), (coef_f, row_f, col_f, part_f, logit_f) = results
        loss = part_h + part_f - jnp.sum(labels * (logit_h + logit_f), axis=1, keepdims=True)
        coefs.append(((coef_h + coef_f).astype(BF16), coef_f.astype(BF16)))
        half_rows.append(to_row(row_h + row_f))
        full_rows.append(to_row(row_f))
        half_cols.append(col_h + col_f)
        full_cols.append(col_f)
        losses.append(to_row(loss))
    loss_ref[...] = jnp.concatenate(losses, axis=1)

    def aux_rows(rows_list, cols_list):
        line = jnp.concatenate(rows_list + [jnp.zeros((1, width - base), F32)], axis=1)
        table = jnp.concatenate(cols_list + [line], axis=0)
        table = jnp.concatenate([table, jnp.zeros((AUX - table.shape[0], width), F32)], axis=0)
        first = table.astype(BF16).astype(F32)
        second = (table - first).astype(BF16).astype(F32)
        third = table - first - second
        return jnp.concatenate([first, second, third, jnp.zeros_like(table)], axis=0).astype(BF16)

    aux = (aux_rows(half_rows, half_cols), aux_rows(full_rows, full_cols))
    for shift in range(shards):
        out_ref = outs[shift]
        high_target = lax.rem(shard + shift, shards) >= shards // 2
        for which, chosen in ((1, high_target), (0, jnp.logical_not(high_target))):

            @pl.when(chosen)
            def _():
                for k in range(per_shard):
                    out_ref[k * rows : (k + 1) * rows, :] = coefs[k][which]
                out_ref[base : base + COEF_AUX, :] = aux[which]


def unpack_aux(ref, base):
    packed = ref[base : base + COEF_AUX, :].astype(F32)
    return packed[:AUX] + packed[AUX : 2 * AUX] + packed[2 * AUX : 3 * AUX]


def passage_kernel(
    bounds, shards, per_shard, rows, slot_ref, shard_ref, query_ref, pool_ref, mask_ref, low_col_ref, low_coef_ref, *refs
):
    ins = refs[:shards]
    out_hbm, half_hbm, coef_ref, col_ref, spread_ref, sum_ref, scale_ref, out_ref, half_ref, out_sem, half_sem = refs[shards:]
    shard = shard_ref[0]
    base = per_shard * rows
    blocks = shards * per_shard
    slots, _, width = pool_ref.shape
    cands = coef_ref.shape[1]
    count = cands // PBLK

    scale_ref[...] = jnp.zeros_like(scale_ref)
    for shift in range(shards):
        source = lax.rem(shard - shift + shards, shards)
        coef_ref[pl.ds(source * base, base), :] = ins[shift][:base, :]
        aux = unpack_aux(ins[shift], base)
        for k in range(per_shard):
            col_ref[source * per_shard + k] = aux[k : k + 1, :]

    def add_scales(block, low):
        cols = jnp.broadcast_to(col_ref[block], (8, cands))
        if low:
            cols = cols + low_col_ref[block]
        col_cols = columns(cols)
        for n in range(count):
            slot = slot_ref[block * count + n]
            scale_ref[slot] = scale_ref[slot] + col_cols[n * PBLK : (n + 1) * PBLK, :]

    def send(start, end):
        done = pl.ds(start, end - start)
        pltpu.make_async_copy(out_ref.at[:, :, done], out_hbm.at[:, :, done], out_sem).start()

    @pl.when(shard == 0)
    def _():
        sum_ref[...] = jnp.zeros_like(sum_ref)
        levels = len(bounds)

        def step(block, carry):
            here = pl.ds(block * rows, rows)
            add_scales(block, True)
            base_coef = coef_ref[here, :].astype(F32)
            coefs = [(base_coef + low_coef_ref[level, here, :]).astype(BF16) for level in range(levels)]
            for level in range(levels):
                half_ref[level, here, :] = coefs[level]
            grads = [contract(coefs[0], mask_ref[0, here, :], 0, 0) + contract(coefs[1], mask_ref[1, here, :], 0, 0)]
            starts = [0]
            for level in range(2, levels):
                lo, hi = bounds[level]
                grads.append(contract(coefs[level], query_ref[here, lo:hi], 0, 0))
                starts.append(lo)
            for n in range(count):
                slot = slot_ref[block * count + n]
                for start, grad in zip(starts, grads):
                    lanes = slice(start, start + grad.shape[1])
                    sum_ref[slot, :, lanes] = sum_ref[slot, :, lanes] + grad[n * PBLK : (n + 1) * PBLK, :]
            return carry

        lax.fori_loop(0, blocks, step, 0)
        copy = pltpu.make_async_copy(half_ref, half_hbm, half_sem)
        copy.start()
        first = lax.broadcasted_iota(jnp.int32, (1, LANES), 1) < bounds[0][1]
        step_slots = slots // CHUNKS
        for chunk in range(CHUNKS):
            part = pl.ds(chunk * step_slots, step_slots)

            def finish(i, carry):
                slot = chunk * step_slots + i
                scale = scale_ref[slot]
                wide = [jnp.where(first, scale[:, 0:1], scale[:, 1:2])]
                for level in range(2, levels):
                    lo, hi = bounds[level]
                    wide.append(jnp.broadcast_to(scale[:, level : level + 1], (PBLK, hi - lo)))
                pool = pool_ref[slot].astype(F32)
                out_ref[slot] = (sum_ref[slot] - jnp.concatenate(wide, axis=1) * pool).astype(BF16)
                return carry

            lax.fori_loop(0, step_slots, finish, 0, unroll=4)
            pltpu.make_async_copy(out_ref.at[part], out_hbm.at[part], out_sem).start()
        copy.wait()
        pltpu.make_async_copy(out_ref, out_hbm, out_sem).wait()

    @pl.when(shard != 0)
    def _():
        spread_ref[...] = jnp.zeros_like(spread_ref)
        for block in range(blocks):
            add_scales(block, False)
            turned = coef_ref[pl.ds(block * rows, rows), :].astype(F32).T.astype(BF16)
            for n in range(count):
                spread_ref[slot_ref[block * count + n], :, block * rows : (block + 1) * rows] = turned[
                    n * PBLK : (n + 1) * PBLK, :
                ]
        spread = spread_ref[0:slots].reshape(slots * PBLK, blocks * rows)
        scale = scale_ref[0:slots].reshape(slots * PBLK, LANES)[:, 0:1]
        for start in range(0, width, PIECE):
            end = start + PIECE
            grad = contract(spread, query_ref[:, start:end], 1, 0)
            pool = pool_ref[:, :, start:end].reshape(slots * PBLK, end - start).astype(F32)
            out_ref[:, :, start:end] = (grad - scale * pool).astype(BF16).reshape(slots, PBLK, end - start)
            send(start, end)
        pltpu.make_async_copy(out_ref, out_hbm, out_sem).wait()


def query_kernel(
    bounds, shards, per_shard, rows, loss_scale, slot_ref, shard_ref, query_ref, pool_ref, low_row_ref, low_loss_ref,
    high_loss_ref, low_half_hbm, *refs
):
    ins = refs[:shards]
    query_grad_ref, loss_ref = refs[shards : shards + 2]
    cand_ref, coef_ref, row_ref, low_half_ref, sem = refs[shards + 2 :]
    shard = shard_ref[0]
    base = per_shard * rows
    blocks = shards * per_shard
    count = cand_ref.shape[0]
    width = query_ref.shape[1]
    cands = coef_ref.shape[1]
    copy = pltpu.make_async_copy(low_half_hbm, low_half_ref, sem)

    @pl.when(shard == 0)
    def _():
        copy.start()

    for shift in range(shards):
        source = lax.rem(shard - shift + shards, shards)
        coef_ref[pl.ds(source * base, base), :] = ins[shift][:base, :]
        aux = unpack_aux(ins[shift], base)
        for k in range(per_shard):
            row_ref[source * per_shard + k] = aux[per_shard : per_shard + 1, k * rows : (k + 1) * rows]
    for block in range(blocks):
        j = block % per_shard
        loss_ref[block // per_shard : block // per_shard + 1, j * rows : (j + 1) * rows] = low_loss_ref[block : block + 1, :]
    loss_ref[pl.ds(shard, 1), :] = loss_ref[pl.ds(shard, 1), :] + high_loss_ref[...]
    loss_ref[...] = loss_ref[...] * loss_scale

    def run(spans, low):
        def step(block, carry):
            take_blocks(pool_ref, slot_ref, block, count, cand_ref)
            rows_here = jnp.broadcast_to(row_ref[block], (8, rows))
            if low:
                rows_here = rows_here + low_row_ref[block]
            row_cols = columns(rows_here)
            here = pl.ds(block * rows, rows)
            for level, (lo, hi) in enumerate(spans):
                coef = low_half_ref[level, here, :] if low else coef_ref[here, :]
                query = query_ref[here, lo:hi].astype(F32)
                cand = cand_ref[:, :, lo:hi].reshape(cands, hi - lo)
                grad = contract(coef, cand, 1, 0) - row_cols[:rows, level : level + 1] * query
                query_grad_ref[here, lo:hi] = grad.astype(BF16)
            return carry

        lax.fori_loop(0, blocks, step, 0)

    @pl.when(shard == 0)
    def _():
        copy.wait()
        run(bounds, True)

    @pl.when(shard != 0)
    def _():
        run([(0, width)], False)


def collect_kernel(target_ref, back_hbm, out_ref, back_ref, sem):
    rows = out_ref.shape[0]
    count = back_ref.shape[0]
    copy = pltpu.make_async_copy(back_hbm, back_ref, sem)
    copy.start()
    here = lax.broadcasted_iota(jnp.int32, (rows, count), 0)
    choose = jnp.where(here == target_ref[...], 1.0, 0.0).astype(BF16)
    copy.wait()
    out_ref[...] = contract(choose, back_ref[...], 1, 0).astype(BF16)


def per_device(queries, passages, neg_lists, positives):
    peers = lax.axis_size("dp")
    shards = lax.axis_size("tensor")
    total_rows, width = queries.shape
    blocks = neg_lists.shape[0] // peers
    count = neg_lists.shape[1]
    rows = total_rows // blocks
    local_blocks = passages.shape[0] // PBLK
    cands = count * PBLK
    per_shard = blocks // shards
    base = per_shard * rows
    slots = peers
    my_index = lax.axis_index("dp")
    shard = lax.axis_index("tensor")
    sizes = [MINP * 2**level for level in range(NPRE)]
    low_sizes = [size for size in sizes if size <= width]
    high_sizes = [size for size in sizes if size > width]
    assert high_sizes == [width * shards // 2, width * shards] and low_sizes[-1] == width
    assert shards == 4 and base == LANES
    bounds = list(zip([0] + low_sizes[:-1], low_sizes))
    levels = len(bounds)
    weight_total = sum(size / MINP for size in sizes)

    flat = neg_lists.reshape(peers, blocks * count)
    mine = (flat >= 0) & (flat // local_blocks == my_index)
    wanted = jnp.max(jnp.where(mine, flat % local_blocks, -1), axis=1)
    own = lax.dynamic_slice_in_dim(neg_lists, my_index * blocks, blocks, 0)
    valid = own >= 0
    slot = jnp.where(valid, own // local_blocks, 0).reshape(blocks * count)
    spare_slot = jnp.where(valid, own // local_blocks, slots).reshape(blocks * count)
    within = jnp.arange(PBLK, dtype=jnp.int32)
    ids = jnp.where(valid[:, :, None], own[:, :, None] * PBLK + within[None, None, :], -1)
    ids = ids.reshape(blocks, cands).astype(F32)
    target = jnp.where(wanted[:, None] >= 0, wanted[:, None] * PBLK + within[None, :], -1).reshape(1, slots * PBLK)
    pos = positives.reshape(blocks, rows).astype(F32)
    shard_arr = shard.reshape(1).astype(jnp.int32)
    pool_shape = (slots, PBLK, width)

    pinned = partial(pltpu.with_memory_space_constraint, memory_space=pltpu.HBM)
    panels = pl.pallas_call(
        pack_kernel,
        out_shape=pltpu.HBM(pool_shape, BF16),
        in_specs=[smem(), hbm()],
        out_specs=hbm(),
        scratch_shapes=[
            pltpu.VMEM((local_blocks, PBLK, width), BF16),
            pltpu.VMEM(pool_shape, BF16),
            pltpu.SemaphoreType.DMA(()),
            pltpu.SemaphoreType.DMA(()),
        ],
        compiler_params=params(),
        name="pack",
    )(wanted, pinned(passages.reshape(local_blocks, PBLK, width)))
    pool = lax.all_to_all(panels, "dp", split_axis=0, concat_axis=0, tiled=True)
    scales, full_norms, labels, masked = pl.pallas_call(
        partial(prep_kernel, bounds, rows),
        out_shape=[
            jax.ShapeDtypeStruct((levels, total_rows, LANES), F32),
            jax.ShapeDtypeStruct((blocks, 1, rows), F32),
            jax.ShapeDtypeStruct((total_rows, cands), F32),
            jax.ShapeDtypeStruct((2, total_rows, LANES), BF16),
        ],
        in_specs=[vmem()] * 3,
        out_specs=[vmem()] * 4,
        compiler_params=params(),
        name="prep",
    )(queries, ids, pos)

    def shift_by(part, s):
        return lax.ppermute(part, "tensor", [(i, (i + s) % shards) for i in range(shards)])

    cand_scratch = pltpu.VMEM((count, PBLK, width), BF16)
    message = jax.ShapeDtypeStruct((base + AUX, cands), F32)
    norm_shape = (slots, PBLK, LANES)
    norms, far, right, left = pl.pallas_call(
        partial(first_dots_kernel, bounds, shards, per_shard, rows, (2, 1, 3)),
        out_shape=[jax.ShapeDtypeStruct(norm_shape, F32)] + [message] * 3,
        in_specs=[smem(), smem(), vmem(), vmem(), vmem()],
        out_specs=[vmem()] * 4,
        scratch_shapes=[cand_scratch],
        compiler_params=params(),
        name="dots",
    )(slot, shard_arr, queries, pool, full_norms)
    (here,) = pl.pallas_call(
        partial(dots_kernel, shards, per_shard, rows, levels - 1, (0,)),
        out_shape=[message],
        in_specs=[smem(), smem()] + [vmem()] * 4,
        out_specs=[vmem()],
        scratch_shapes=[cand_scratch],
        compiler_params=params(),
        name="dots_own",
    )(slot, shard_arr, queries, pool, full_norms, norms)
    arrived = [here, shift_by(right, 1), shift_by(far, 2), shift_by(left, 3)]

    *coefs, high_loss = pl.pallas_call(
        partial(high_kernel, shards, per_shard, rows, [size / MINP for size in high_sizes]),
        out_shape=[jax.ShapeDtypeStruct((base + COEF_AUX, cands), BF16)] * shards
        + [jax.ShapeDtypeStruct((1, base), F32)],
        in_specs=[smem()] + [vmem()] * (2 + shards),
        out_specs=[vmem()] * (shards + 1),
        compiler_params=params(),
        name="high",
    )(shard_arr, ids, labels, *arrived)
    low_coef, low_row, low_col, low_loss = pl.pallas_call(
        partial(low_kernel, bounds, rows),
        out_shape=[
            jax.ShapeDtypeStruct((levels, total_rows, cands), F32),
            jax.ShapeDtypeStruct((blocks, 8, rows), F32),
            jax.ShapeDtypeStruct((blocks, 8, cands), F32),
            jax.ShapeDtypeStruct((blocks, rows), F32),
        ],
        in_specs=[smem(), smem()] + [vmem()] * 7 + [pl.BlockSpec(memory_space=pl.ANY)],
        out_specs=[vmem()] * 4,
        scratch_shapes=[cand_scratch, pltpu.VMEM((levels, rows, cands), F32)],
        compiler_params=params(),
        name="low",
    )(slot, shard_arr, queries, pool, norms, ids, scales, labels, masked, high_loss)
    coefs = [coefs[0]] + [shift_by(coefs[s], s) for s in range(1, shards)]

    half_shape = (levels, total_rows, cands)
    slot_grad, low_half = pl.pallas_call(
        partial(passage_kernel, bounds, shards, per_shard, rows),
        out_shape=[pltpu.HBM(pool_shape, BF16), pltpu.HBM(half_shape, BF16)],
        in_specs=[smem(), smem()] + [vmem()] * (5 + shards),
        out_specs=[hbm()] * 2,
        scratch_shapes=[
            pltpu.VMEM((total_rows, cands), BF16),
            pltpu.VMEM((blocks, 1, cands), F32),
            pltpu.VMEM((slots + 1, PBLK, total_rows), BF16),
            pltpu.VMEM((slots + 1, PBLK, width), F32),
            pltpu.VMEM((slots + 1, PBLK, LANES), F32),
            pltpu.VMEM(pool_shape, BF16),
            pltpu.VMEM(half_shape, BF16),
            pltpu.SemaphoreType.DMA(()),
            pltpu.SemaphoreType.DMA(()),
        ],
        compiler_params=params(),
        name="passage",
    )(spare_slot, shard_arr, queries, pool, masked, low_col, low_coef, *coefs)
    back = lax.all_to_all(slot_grad, "dp", split_axis=0, concat_axis=0, tiled=True)

    query_grad, loss = pl.pallas_call(
        partial(query_kernel, bounds, shards, per_shard, rows, 1.0 / weight_total),
        out_shape=[
            jax.ShapeDtypeStruct((total_rows, width), BF16),
            jax.ShapeDtypeStruct((shards, base), F32),
        ],
        in_specs=[smem(), smem()] + [vmem()] * 5 + [hbm()] + [vmem()] * shards,
        out_specs=[vmem()] * 2,
        scratch_shapes=[
            cand_scratch,
            pltpu.VMEM((total_rows, cands), BF16),
            pltpu.VMEM((blocks, 1, rows), F32),
            pltpu.VMEM(half_shape, BF16),
            pltpu.SemaphoreType.DMA(()),
        ],
        compiler_params=params(),
        name="query",
    )(slot, shard_arr, queries, pool, low_row, low_loss, high_loss, pinned(low_half), *coefs)
    loss = lax.psum(loss, "tensor")

    passage_grad = pl.pallas_call(
        collect_kernel,
        out_shape=jax.ShapeDtypeStruct((local_blocks * PBLK, width), BF16),
        in_specs=[vmem(), hbm()],
        out_specs=vmem(),
        scratch_shapes=[pltpu.VMEM((slots * PBLK, width), BF16), pltpu.SemaphoreType.DMA(())],
        compiler_params=params(),
        name="collect",
    )(target, pinned(back.reshape(slots * PBLK, width)))
    return (
        query_grad,
        passage_grad,
        loss.reshape(total_rows),
    )


def solution(mesh):
    return jax.shard_map(
        per_device,
        mesh=mesh,
        in_specs=(P("dp", "tensor"), P("dp", "tensor"), P(), P("dp")),
        out_specs=(P("dp", "tensor"), P("dp", "tensor"), P("dp")),
        check_vma=False,
    )
```

time: 226 us -> 167 us (0.74)
  Pallas kernels: 94.1 us -> 31.6 us
  waiting for transfers between devices: 98.6 us -> 87.2 us
  blocking collectives: 0 us -> 7.38 us
  local copies, waits for them, and re-layouts: 2.31 us -> 7.76 us
    pallas_call x1, Pallas kernels: 65.2 us -> 2.98 us  [per_device(): pl.pallas_call(pack_kernel, out_shape=pltpu.HBM(pool_shape, BF16), in_spe...]
    all_to_all x1, waiting for transfers between devices: 45.1 us -> 37.3 us  [per_device(): lax.all_to_all(slot_grad, 'dp', split_axis=0, concat_axis=0, tiled=True)]
    psum x0 -> x1, blocking collectives: none -> 7.38 us  [per_device(): loss = lax.psum(loss, 'tensor')]
    unnamed x9 -> x19, local copies, waits for them, and re-layouts: 0.69 us -> 6.14 us
    all_to_all x1, waiting for transfers between devices: 49.7 us -> 46.5 us  [per_device(): pool = lax.all_to_all(panels, 'dp', split_axis=0, concat_axis=0, tiled=True)]
  transfers between devices with their start and end apart: 8 -> 8, of which waited for: 4 -> 3; matrix products, arithmetic and copies ran while one was open for 1% -> 1% of each run, Pallas kernels for 6% -> 8%
where the time goes in v3:
time: 167 us; the launch traced here: 166 us
  waiting for transfers between devices  87.2 us (52%)
  Pallas kernels  31.6 us (19%)
  starting transfers between devices  30.2 us (18%)
  local copies, waits for them, and re-layouts  7.76 us (5%)
  blocking collectives  7.38 us (4%)
    all_to_all x1, waiting for transfers between devices, per_device(): pool = lax.all_to_all(panels, 'dp', split_axis=0, concat_axis=0, tiled=True)  46.5 us
    all_to_all x1, waiting for transfers between devices, per_device(): lax.all_to_all(slot_grad, 'dp', split_axis=0, concat_axis=0, tiled=True)  37.3 us
    all_to_all x1, starting transfers between devices, per_device(): pool = lax.all_to_all(panels, 'dp', split_axis=0, concat_axis=0, tiled=True)  13.3 us
    ppermute x6, starting transfers between devices, shift_by(): lax.ppermute(part, 'tensor', [(i, (i + s) % shards) for i in range(shards)])  9.05 us
    all_to_all x1, starting transfers between devices, per_device(): lax.all_to_all(slot_grad, 'dp', split_axis=0, concat_axis=0, tiled=True)  7.82 us
    pallas_call x1, Pallas kernels, per_device(): pl.pallas_call(partial(passage_kernel, bounds, shards, per_shard, rows),...  7.6 us
    psum x1, blocking collectives, per_device(): loss = lax.psum(loss, 'tensor')  7.38 us
    pallas_call x1, Pallas kernels, per_device(): pl.pallas_call(partial(query_kernel, bounds, shards, per_shard, rows, 1.0...  6.27 us
  transfers between devices with their start and end apart: 8, of which 3 were waited for; matrix products, arithmetic and copies ran while one was open for 1% of the time, Pallas kernels for 8%

profile of v3, /device:TPU:1, one launch (start us, length us, event | category | flops | bytes accessed | tf_op | source)
XLA Modules:
  0.0 166.0 jit_solution(3565575781212055289)
XLA Ops:
  0.6 0.8 fusion.2
  1.4 0.1 reduce_max.14
  1.5 0.1 reduce_max.18.wanted_ref
  1.7 3.0 %pack.1 = bf16[64,16,1024]{2,1,0:T(8,128)(2,1)} custom-call(s32[64]{0:T(128)S(1)} %reduce_max.18.wanted_ref, bf16[16,16,1024]{2,1,0:T(8,128)(2,1)} %bitcast.5), custom_call_target="tpu_custom_call" | custom-call | tf_op jit(solution)/shard_map/pack/pallas_call | solution.py:536
  4.6 0.0 copy-start.8
  4.7 0.0 copy-start
  4.7 13.3 %all-to-all-start = ((bf16[64,16,1024]{2,1,0:T(8,128)(2,1)}), bf16[64,16,1024]{2,1,0:T(8,128)(2,1)S(1)}, u32[]{:S(2)}, u32[]{:S(2)}) async-start(bf16[64,16,1024]{2,1,0:T(8,128)(2,1)} %pack.1), calls=%async_computation | async-start | bytes 4194304 | tf_op jit(solution)/shard_map/all_to_all | solution.py:550
  18.0 0.8 constant_dynamic-slice_fusion
  18.7 0.1 copy.16
  18.8 0.1 reshape.80.slot_ref
  18.9 0.1 broadcast_in_dim.39
  19.0 0.1 broadcast_in_dim.40
  19.1 0.1 add.58
  19.2 0.1 add.59
  19.3 0.1 add.61
  19.4 0.0 copy-done.8
  19.4 0.1 convert_element_type.10.pos_ref
  19.5 0.0 copy-done
  19.5 1.4 prep.1
  20.9 0.0 copy-start.3
  20.9 0.8 copy-done.3
  21.7 0.0 copy-start.6
  21.7 1.1 copy-done.6
  22.8 46.5 %all-to-all-done.pool_ref = bf16[64,16,1024]{2,1,0:T(8,128)(2,1)S(1)} async-done(((bf16[64,16,1024]{2,1,0:T(8,128)(2,1)}), bf16[64,16,1024]{2,1,0:T(8,128)(2,1)S(1)}, u32[]{:S(2)}, u32[]{:S(2)}) %all-to-all-start) | async-done | bytes 2097184 | tf_op jit(solution)/shard_map/all_to_all | solution.py:550
  69.2 2.6 %dots.1 = (f32[64,16,128]{2,1,0:T(8,128)S(1)}, f32[136,256]{1,0:T(8,128)S(1)}, f32[136,256]{1,0:T(8,128)S(1)}, f32[136,256]{1,0:T(8,128)S(1)}) custom-call(s32[128]{0:T(128)S(1)} %reshape.80.slot_ref, s32[1]{0:T(128)} %bitcast.shard_ref, bf16[512,1024]{1,0:T(8,128)(2,1)S(1)} %copy-done, bf16[64,16,1024]{2,1,0:T(8,128)(2,1)S(1)} %all-to-all-done.pool_ref, ...), custom_call_target="tpu_custom_call" | custom-call | tf_op jit(solution)/shard_map/dots/pallas_call | solution.py:571
  71.8 0.0 copy-start.4
  71.8 1.3 collective-permute-start
  73.1 2.4 %collective-permute-start.1 = (f32[136,256]{1,0:T(8,128)S(1)}, f32[136,256]{1,0:T(8,128)S(1)}, u32[]{:S(2)}, u32[]{:S(2)}) collective-permute-start(f32[136,256]{1,0:T(8,128)S(1)} %get-tuple-element.30), channel_id=1, source_target_pairs={{0,2},{1,3},{2,0},{3,1},{4,6},{5,7},{6,4},{7,5},{8,10},{9,11},{10,... | collective-permute-start | bytes 417800 | tf_op jit(solution)/shard_map/ppermute | solution.py:566
  75.6 1.2 collective-permute-start.2
  76.7 1.0 dots_own.1.refs_0_
  77.7 0.0 copy-start.1
  77.7 0.8 copy-done.1
  78.5 0.0 collective-permute-done.refs_1_
  78.5 3.4 %collective-permute-done.1.refs_2_ = f32[136,256]{1,0:T(8,128)S(1)} collective-permute-done((f32[136,256]{1,0:T(8,128)S(1)}, f32[136,256]{1,0:T(8,128)S(1)}, u32[]{:S(2)}, u32[]{:S(2)}) %collective-permute-start.1) | collective-permute-done | bytes 139296 | tf_op jit(solution)/shard_map/ppermute | solution.py:566
  82.0 0.0 collective-permute-done.2.refs_3_
  82.0 0.0 copy-done.4
  82.0 1.2 high.1
  83.2 1.1 collective-permute-start.3
  84.2 2.2 %collective-permute-start.4 = (bf16[160,256]{1,0:T(8,128)(2,1)}, bf16[160,256]{1,0:T(8,128)(2,1)}, u32[]{:S(2)}, u32[]{:S(2)}) collective-permute-start(bf16[160,256]{1,0:T(8,128)(2,1)} %get-tuple-element.39), channel_id=1, source_target_pairs={{0,2},{1,3},{2,0},{3,1},{4,6},{5,7},{6,4},{7,5},{8,10},{9,11},{10,... | collective-permute-start | bytes 245768 | tf_op jit(solution)/shard_map/ppermute | solution.py:566
  86.4 0.9 collective-permute-start.5
  87.3 0.1 reshape.83.slot_ref
  87.4 0.0 copy-start.2
  87.4 1.0 copy-done.2
  88.5 0.0 copy-start.5
  88.5 1.0 copy-done.5
  89.5 0.0 copy-start.7
  89.5 1.3 copy-done.7
  90.8 5.4 %low.1 = (f32[5,512,256]{2,1,0:T(8,128)S(1)}, f32[8,8,64]{2,1,0:T(8,128)S(1)}, f32[8,8,256]{2,1,0:T(8,128)S(1)}, f32[8,64]{1,0:T(8,128)S(1)}) custom-call(s32[128]{0:T(128)S(1)} %reshape.80.slot_ref, s32[1]{0:T(128)} %bitcast.shard_ref, bf16[512,1024]{1,0:T(8,128)(2,1)S(1)} %copy-done, bf16[64,16,1024]{2,1,0:T(8,128)(2,1)S(1)} %all-to-all-done.pool_ref, ...), custom_call_target="tpu_custom_call" | custom-call | tf_op jit(solution)/shard_map/low/pallas_call | solution.py:600
  96.3 0.0 collective-permute-done.3.refs_1_
  96.3 0.0 collective-permute-done.4.refs_2_
  96.3 0.0 collective-permute-done.5.refs_3_
  96.3 7.6 %passage.1 = (bf16[64,16,1024]{2,1,0:T(8,128)(2,1)}, bf16[5,512,256]{2,1,0:T(8,128)(2,1)}) custom-call(s32[128]{0:T(128)S(1)} %reshape.83.slot_ref, s32[1]{0:T(128)} %bitcast.shard_ref, bf16[512,1024]{1,0:T(8,128)(2,1)S(1)} %copy-done, bf16[64,16,1024]{2,1,0:T(8,128)(2,1)S(1)} %all-to-all-done.pool_ref, bf16[2,512,128]{2,1,0:T(8,128)(2,1)S(1)} %get-tuple-element.28.mask_ref, ...), custom_call_target="tpu_custom_call" | custom-call | tf_op jit(solution)/shard_map/passage/pallas_call | solution.py:617
  103.9 7.8 %all-to-all-start.1 = ((bf16[64,16,1024]{2,1,0:T(8,128)(2,1)}), bf16[64,16,1024]{2,1,0:T(8,128)(2,1)}, u32[]{:S(2)}, u32[]{:S(2)}) async-start(bf16[64,16,1024]{2,1,0:T(8,128)(2,1)} %get-tuple-element.43), calls=%async_computation.1 | async-start | bytes 4194304 | tf_op jit(solution)/shard_map/all_to_all | solution.py:636
  111.8 0.1 add_select_fusion.2
  111.9 0.1 select_n.63.target_ref
  111.9 6.3 %query.1 = (bf16[512,1024]{1,0:T(8,128)(2,1)}, f32[4,128]{1,0:T(4,128)S(1)}) custom-call(s32[128]{0:T(128)S(1)} %reshape.80.slot_ref, s32[1]{0:T(128)} %bitcast.shard_ref, bf16[512,1024]{1,0:T(8,128)(2,1)S(1)} %copy-done, bf16[64,16,1024]{2,1,0:T(8,128)(2,1)S(1)} %all-to-all-done.pool_ref, f32[8,8,64]{2,1,0:T(8,128)S(1)} %get-tuple-element.33.low_row_ref, ...), custom_call_target="tpu_custom_call" | custom-call | tf_op jit(solution)/shard_map/query/pallas_call | solution.py:638
  118.2 7.4 %psum.7 = f32[512]{0:T(512)} all-reduce(f32[512]{0:T(512)S(1)} %bitcast.4), channel_id=1, replica_groups=mesh['dp'=64,'tensor'=4] {'tensor'}, use_global_device_ids=true, to_apply=%region_2.3 | all-reduce | flops 512 | bytes 4096 | tf_op jit(solution)/shard_map/psum | solution.py:656
  125.6 37.3 %all-to-all-done.1 = bf16[64,16,1024]{2,1,0:T(8,128)(2,1)} async-done(((bf16[64,16,1024]{2,1,0:T(8,128)(2,1)}), bf16[64,16,1024]{2,1,0:T(8,128)(2,1)}, u32[]{:S(2)}, u32[]{:S(2)}) %all-to-all-start.1) | async-done | bytes 2097184 | tf_op jit(solution)/shard_map/all_to_all | solution.py:636
  162.9 3.1 %collect.1 = bf16[256,1024]{1,0:T(8,128)(2,1)} custom-call(s32[1,1024]{1,0:T(1,128)S(1)} %select_n.63.target_ref, bf16[1024,1024]{1,0:T(8,128)(2,1)} %bitcast.2.back_hbm), custom_call_target="tpu_custom_call" | custom-call | tf_op jit(solution)/shard_map/collect/pallas_call | solution.py:658
  (7 shorter events, 0.0 us)
Async XLA Ops:
  4.6 14.8 %copy-start.8 = (s32[512]{0:T(512)S(1)}, s32[512]{0:T(512)}, u32[]{:S(2)}) copy-start(s32[512]{0:T(512)} %param.7) | copy-start | bytes 6148
  4.7 14.8 %copy-start = (bf16[512,1024]{1,0:T(8,128)(2,1)S(1)}, bf16[512,1024]{1,0:T(8,128)(2,1)}, u32[]{:S(2)}) copy-start(bf16[512,1024]{1,0:T(8,128)(2,1)} %query_ref.11) | copy-start | bytes 3145732
  4.7 64.6 %all-to-all-start = ((bf16[64,16,1024]{2,1,0:T(8,128)(2,1)}), bf16[64,16,1024]{2,1,0:T(8,128)(2,1)S(1)}, u32[]{:S(2)}, u32[]{:S(2)}) async-start(bf16[64,16,1024]{2,1,0:T(8,128)(2,1)} %pack.1), calls=%async_computation | async-start | bytes 4194304 | tf_op jit(solution)/shard_map/all_to_all | solution.py:550
  20.9 0.8 copy-start.3
  21.7 1.1 copy-start.6
  71.8 10.1 %copy-start.4 = (f32[512,256]{1,0:T(8,128)S(1)}, f32[512,256]{1,0:T(8,128)}, u32[]{:S(2)}) copy-start(f32[512,256]{1,0:T(8,128)} %copy-done.3) | copy-start | bytes 1572868
  71.8 6.7 %collective-permute-start = (f32[136,256]{1,0:T(8,128)S(1)}, f32[136,256]{1,0:T(8,128)S(1)}, u32[]{:S(2)}, u32[]{:S(2)}) collective-permute-start(f32[136,256]{1,0:T(8,128)S(1)} %get-tuple-element.29), channel_id=1, source_target_pairs={{0,1},{1,2},{2,3},{3,0},{4,5},{5,6},{6,7},{7,4},{8,9},{9,10},{10,1... | collective-permute-start | bytes 417800 | tf_op jit(solution)/shard_map/ppermute | solution.py:566
  73.1 8.8 %collective-permute-start.1 = (f32[136,256]{1,0:T(8,128)S(1)}, f32[136,256]{1,0:T(8,128)S(1)}, u32[]{:S(2)}, u32[]{:S(2)}) collective-permute-start(f32[136,256]{1,0:T(8,128)S(1)} %get-tuple-element.30), channel_id=1, source_target_pairs={{0,2},{1,3},{2,0},{3,1},{4,6},{5,7},{6,4},{7,5},{8,10},{9,11},{10,... | collective-permute-start | bytes 417800 | tf_op jit(solution)/shard_map/ppermute | solution.py:566
  75.6 6.4 %collective-permute-start.2 = (f32[136,256]{1,0:T(8,128)S(1)}, f32[136,256]{1,0:T(8,128)S(1)}, u32[]{:S(2)}, u32[]{:S(2)}) collective-permute-start(f32[136,256]{1,0:T(8,128)S(1)} %get-tuple-element.31), channel_id=1, source_target_pairs={{0,3},{1,0},{2,1},{3,2},{4,7},{5,4},{6,5},{7,6},{8,11},{9,8},{10,9... | collective-permute-start | bytes 417800 | tf_op jit(solution)/shard_map/ppermute | solution.py:566
  77.7 0.8 copy-start.1
  83.2 13.1 %collective-permute-start.3 = (bf16[160,256]{1,0:T(8,128)(2,1)}, bf16[160,256]{1,0:T(8,128)(2,1)}, u32[]{:S(2)}, u32[]{:S(2)}) collective-permute-start(bf16[160,256]{1,0:T(8,128)(2,1)} %get-tuple-element.38), channel_id=1, source_target_pairs={{0,1},{1,2},{2,3},{3,0},{4,5},{5,6},{6,7},{7,4},{8,9},{9,10},{10,1... | collective-permute-start | bytes 245768 | tf_op jit(solution)/shard_map/ppermute | solution.py:566
  84.2 12.0 %collective-permute-start.4 = (bf16[160,256]{1,0:T(8,128)(2,1)}, bf16[160,256]{1,0:T(8,128)(2,1)}, u32[]{:S(2)}, u32[]{:S(2)}) collective-permute-start(bf16[160,256]{1,0:T(8,128)(2,1)} %get-tuple-element.39), channel_id=1, source_target_pairs={{0,2},{1,3},{2,0},{3,1},{4,6},{5,7},{6,4},{7,5},{8,10},{9,11},{10,... | collective-permute-start | bytes 245768 | tf_op jit(solution)/shard_map/ppermute | solution.py:566
  86.4 9.9 %collective-permute-start.5 = (bf16[160,256]{1,0:T(8,128)(2,1)}, bf16[160,256]{1,0:T(8,128)(2,1)}, u32[]{:S(2)}, u32[]{:S(2)}) collective-permute-start(bf16[160,256]{1,0:T(8,128)(2,1)} %get-tuple-element.40), channel_id=1, source_target_pairs={{0,3},{1,0},{2,1},{3,2},{4,7},{5,4},{6,5},{7,6},{8,11},{9,8},{10,9... | collective-permute-start | bytes 245768 | tf_op jit(solution)/shard_map/ppermute | solution.py:566
  87.4 1.0 copy-start.2
  88.5 1.0 copy-start.5
  89.5 1.3 copy-start.7
  103.9 59.0 %all-to-all-start.1 = ((bf16[64,16,1024]{2,1,0:T(8,128)(2,1)}), bf16[64,16,1024]{2,1,0:T(8,128)(2,1)}, u32[]{:S(2)}, u32[]{:S(2)}) async-start(bf16[64,16,1024]{2,1,0:T(8,128)(2,1)} %get-tuple-element.43), calls=%async_computation.1 | async-start | bytes 4194304 | tf_op jit(solution)/shard_map/all_to_all | solution.py:636

commit v4 on v3

--- a/solution.py
+++ b/solution.py
@@ -139,25 +139,18 @@
     pltpu.make_async_copy(out_ref, out_hbm, out_sem).wait()
 
 
-def prep_kernel(bounds, rows, query_ref, ids_ref, pos_ref, scale_ref, full_ref, label_ref, mask_ref):
-    blocks, cands = ids_ref.shape
+def prep_kernel(split, rows, query_ref, full_ref, mask_ref):
     lane = lax.broadcasted_iota(jnp.int32, (rows, LANES), 1)
 
     def step(block, carry):
         here = pl.ds(block * rows, rows)
-        total = jnp.zeros((rows, 1), F32)
-        for level, (low, high) in enumerate(bounds):
-            total = total + square_sums(query_ref[here, low:high])
-            scale_ref[level, here, :] = jnp.broadcast_to(lax.rsqrt(total + EPS), (rows, LANES))
-        full_ref[block] = to_row(total)
+        full_ref[block] = to_row(square_sums(query_ref[here, :]))
         first = query_ref[here, :LANES].astype(F32)
-        split = bounds[0][1]
         mask_ref[0, here, :] = jnp.where(lane < split, first, 0.0).astype(BF16)
         mask_ref[1, here, :] = jnp.where(lane < split, 0.0, first).astype(BF16)
-        label_ref[here, :] = jnp.where(ids_ref[pl.ds(block, 1), :] == to_col(pos_ref[pl.ds(block, 1), :]), 1.0, 0.0)
         return carry
 
-    lax.fori_loop(0, blocks, step, 0)
+    lax.fori_loop(0, full_ref.shape[0], step, 0)
 
 
 def dots_kernel(
@@ -188,11 +181,15 @@
     )
 
 
-def prefix_dots(bounds, rows, block, query_ref, mask_ref, cand_ref):
+def prefix_dots(bounds, rows, block, query_ref, cand_ref):
     here = pl.ds(block * rows, rows)
     cands = cand_ref.shape[0] * PBLK
-    first = jnp.concatenate([mask_ref[0, here, :], query_ref[here, :LANES]], axis=0)
-    both = contract(first, cand_ref[:, :, :LANES].reshape(cands, LANES), 1, 1)
+    lane = lax.broadcasted_iota(jnp.int32, (rows, LANES), 1)
+    first = query_ref[here, :LANES]
+    short = jnp.where(lane < bounds[0][1], first.astype(F32), 0.0).astype(BF16)
+    both = contract(
+        jnp.concatenate([short, first], axis=0), cand_ref[:, :, :LANES].reshape(cands, LANES), 1, 1
+    )
     yield both[:rows]
     dots = both[rows:]
     yield dots
@@ -202,11 +199,10 @@
 
 
 def low_kernel(
-    bounds, rows, slot_ref, shard_ref, query_ref, pool_ref, norm_ref, ids_ref, scale_ref, label_ref, mask_ref, after_ref,
-    coef_ref, row_ref, col_ref, loss_ref, cand_ref, term_ref,
+    bounds, rows, slot_ref, shard_ref, query_ref, pool_ref, norm_ref, ids_ref, pos_ref,
+    coef_hbm, row_hbm, col_hbm, loss_ref, cand_ref, term_ref, coef_ref, row_ref, col_ref, sem, row_sem, col_sem,
 ):
-    del after_ref
-    count = cand_ref.shape[0]
+    count = cand_ref.shape[1]
     levels, _, cands = coef_ref.shape
     blocks = loss_ref.shape[0]
 
@@ -215,21 +211,22 @@
         row_ref[...] = jnp.zeros_like(row_ref)
         col_ref[...] = jnp.zeros_like(col_ref)
 
-        def step(block, carry):
+        def one(block, cand_ref, term_ref):
             here = pl.ds(block * rows, rows)
             take_blocks(pool_ref, slot_ref, block, count, cand_ref)
             pp = norm_rows(norm_ref, slot_ref, block, count)
-            live = ids_ref[pl.ds(block, 1), :] >= 0.0
-            labels = label_ref[here, :]
+            ids = ids_ref[pl.ds(block, 1), :]
+            live = ids >= 0.0
+            labels = jnp.where(ids == to_col(pos_ref[pl.ds(block, 1), :]), 1.0, 0.0)
+            qq = jnp.zeros((rows, 1), F32)
             entropy = jnp.zeros((rows, 1), F32)
             logit_sum = jnp.zeros((rows, cands), F32)
             row_terms, col_terms = [], []
-            sums = prefix_dots(bounds, rows, block, query_ref, mask_ref, cand_ref)
+            sums = prefix_dots(bounds, rows, block, query_ref, cand_ref)
             for level, ((low, high), dots) in enumerate(zip(bounds, sums)):
-                scale = scale_ref[level, here, :]
-                scale = jnp.concatenate([scale] * (cands // LANES), axis=1)
+                qq = qq + square_sums(query_ref[here, low:high])
                 coef, row, col, part, logits = terms(
-                    dots, scale, pp[level : level + 1, :], live, labels, float(high // MINP)
+                    dots, lax.rsqrt(qq + EPS), pp[level : level + 1, :], live, labels, float(high // MINP)
                 )
                 term_ref[level] = coef
                 row_terms.append(row)
@@ -248,16 +245,32 @@
                 row_ref[block, level : level + 1, :] = to_row(row)
                 col_ref[block, level : level + 1, :] = col
             loss_ref[pl.ds(block, 1), :] = to_row(loss)
+
+        def step(pair, carry):
+            for j in range(2):
+                one(pair * 2 + j, cand_ref.at[j], term_ref.at[j])
+            here = pl.ds(pair * 2 * rows, 2 * rows)
+            pltpu.make_async_copy(coef_ref.at[:, here], coef_hbm.at[:, here], sem).start()
             return carry
 
-        lax.fori_loop(0, blocks, step, 0)
+        lax.fori_loop(0, blocks // 2, step, 0)
+        copies = [
+            pltpu.make_async_copy(row_ref, row_hbm, row_sem),
+            pltpu.make_async_copy(col_ref, col_hbm, col_sem),
+        ]
+        for copy in copies:
+            copy.start()
+        for copy in copies:
+            copy.wait()
+        pltpu.make_async_copy(coef_ref, coef_hbm, sem).wait()
 
     @pl.when(shard_ref[0] != 0)
     def _():
         loss_ref[...] = jnp.zeros_like(loss_ref)
 
 
-def high_kernel(shards, per_shard, rows, weights, shard_ref, ids_ref, label_ref, *refs):
+def high_kernel(shards, per_shard, rows, weights, shard_ref, ids_ref, pos_ref, after_ref, *refs):
+    del after_ref
     ins, outs, loss_ref = refs[:shards], refs[shards:-1], refs[-1]
     shard = shard_ref[0]
     base = per_shard * rows
@@ -278,7 +291,7 @@
         block = shard * per_shard + k
         ids = ids_ref[pl.ds(block, 1), :]
         live = ids >= 0.0
-        labels = label_ref[pl.ds(block * rows, rows), :]
+        labels = jnp.where(ids == to_col(pos_ref[pl.ds(block, 1), :]), 1.0, 0.0)
         span = slice(k * rows, (k + 1) * rows)
         results = []
         for keep, aux, weight in ((True, aux_half, weights[0]), (False, aux_full, weights[1])):
@@ -322,16 +335,31 @@
 
 
 def passage_kernel(
-    bounds, shards, per_shard, rows, slot_ref, shard_ref, query_ref, pool_ref, mask_ref, low_col_ref, low_coef_ref, *refs
+    bounds, shards, per_shard, rows, slot_ref, shard_ref, query_ref, pool_ref, mask_ref, low_row_hbm, low_col_hbm,
+    low_coef_hbm, *refs
 ):
     ins = refs[:shards]
-    out_hbm, half_hbm, coef_ref, col_ref, spread_ref, sum_ref, scale_ref, out_ref, half_ref, out_sem, half_sem = refs[shards:]
+    out_hbm, half_hbm, row_hbm, coef_ref, row_ref, col_ref, spread_ref, sum_ref, scale_ref, out_ref, half_ref = refs[shards:-7]
+    low_row_ref, low_col_ref, low_coef_ref, out_sem, half_sem, row_sem, low_sem = refs[-7:]
     shard = shard_ref[0]
     base = per_shard * rows
     blocks = shards * per_shard
     slots, _, width = pool_ref.shape
     cands = coef_ref.shape[1]
     count = cands // PBLK
+
+    loads = [
+        pltpu.make_async_copy(low_row_hbm, low_row_ref, low_sem.at[0]),
+        pltpu.make_async_copy(low_col_hbm, low_col_ref, low_sem.at[1]),
+        pltpu.make_async_copy(low_coef_hbm, low_coef_ref, low_sem.at[2]),
+    ]
+    row_copy = pltpu.make_async_copy(row_ref, row_hbm, row_sem)
+
+    @pl.when(shard == 0)
+    def _():
+        for load in loads:
+            load.start()
+        sum_ref[...] = jnp.zeros_like(sum_ref)
 
     scale_ref[...] = jnp.zeros_like(scale_ref)
     for shift in range(shards):
@@ -340,6 +368,8 @@
         aux = unpack_aux(ins[shift], base)
         for k in range(per_shard):
             col_ref[source * per_shard + k] = aux[k : k + 1, :]
+            line = aux[per_shard : per_shard + 1, k * rows : (k + 1) * rows]
+            row_ref[source * per_shard + k] = jnp.broadcast_to(line, (8, rows))
 
     def add_scales(block, low):
         cols = jnp.broadcast_to(col_ref[block], (8, cands))
@@ -356,10 +386,13 @@
 
     @pl.when(shard == 0)
     def _():
-        sum_ref[...] = jnp.zeros_like(sum_ref)
         levels = len(bounds)
-
-        def step(block, carry):
+        for load in loads:
+            load.wait()
+        row_ref[...] = row_ref[...] + low_row_ref[...]
+        row_copy.start()
+
+        def one(block):
             here = pl.ds(block * rows, rows)
             add_scales(block, True)
             base_coef = coef_ref[here, :].astype(F32)
@@ -377,9 +410,13 @@
                 for start, grad in zip(starts, grads):
                     lanes = slice(start, start + grad.shape[1])
                     sum_ref[slot, :, lanes] = sum_ref[slot, :, lanes] + grad[n * PBLK : (n + 1) * PBLK, :]
+
+        def step(pair, carry):
+            for j in range(2):
+                one(pair * 2 + j)
             return carry
 
-        lax.fori_loop(0, blocks, step, 0)
+        lax.fori_loop(0, blocks // 2, step, 0)
         copy = pltpu.make_async_copy(half_ref, half_hbm, half_sem)
         copy.start()
         first = lax.broadcasted_iota(jnp.int32, (1, LANES), 1) < bounds[0][1]
@@ -401,10 +438,14 @@
             lax.fori_loop(0, step_slots, finish, 0, unroll=4)
             pltpu.make_async_copy(out_ref.at[part], out_hbm.at[part], out_sem).start()
         copy.wait()
+        row_copy.wait()
         pltpu.make_async_copy(out_ref, out_hbm, out_sem).wait()
 
     @pl.when(shard != 0)
     def _():
+        row_copy.start()
+        copy = pltpu.make_async_copy(coef_ref, half_hbm.at[0], half_sem)
+        copy.start()
         spread_ref[...] = jnp.zeros_like(spread_ref)
         for block in range(blocks):
             add_scales(block, False)
@@ -421,66 +462,59 @@
             pool = pool_ref[:, :, start:end].reshape(slots * PBLK, end - start).astype(F32)
             out_ref[:, :, start:end] = (grad - scale * pool).astype(BF16).reshape(slots, PBLK, end - start)
             send(start, end)
+        copy.wait()
+        row_copy.wait()
         pltpu.make_async_copy(out_ref, out_hbm, out_sem).wait()
 
 
 def query_kernel(
-    bounds, shards, per_shard, rows, loss_scale, slot_ref, shard_ref, query_ref, pool_ref, low_row_ref, low_loss_ref,
-    high_loss_ref, low_half_hbm, *refs
+    bounds, rows, loss_scale, slot_ref, shard_ref, query_ref, pool_ref, row_ref, low_loss_ref, high_loss_ref, half_hbm,
+    query_grad_ref, loss_ref, cand_ref, half_ref, sem,
 ):
-    ins = refs[:shards]
-    query_grad_ref, loss_ref = refs[shards : shards + 2]
-    cand_ref, coef_ref, row_ref, low_half_ref, sem = refs[shards + 2 :]
     shard = shard_ref[0]
-    base = per_shard * rows
-    blocks = shards * per_shard
+    blocks, cands = low_loss_ref.shape[0], half_ref.shape[2]
     count = cand_ref.shape[0]
     width = query_ref.shape[1]
-    cands = coef_ref.shape[1]
-    copy = pltpu.make_async_copy(low_half_hbm, low_half_ref, sem)
+    per_line = LANES // rows
+    first = pltpu.make_async_copy(half_hbm.at[0], half_ref.at[0], sem.at[0])
+    rest = pl.ds(1, half_ref.shape[0] - 1)
+    others = pltpu.make_async_copy(half_hbm.at[rest], half_ref.at[rest], sem.at[1])
+    first.start()
 
     @pl.when(shard == 0)
     def _():
-        copy.start()
-
-    for shift in range(shards):
-        source = lax.rem(shard - shift + shards, shards)
-        coef_ref[pl.ds(source * base, base), :] = ins[shift][:base, :]
-        aux = unpack_aux(ins[shift], base)
-        for k in range(per_shard):
-            row_ref[source * per_shard + k] = aux[per_shard : per_shard + 1, k * rows : (k + 1) * rows]
+        others.start()
+
     for block in range(blocks):
-        j = block % per_shard
-        loss_ref[block // per_shard : block // per_shard + 1, j * rows : (j + 1) * rows] = low_loss_ref[block : block + 1, :]
+        j = block % per_line
+        loss_ref[block // per_line : block // per_line + 1, j * rows : (j + 1) * rows] = low_loss_ref[block : block + 1, :]
     loss_ref[pl.ds(shard, 1), :] = loss_ref[pl.ds(shard, 1), :] + high_loss_ref[...]
     loss_ref[...] = loss_ref[...] * loss_scale
 
-    def run(spans, low):
+    def run(spans):
         def step(block, carry):
             take_blocks(pool_ref, slot_ref, block, count, cand_ref)
-            rows_here = jnp.broadcast_to(row_ref[block], (8, rows))
-            if low:
-                rows_here = rows_here + low_row_ref[block]
-            row_cols = columns(rows_here)
+            row_cols = columns(row_ref[block])
             here = pl.ds(block * rows, rows)
             for level, (lo, hi) in enumerate(spans):
-                coef = low_half_ref[level, here, :] if low else coef_ref[here, :]
                 query = query_ref[here, lo:hi].astype(F32)
                 cand = cand_ref[:, :, lo:hi].reshape(cands, hi - lo)
-                grad = contract(coef, cand, 1, 0) - row_cols[:rows, level : level + 1] * query
+                grad = contract(half_ref[level, here, :], cand, 1, 0) - row_cols[:rows, level : level + 1] * query
                 query_grad_ref[here, lo:hi] = grad.astype(BF16)
             return carry
 
         lax.fori_loop(0, blocks, step, 0)
 
+    first.wait()
+
     @pl.when(shard == 0)
     def _():
-        copy.wait()
-        run(bounds, True)
+        others.wait()
+        run(bounds)
 
     @pl.when(shard != 0)
     def _():
-        run([(0, width)], False)
+        run([(0, width)])
 
 
 def collect_kernel(target_ref, back_hbm, out_ref, back_ref, sem):
@@ -548,19 +582,17 @@
         name="pack",
     )(wanted, pinned(passages.reshape(local_blocks, PBLK, width)))
     pool = lax.all_to_all(panels, "dp", split_axis=0, concat_axis=0, tiled=True)
-    scales, full_norms, labels, masked = pl.pallas_call(
-        partial(prep_kernel, bounds, rows),
+    full_norms, masked = pl.pallas_call(
+        partial(prep_kernel, bounds[0][1], rows),
         out_shape=[
-            jax.ShapeDtypeStruct((levels, total_rows, LANES), F32),
             jax.ShapeDtypeStruct((blocks, 1, rows), F32),
-            jax.ShapeDtypeStruct((total_rows, cands), F32),
             jax.ShapeDtypeStruct((2, total_rows, LANES), BF16),
         ],
-        in_specs=[vmem()] * 3,
-        out_specs=[vmem()] * 4,
+        in_specs=[vmem()],
+        out_specs=[vmem()] * 2,
         compiler_params=params(),
         name="prep",
-    )(queries, ids, pos)
+    )(queries)
 
     def shift_by(part, s):
         return lax.ppermute(part, "tensor", [(i, (i + s) % shards) for i in range(shards)])
@@ -588,71 +620,83 @@
     )(slot, shard_arr, queries, pool, full_norms, norms)
     arrived = [here, shift_by(right, 1), shift_by(far, 2), shift_by(left, 3)]
 
+    low_coef, low_row, low_col, low_loss = pl.pallas_call(
+        partial(low_kernel, bounds, rows),
+        out_shape=[
+            pltpu.HBM((levels, total_rows, cands), F32),
+            pltpu.HBM((blocks, 8, rows), F32),
+            pltpu.HBM((blocks, 8, cands), F32),
+            jax.ShapeDtypeStruct((blocks, rows), F32),
+        ],
+        in_specs=[smem(), smem()] + [vmem()] * 5,
+        out_specs=[hbm()] * 3 + [vmem()],
+        scratch_shapes=[
+            pltpu.VMEM((2, count, PBLK, width), BF16),
+            pltpu.VMEM((2, levels, rows, cands), F32),
+            pltpu.VMEM((levels, total_rows, cands), F32),
+            pltpu.VMEM((blocks, 8, rows), F32),
+            pltpu.VMEM((blocks, 8, cands), F32),
+            pltpu.SemaphoreType.DMA(()),
+            pltpu.SemaphoreType.DMA(()),
+            pltpu.SemaphoreType.DMA(()),
+        ],
+        compiler_params=params(),
+        name="low",
+    )(slot, shard_arr, queries, pool, norms, ids, pos)
     *coefs, high_loss = pl.pallas_call(
         partial(high_kernel, shards, per_shard, rows, [size / MINP for size in high_sizes]),
         out_shape=[jax.ShapeDtypeStruct((base + COEF_AUX, cands), BF16)] * shards
         + [jax.ShapeDtypeStruct((1, base), F32)],
-        in_specs=[smem()] + [vmem()] * (2 + shards),
+        in_specs=[smem()] + [vmem()] * 2 + [hbm()] + [vmem()] * shards,
         out_specs=[vmem()] * (shards + 1),
         compiler_params=params(),
         name="high",
-    )(shard_arr, ids, labels, *arrived)
-    low_coef, low_row, low_col, low_loss = pl.pallas_call(
-        partial(low_kernel, bounds, rows),
-        out_shape=[
-            jax.ShapeDtypeStruct((levels, total_rows, cands), F32),
-            jax.ShapeDtypeStruct((blocks, 8, rows), F32),
-            jax.ShapeDtypeStruct((blocks, 8, cands), F32),
-            jax.ShapeDtypeStruct((blocks, rows), F32),
-        ],
-        in_specs=[smem(), smem()] + [vmem()] * 7 + [pl.BlockSpec(memory_space=pl.ANY)],
-        out_specs=[vmem()] * 4,
-        scratch_shapes=[cand_scratch, pltpu.VMEM((levels, rows, cands), F32)],
-        compiler_params=params(),
-        name="low",
-    )(slot, shard_arr, queries, pool, norms, ids, scales, labels, masked, high_loss)
+    )(shard_arr, ids, pos, pinned(low_row), *arrived)
     coefs = [coefs[0]] + [shift_by(coefs[s], s) for s in range(1, shards)]
 
     half_shape = (levels, total_rows, cands)
-    slot_grad, low_half = pl.pallas_call(
+    slot_grad, half, row_table = pl.pallas_call(
         partial(passage_kernel, bounds, shards, per_shard, rows),
-        out_shape=[pltpu.HBM(pool_shape, BF16), pltpu.HBM(half_shape, BF16)],
-        in_specs=[smem(), smem()] + [vmem()] * (5 + shards),
-        out_specs=[hbm()] * 2,
+        out_shape=[pltpu.HBM(pool_shape, BF16), pltpu.HBM(half_shape, BF16), pltpu.HBM((blocks, 8, rows), F32)],
+        in_specs=[smem(), smem()] + [vmem()] * 3 + [hbm()] * 3 + [vmem()] * shards,
+        out_specs=[hbm()] * 3,
         scratch_shapes=[
             pltpu.VMEM((total_rows, cands), BF16),
+            pltpu.VMEM((blocks, 8, rows), F32),
             pltpu.VMEM((blocks, 1, cands), F32),
             pltpu.VMEM((slots + 1, PBLK, total_rows), BF16),
             pltpu.VMEM((slots + 1, PBLK, width), F32),
             pltpu.VMEM((slots + 1, PBLK, LANES), F32),
             pltpu.VMEM(pool_shape, BF16),
             pltpu.VMEM(half_shape, BF16),
+            pltpu.VMEM((blocks, 8, rows), F32),
+            pltpu.VMEM((blocks, 8, cands), F32),
+            pltpu.VMEM((levels, total_rows, cands), F32),
             pltpu.SemaphoreType.DMA(()),
             pltpu.SemaphoreType.DMA(()),
+            pltpu.SemaphoreType.DMA(()),
+            pltpu.SemaphoreType.DMA((3,)),
         ],
         compiler_params=params(),
         name="passage",
-    )(spare_slot, shard_arr, queries, pool, masked, low_col, low_coef, *coefs)
+    )(
+        spare_slot, shard_arr, queries, pool, masked,
+        pinned(low_row), pinned(low_col), pinned(low_coef), *coefs,
+    )
     back = lax.all_to_all(slot_grad, "dp", split_axis=0, concat_axis=0, tiled=True)
 
     query_grad, loss = pl.pallas_call(
-        partial(query_kernel, bounds, shards, per_shard, rows, 1.0 / weight_total),
+        partial(query_kernel, bounds, rows, 1.0 / weight_total),
         out_shape=[
             jax.ShapeDtypeStruct((total_rows, width), BF16),
             jax.ShapeDtypeStruct((shards, base), F32),
         ],
-        in_specs=[smem(), smem()] + [vmem()] * 5 + [hbm()] + [vmem()] * shards,
+        in_specs=[smem(), smem()] + [vmem()] * 5 + [hbm()],
         out_specs=[vmem()] * 2,
-        scratch_shapes=[
-            cand_scratch,
-            pltpu.VMEM((total_rows, cands), BF16),
-            pltpu.VMEM((blocks, 1, rows), F32),
-            pltpu.VMEM(half_shape, BF16),
-            pltpu.SemaphoreType.DMA(()),
-        ],
+        scratch_shapes=[cand_scratch, pltpu.VMEM(half_shape, BF16), pltpu.SemaphoreType.DMA((2,))],
         compiler_params=params(),
         name="query",
-    )(slot, shard_arr, queries, pool, low_row, low_loss, high_loss, pinned(low_half), *coefs)
+    )(slot, shard_arr, queries, pool, row_table, low_loss, high_loss, pinned(half))
     loss = lax.psum(loss, "tensor")
 
     passage_grad = pl.pallas_call(

time: 167 us -> 162 us (0.970)
  local copies, waits for them, and re-layouts: 7.76 us -> 1.7 us
  waiting for transfers between devices: 87.2 us -> 90.3 us
    unnamed x19 -> x7, local copies, waits for them, and re-layouts: 6.14 us -> 0.09 us
    all_to_all x1, waiting for transfers between devices: 46.5 us -> 48.8 us  [per_device(): pool = lax.all_to_all(panels, 'dp', split_axis=0, concat_axis=0, tiled=True)]
  transfers between devices with their start and end apart: 8 -> 8, of which waited for: 3 -> 4; matrix products, arithmetic and copies ran while one was open for 1% -> 1% of each run, Pallas kernels for 8% -> 8%
where the time goes in v4:
time: 162 us
  waiting for transfers between devices  90.3 us (56%)
  Pallas kernels  31.5 us (19%)
  starting transfers between devices  28.9 us (18%)
  blocking collectives  7.38 us (5%)
  local copies, waits for them, and re-layouts  1.7 us (1%)
    all_to_all x1, waiting for transfers between devices, per_device(): pool = lax.all_to_all(panels, 'dp', split_axis=0, concat_axis=0, tiled=True)  48.8 us
    all_to_all x1, waiting for transfers between devices, per_device(): lax.all_to_all(slot_grad, 'dp', split_axis=0, concat_axis=0, tiled=True)  37.8 us
    all_to_all x1, starting transfers between devices, per_device(): pool = lax.all_to_all(panels, 'dp', split_axis=0, concat_axis=0, tiled=True)  13.3 us
    pallas_call x1, Pallas kernels, per_device(): pl.pallas_call(partial(passage_kernel, bounds, shards, per_shard, rows),...  8.27 us
    all_to_all x1, starting transfers between devices, per_device(): lax.all_to_all(slot_grad, 'dp', split_axis=0, concat_axis=0, tiled=True)  7.99 us
    ppermute x6, starting transfers between devices, shift_by(): lax.ppermute(part, 'tensor', [(i, (i + s) % shards) for i in range(shards)])  7.65 us
    psum x1, blocking collectives, per_device(): loss = lax.psum(loss, 'tensor')  7.38 us
    pallas_call x1, Pallas kernels, per_device(): pl.pallas_call(partial(query_kernel, bounds, rows, 1.0 / weight_total), o...  5.8 us
  transfers between devices with their start and end apart: 8, of which 4 were waited for; matrix products, arithmetic and copies ran while one was open for 1% of the time, Pallas kernels for 8%

profile of v4, /device:TPU:1, one launch (start us, length us, event | category | flops | bytes accessed | tf_op | source)
XLA Modules:
  0.0 161.7 jit_solution(8828179172718903060)
XLA Ops:
  0.6 0.8 fusion.2
  1.4 0.1 reduce_max.14
  1.5 0.1 reduce_max.18.wanted_ref
  1.7 3.0 %pack.1 = bf16[64,16,1024]{2,1,0:T(8,128)(2,1)} custom-call(s32[64]{0:T(128)S(1)} %reduce_max.18.wanted_ref, bf16[16,16,1024]{2,1,0:T(8,128)(2,1)} %bitcast.5), custom_call_target="tpu_custom_call" | custom-call | tf_op jit(solution)/shard_map/pack/pallas_call | solution.py:570
  4.6 0.0 copy-start
  4.6 0.0 copy-start.2
  4.7 13.3 %all-to-all-start = ((bf16[64,16,1024]{2,1,0:T(8,128)(2,1)}), bf16[64,16,1024]{2,1,0:T(8,128)(2,1)S(1)}, u32[]{:S(2)}, u32[]{:S(2)}) async-start(bf16[64,16,1024]{2,1,0:T(8,128)(2,1)} %pack.1), calls=%async_computation | async-start | bytes 4194304 | tf_op jit(solution)/shard_map/all_to_all | solution.py:584
  18.0 0.8 constant_dynamic-slice_fusion
  18.7 0.1 copy.16
  18.8 0.1 reshape.80.slot_ref
  18.9 0.0 copy-done
  18.9 0.9 prep.1
  19.9 0.1 add.58
  20.0 0.1 add.59
  20.1 0.1 broadcast_in_dim.40
  20.1 0.1 broadcast_in_dim.41
  20.2 0.1 add.61
  20.3 0.0 copy-done.2
  20.3 0.1 convert_element_type.10.pos_ref
  20.4 48.8 %all-to-all-done.pool_ref = bf16[64,16,1024]{2,1,0:T(8,128)(2,1)S(1)} async-done(((bf16[64,16,1024]{2,1,0:T(8,128)(2,1)}), bf16[64,16,1024]{2,1,0:T(8,128)(2,1)S(1)}, u32[]{:S(2)}, u32[]{:S(2)}) %all-to-all-start) | async-done | bytes 2097184 | tf_op jit(solution)/shard_map/all_to_all | solution.py:584
  69.2 2.6 %dots.1 = (f32[64,16,128]{2,1,0:T(8,128)S(1)}, f32[136,256]{1,0:T(8,128)S(1)}, f32[136,256]{1,0:T(8,128)S(1)}, f32[136,256]{1,0:T(8,128)S(1)}) custom-call(s32[128]{0:T(128)S(1)} %reshape.80.slot_ref, s32[1]{0:T(128)} %bitcast.shard_ref, bf16[512,1024]{1,0:T(8,128)(2,1)S(1)} %copy-done, bf16[64,16,1024]{2,1,0:T(8,128)(2,1)S(1)} %all-to-all-done.pool_ref, ...), custom_call_target="tpu_custom_call" | custom-call | tf_op jit(solution)/shard_map/dots/pallas_call | solution.py:603
  71.8 1.3 collective-permute-start
  73.1 2.5 %collective-permute-start.1 = (f32[136,256]{1,0:T(8,128)S(1)}, f32[136,256]{1,0:T(8,128)S(1)}, u32[]{:S(2)}, u32[]{:S(2)}) collective-permute-start(f32[136,256]{1,0:T(8,128)S(1)} %get-tuple-element.30), channel_id=1, source_target_pairs={{0,2},{1,3},{2,0},{3,1},{4,6},{5,7},{6,4},{7,5},{8,10},{9,11},{10,... | collective-permute-start | bytes 417800 | tf_op jit(solution)/shard_map/ppermute | solution.py:598
  75.6 1.2 collective-permute-start.2
  76.7 1.0 dots_own.1.refs_0_
  77.7 5.6 %low.1 = (f32[5,512,256]{2,1,0:T(8,128)}, f32[8,8,64]{2,1,0:T(8,128)}, f32[8,8,256]{2,1,0:T(8,128)}, f32[8,64]{1,0:T(8,128)S(1)}) custom-call(s32[128]{0:T(128)S(1)} %reshape.80.slot_ref, s32[1]{0:T(128)} %bitcast.shard_ref, bf16[512,1024]{1,0:T(8,128)(2,1)S(1)} %copy-done, bf16[64,16,1024]{2,1,0:T(8,128)(2,1)S(1)} %all-to-all-done.pool_ref, ...), custom_call_target="tpu_custom_call" | custom-call | tf_op jit(solution)/shard_map/low/pallas_call | solution.py:623
  83.3 0.0 collective-permute-done.refs_1_
  83.3 0.0 collective-permute-done.1.refs_2_
  83.3 0.0 collective-permute-done.2.refs_3_
  83.3 1.2 high.1
  84.6 0.0 collective-permute-start.3
  84.6 1.8 %collective-permute-start.4 = (bf16[160,256]{1,0:T(8,128)(2,1)}, bf16[160,256]{1,0:T(8,128)(2,1)}, u32[]{:S(2)}, u32[]{:S(2)}) collective-permute-start(bf16[160,256]{1,0:T(8,128)(2,1)} %get-tuple-element.34), channel_id=1, source_target_pairs={{0,2},{1,3},{2,0},{3,1},{4,6},{5,7},{6,4},{7,5},{8,10},{9,11},{10,... | collective-permute-start | bytes 245768 | tf_op jit(solution)/shard_map/ppermute | solution.py:598
  86.4 0.9 collective-permute-start.5
  87.3 0.1 reshape.83.slot_ref
  87.4 2.9 %collective-permute-done.3.refs_1_ = bf16[160,256]{1,0:T(8,128)(2,1)} collective-permute-done((bf16[160,256]{1,0:T(8,128)(2,1)}, bf16[160,256]{1,0:T(8,128)(2,1)}, u32[]{:S(2)}, u32[]{:S(2)}) %collective-permute-start.3) | collective-permute-done | bytes 81952 | tf_op jit(solution)/shard_map/ppermute | solution.py:598
  90.3 0.0 collective-permute-done.4.refs_2_
  90.3 0.9 collective-permute-done.5.refs_3_
  91.1 8.3 %passage.1 = (bf16[64,16,1024]{2,1,0:T(8,128)(2,1)}, bf16[5,512,256]{2,1,0:T(8,128)(2,1)}, f32[8,8,64]{2,1,0:T(8,128)}) custom-call(s32[128]{0:T(128)S(1)} %reshape.83.slot_ref, s32[1]{0:T(128)} %bitcast.shard_ref, bf16[512,1024]{1,0:T(8,128)(2,1)S(1)} %copy-done, bf16[64,16,1024]{2,1,0:T(8,128)(2,1)S(1)} %all-to-all-done.pool_ref, ...), custom_call_target="tpu_custom_call" | custom-call | tf_op jit(solution)/shard_map/passage/pallas_call | solution.py:658
  99.4 0.0 copy-start.1
  99.4 8.0 %all-to-all-start.1 = ((bf16[64,16,1024]{2,1,0:T(8,128)(2,1)}), bf16[64,16,1024]{2,1,0:T(8,128)(2,1)}, u32[]{:S(2)}, u32[]{:S(2)}) async-start(bf16[64,16,1024]{2,1,0:T(8,128)(2,1)} %get-tuple-element.41), calls=%async_computation.1 | async-start | bytes 4194304 | tf_op jit(solution)/shard_map/all_to_all | solution.py:686
  107.4 0.1 add_select_fusion.2
  107.5 0.1 select_n.63.target_ref
  107.6 0.0 copy-done.1
  107.6 5.8 %query.1 = (bf16[512,1024]{1,0:T(8,128)(2,1)}, f32[4,128]{1,0:T(4,128)S(1)}) custom-call(s32[128]{0:T(128)S(1)} %reshape.80.slot_ref, s32[1]{0:T(128)} %bitcast.shard_ref, bf16[512,1024]{1,0:T(8,128)(2,1)S(1)} %copy-done, bf16[64,16,1024]{2,1,0:T(8,128)(2,1)S(1)} %all-to-all-done.pool_ref, f32[8,8,64]{2,1,0:T(8,128)S(1)} %copy-done.1, ...), custom_call_target="tpu_custom_call" | custom-call | tf_op jit(solution)/shard_map/query/pallas_call | solution.py:688
  113.4 7.4 %psum.7 = f32[512]{0:T(512)} all-reduce(f32[512]{0:T(512)S(1)} %bitcast.4), channel_id=1, replica_groups=mesh['dp'=64,'tensor'=4] {'tensor'}, use_global_device_ids=true, to_apply=%region_2.3 | all-reduce | flops 512 | bytes 4096 | tf_op jit(solution)/shard_map/psum | solution.py:700
  120.8 37.8 %all-to-all-done.1 = bf16[64,16,1024]{2,1,0:T(8,128)(2,1)} async-done(((bf16[64,16,1024]{2,1,0:T(8,128)(2,1)}), bf16[64,16,1024]{2,1,0:T(8,128)(2,1)}, u32[]{:S(2)}, u32[]{:S(2)}) %all-to-all-start.1) | async-done | bytes 2097184 | tf_op jit(solution)/shard_map/all_to_all | solution.py:686
  158.6 3.1 %collect.1 = bf16[256,1024]{1,0:T(8,128)(2,1)} custom-call(s32[1,1024]{1,0:T(1,128)S(1)} %select_n.63.target_ref, bf16[1024,1024]{1,0:T(8,128)(2,1)} %bitcast.2.back_hbm), custom_call_target="tpu_custom_call" | custom-call | tf_op jit(solution)/shard_map/collect/pallas_call | solution.py:702
  (7 shorter events, 0.0 us)
Async XLA Ops:
  4.6 14.3 %copy-start = (bf16[512,1024]{1,0:T(8,128)(2,1)S(1)}, bf16[512,1024]{1,0:T(8,128)(2,1)}, u32[]{:S(2)}) copy-start(bf16[512,1024]{1,0:T(8,128)(2,1)} %query_ref.11) | copy-start | bytes 3145732
  4.6 15.7 %copy-start.2 = (s32[512]{0:T(512)S(1)}, s32[512]{0:T(512)}, u32[]{:S(2)}) copy-start(s32[512]{0:T(512)} %param.7) | copy-start | bytes 6148
  4.7 64.6 %all-to-all-start = ((bf16[64,16,1024]{2,1,0:T(8,128)(2,1)}), bf16[64,16,1024]{2,1,0:T(8,128)(2,1)S(1)}, u32[]{:S(2)}, u32[]{:S(2)}) async-start(bf16[64,16,1024]{2,1,0:T(8,128)(2,1)} %pack.1), calls=%async_computation | async-start | bytes 4194304 | tf_op jit(solution)/shard_map/all_to_all | solution.py:584
  71.8 11.5 %collective-permute-start = (f32[136,256]{1,0:T(8,128)S(1)}, f32[136,256]{1,0:T(8,128)S(1)}, u32[]{:S(2)}, u32[]{:S(2)}) collective-permute-start(f32[136,256]{1,0:T(8,128)S(1)} %get-tuple-element.29), channel_id=1, source_target_pairs={{0,1},{1,2},{2,3},{3,0},{4,5},{5,6},{6,7},{7,4},{8,9},{9,10},{10,1... | collective-permute-start | bytes 417800 | tf_op jit(solution)/shard_map/ppermute | solution.py:598
  73.1 10.2 %collective-permute-start.1 = (f32[136,256]{1,0:T(8,128)S(1)}, f32[136,256]{1,0:T(8,128)S(1)}, u32[]{:S(2)}, u32[]{:S(2)}) collective-permute-start(f32[136,256]{1,0:T(8,128)S(1)} %get-tuple-element.30), channel_id=1, source_target_pairs={{0,2},{1,3},{2,0},{3,1},{4,6},{5,7},{6,4},{7,5},{8,10},{9,11},{10,... | collective-permute-start | bytes 417800 | tf_op jit(solution)/shard_map/ppermute | solution.py:598
  75.6 7.8 %collective-permute-start.2 = (f32[136,256]{1,0:T(8,128)S(1)}, f32[136,256]{1,0:T(8,128)S(1)}, u32[]{:S(2)}, u32[]{:S(2)}) collective-permute-start(f32[136,256]{1,0:T(8,128)S(1)} %get-tuple-element.31), channel_id=1, source_target_pairs={{0,3},{1,0},{2,1},{3,2},{4,7},{5,4},{6,5},{7,6},{8,11},{9,8},{10,9... | collective-permute-start | bytes 417800 | tf_op jit(solution)/shard_map/ppermute | solution.py:598
  84.6 5.7 %collective-permute-start.3 = (bf16[160,256]{1,0:T(8,128)(2,1)}, bf16[160,256]{1,0:T(8,128)(2,1)}, u32[]{:S(2)}, u32[]{:S(2)}) collective-permute-start(bf16[160,256]{1,0:T(8,128)(2,1)} %get-tuple-element.33), channel_id=1, source_target_pairs={{0,1},{1,2},{2,3},{3,0},{4,5},{5,6},{6,7},{7,4},{8,9},{9,10},{10,1... | collective-permute-start | bytes 245768 | tf_op jit(solution)/shard_map/ppermute | solution.py:598
  84.6 5.7 %collective-permute-start.4 = (bf16[160,256]{1,0:T(8,128)(2,1)}, bf16[160,256]{1,0:T(8,128)(2,1)}, u32[]{:S(2)}, u32[]{:S(2)}) collective-permute-start(bf16[160,256]{1,0:T(8,128)(2,1)} %get-tuple-element.34), channel_id=1, source_target_pairs={{0,2},{1,3},{2,0},{3,1},{4,6},{5,7},{6,4},{7,5},{8,10},{9,11},{10,... | collective-permute-start | bytes 245768 | tf_op jit(solution)/shard_map/ppermute | solution.py:598
  86.4 4.7 %collective-permute-start.5 = (bf16[160,256]{1,0:T(8,128)(2,1)}, bf16[160,256]{1,0:T(8,128)(2,1)}, u32[]{:S(2)}, u32[]{:S(2)}) collective-permute-start(bf16[160,256]{1,0:T(8,128)(2,1)} %get-tuple-element.35), channel_id=1, source_target_pairs={{0,3},{1,0},{2,1},{3,2},{4,7},{5,4},{6,5},{7,6},{8,11},{9,8},{10,9... | collective-permute-start | bytes 245768 | tf_op jit(solution)/shard_map/ppermute | solution.py:598
  99.4 8.2 %copy-start.1 = (f32[8,8,64]{2,1,0:T(8,128)S(1)}, f32[8,8,64]{2,1,0:T(8,128)}, u32[]{:S(2)}) copy-start(f32[8,8,64]{2,1,0:T(8,128)} %get-tuple-element.36.row_ref) | copy-start | bytes 49156
  99.4 59.2 %all-to-all-start.1 = ((bf16[64,16,1024]{2,1,0:T(8,128)(2,1)}), bf16[64,16,1024]{2,1,0:T(8,128)(2,1)}, u32[]{:S(2)}, u32[]{:S(2)}) async-start(bf16[64,16,1024]{2,1,0:T(8,128)(2,1)} %get-tuple-element.41), calls=%async_computation.1 | async-start | bytes 4194304 | tf_op jit(solution)/shard_map/all_to_all | solution.py:686

commit v5 on v4

--- a/solution.py
+++ b/solution.py
@@ -121,20 +121,38 @@
     return table.T[:8, :]
 
 
-def pack_kernel(wanted_ref, block_hbm, out_hbm, block_ref, out_ref, in_sem, out_sem):
+def pack_kernel(
+    first_ref, lists_hbm, block_hbm, out_hbm, lists_ref, block_ref, out_ref, row_ref, wanted_ref, lists_sem, in_sem, row_sem, out_sem
+):
     load = pltpu.make_async_copy(block_hbm, block_ref, in_sem)
+    lists = pltpu.make_async_copy(lists_hbm, lists_ref, lists_sem)
+    lists.start()
     load.start()
+    lists.wait()
+    local = lists_ref[...] - first_ref[0]
+    local = jnp.where((local >= 0) & (local < block_ref.shape[0]), local, 0).astype(F32)
+    row = jnp.broadcast_to(jnp.max(local, axis=0, keepdims=True), row_ref.shape)
+    size = row.shape[1]
+    step = 1
+    while step < size // out_ref.shape[0]:
+        row = jnp.maximum(row, pltpu.roll(row, size - step, 1))
+        step *= 2
+    row_ref[...] = row.astype(jnp.int32)
+    save = pltpu.make_async_copy(row_ref, wanted_ref, row_sem)
+    save.start()
+    save.wait()
     load.wait()
-    size = out_ref.shape[0] // CHUNKS
+    share = size // out_ref.shape[0]
+    part_size = out_ref.shape[0] // CHUNKS
     for chunk in range(CHUNKS):
 
-        def step(i, carry):
-            d = chunk * size + i
-            out_ref[d] = block_ref[jnp.maximum(wanted_ref[d], 0)]
+        def one(i, carry):
+            d = chunk * part_size + i
+            out_ref[d] = block_ref[wanted_ref[0, d * share]]
             return carry
 
-        lax.fori_loop(0, size, step, 0, unroll=8)
-        part = pl.ds(chunk * size, size)
+        lax.fori_loop(0, part_size, one, 0, unroll=8)
+        part = pl.ds(chunk * part_size, part_size)
         pltpu.make_async_copy(out_ref.at[part], out_hbm.at[part], out_sem).start()
     pltpu.make_async_copy(out_ref, out_hbm, out_sem).wait()
 
@@ -339,8 +357,8 @@
     low_coef_hbm, *refs
 ):
     ins = refs[:shards]
-    out_hbm, half_hbm, row_hbm, coef_ref, row_ref, col_ref, spread_ref, sum_ref, scale_ref, out_ref, half_ref = refs[shards:-7]
-    low_row_ref, low_col_ref, low_coef_ref, out_sem, half_sem, row_sem, low_sem = refs[-7:]
+    out_hbm, half_hbm, row_hbm, coef_ref, row_ref, col_ref, spread_ref, sum_ref, scale_ref, out_ref, half_ref = refs[shards:-8]
+    low_row_ref, low_col_ref, low_coef_ref, out_sem, half_sem, row_sem, low_sem, pair_sem = refs[-8:]
     shard = shard_ref[0]
     base = per_shard * rows
     blocks = shards * per_shard
@@ -351,14 +369,24 @@
     loads = [
         pltpu.make_async_copy(low_row_hbm, low_row_ref, low_sem.at[0]),
         pltpu.make_async_copy(low_col_hbm, low_col_ref, low_sem.at[1]),
-        pltpu.make_async_copy(low_coef_hbm, low_coef_ref, low_sem.at[2]),
     ]
+    pairs = blocks // 2
+
+    def pair_rows(pair):
+        return pl.ds(pair * 2 * rows, 2 * rows)
+
+    def pair_load(pair):
+        here = pair_rows(pair)
+        return pltpu.make_async_copy(low_coef_hbm.at[:, here], low_coef_ref.at[:, here], pair_sem.at[pair])
+
     row_copy = pltpu.make_async_copy(row_ref, row_hbm, row_sem)
 
     @pl.when(shard == 0)
     def _():
         for load in loads:
             load.start()
+        for pair in range(pairs):
+            pair_load(pair).start()
         sum_ref[...] = jnp.zeros_like(sum_ref)
 
     scale_ref[...] = jnp.zeros_like(scale_ref)
@@ -412,30 +440,33 @@
                     sum_ref[slot, :, lanes] = sum_ref[slot, :, lanes] + grad[n * PBLK : (n + 1) * PBLK, :]
 
         def step(pair, carry):
+            pair_load(pair).wait()
             for j in range(2):
                 one(pair * 2 + j)
+            here = pair_rows(pair)
+            pltpu.make_async_copy(half_ref.at[:, here], half_hbm.at[:, here], half_sem).start()
             return carry
 
-        lax.fori_loop(0, blocks // 2, step, 0)
+        lax.fori_loop(0, pairs, step, 0)
         copy = pltpu.make_async_copy(half_ref, half_hbm, half_sem)
-        copy.start()
-        first = lax.broadcasted_iota(jnp.int32, (1, LANES), 1) < bounds[0][1]
+        level_of = lax.broadcasted_iota(jnp.int32, (LANES, width), 0)
+        column = lax.broadcasted_iota(jnp.int32, (LANES, width), 1)
+        member = jnp.zeros((LANES, width), F32)
+        for level, (lo, hi) in enumerate(bounds):
+            member = jnp.where((level_of == level) & (column >= lo) & (column < hi), 1.0, member)
+        member = member.astype(BF16)
         step_slots = slots // CHUNKS
         for chunk in range(CHUNKS):
-            part = pl.ds(chunk * step_slots, step_slots)
-
-            def finish(i, carry):
-                slot = chunk * step_slots + i
-                scale = scale_ref[slot]
-                wide = [jnp.where(first, scale[:, 0:1], scale[:, 1:2])]
-                for level in range(2, levels):
-                    lo, hi = bounds[level]
-                    wide.append(jnp.broadcast_to(scale[:, level : level + 1], (PBLK, hi - lo)))
-                pool = pool_ref[slot].astype(F32)
-                out_ref[slot] = (sum_ref[slot] - jnp.concatenate(wide, axis=1) * pool).astype(BF16)
-                return carry
-
-            lax.fori_loop(0, step_slots, finish, 0, unroll=4)
+            part = slice(chunk * step_slots, (chunk + 1) * step_slots)
+            scale = scale_ref[part].reshape(step_slots * PBLK, LANES)
+            high = scale.astype(BF16)
+            rest = scale - high.astype(F32)
+            middle = rest.astype(BF16)
+            low = (rest - middle.astype(F32)).astype(BF16)
+            wide = contract(high, member, 1, 0) + contract(middle, member, 1, 0) + contract(low, member, 1, 0)
+            pool = pool_ref[part].reshape(step_slots * PBLK, width).astype(F32)
+            total = sum_ref[part].reshape(step_slots * PBLK, width)
+            out_ref[part] = (total - wide * pool).astype(BF16).reshape(step_slots, PBLK, width)
             pltpu.make_async_copy(out_ref.at[part], out_hbm.at[part], out_sem).start()
         copy.wait()
         row_copy.wait()
@@ -519,13 +550,21 @@
 
 def collect_kernel(target_ref, back_hbm, out_ref, back_ref, sem):
     rows = out_ref.shape[0]
-    count = back_ref.shape[0]
-    copy = pltpu.make_async_copy(back_hbm, back_ref, sem)
-    copy.start()
-    here = lax.broadcasted_iota(jnp.int32, (rows, count), 0)
-    choose = jnp.where(here == target_ref[...], 1.0, 0.0).astype(BF16)
-    copy.wait()
-    out_ref[...] = contract(choose, back_ref[...], 1, 0).astype(BF16)
+    size = back_ref.shape[0] // 2
+    copies = []
+    for half in range(2):
+        part = pl.ds(half * size, size)
+        copies.append(pltpu.make_async_copy(back_hbm.at[part], back_ref.at[part], sem.at[half]))
+        copies[-1].start()
+    here = lax.broadcasted_iota(jnp.int32, (rows, size), 0)
+    total = None
+    for half in range(2):
+        part = slice(half * size, (half + 1) * size)
+        choose = jnp.where(here == target_ref[:, part], 1.0, 0.0).astype(BF16)
+        copies[half].wait()
+        grad = contract(choose, back_ref[part, :], 1, 0)
+        total = grad if total is None else total + grad
+    out_ref[...] = total.astype(BF16)
 
 
 def per_device(queries, passages, neg_lists, positives):
@@ -570,17 +609,25 @@
     panels = pl.pallas_call(
         pack_kernel,
         out_shape=pltpu.HBM(pool_shape, BF16),
-        in_specs=[smem(), hbm()],
+        in_specs=[smem(), hbm(), hbm()],
         out_specs=hbm(),
         scratch_shapes=[
+            pltpu.VMEM((count, neg_lists.shape[0]), jnp.int32),
             pltpu.VMEM((local_blocks, PBLK, width), BF16),
             pltpu.VMEM(pool_shape, BF16),
+            pltpu.VMEM((8, neg_lists.shape[0]), jnp.int32),
+            pltpu.SMEM((8, neg_lists.shape[0]), jnp.int32),
+            pltpu.SemaphoreType.DMA(()),
+            pltpu.SemaphoreType.DMA(()),
             pltpu.SemaphoreType.DMA(()),
             pltpu.SemaphoreType.DMA(()),
         ],
         compiler_params=params(),
         name="pack",
-    )(wanted, pinned(passages.reshape(local_blocks, PBLK, width)))
+    )(
+        (my_index * local_blocks).reshape(1).astype(jnp.int32), pinned(neg_lists.T),
+        pinned(passages.reshape(local_blocks, PBLK, width)),
+    )
     pool = lax.all_to_all(panels, "dp", split_axis=0, concat_axis=0, tiled=True)
     full_norms, masked = pl.pallas_call(
         partial(prep_kernel, bounds[0][1], rows),
@@ -600,24 +647,15 @@
     cand_scratch = pltpu.VMEM((count, PBLK, width), BF16)
     message = jax.ShapeDtypeStruct((base + AUX, cands), F32)
     norm_shape = (slots, PBLK, LANES)
-    norms, far, right, left = pl.pallas_call(
-        partial(first_dots_kernel, bounds, shards, per_shard, rows, (2, 1, 3)),
-        out_shape=[jax.ShapeDtypeStruct(norm_shape, F32)] + [message] * 3,
+    norms, far, right, left, here = pl.pallas_call(
+        partial(first_dots_kernel, bounds, shards, per_shard, rows, (2, 1, 3, 0)),
+        out_shape=[jax.ShapeDtypeStruct(norm_shape, F32)] + [message] * shards,
         in_specs=[smem(), smem(), vmem(), vmem(), vmem()],
-        out_specs=[vmem()] * 4,
+        out_specs=[vmem()] * (shards + 1),
         scratch_shapes=[cand_scratch],
         compiler_params=params(),
         name="dots",
     )(slot, shard_arr, queries, pool, full_norms)
-    (here,) = pl.pallas_call(
-        partial(dots_kernel, shards, per_shard, rows, levels - 1, (0,)),
-        out_shape=[message],
-        in_specs=[smem(), smem()] + [vmem()] * 4,
-        out_specs=[vmem()],
-        scratch_shapes=[cand_scratch],
-        compiler_params=params(),
-        name="dots_own",
-    )(slot, shard_arr, queries, pool, full_norms, norms)
     arrived = [here, shift_by(right, 1), shift_by(far, 2), shift_by(left, 3)]
 
     low_coef, low_row, low_col, low_loss = pl.pallas_call(
@@ -675,7 +713,8 @@
             pltpu.SemaphoreType.DMA(()),
             pltpu.SemaphoreType.DMA(()),
             pltpu.SemaphoreType.DMA(()),
-            pltpu.SemaphoreType.DMA((3,)),
+            pltpu.SemaphoreType.DMA((2,)),
+            pltpu.SemaphoreType.DMA((blocks // 2,)),
         ],
         compiler_params=params(),
         name="passage",
@@ -704,7 +743,7 @@
         out_shape=jax.ShapeDtypeStruct((local_blocks * PBLK, width), BF16),
         in_specs=[vmem(), hbm()],
         out_specs=vmem(),
-        scratch_shapes=[pltpu.VMEM((slots * PBLK, width), BF16), pltpu.SemaphoreType.DMA(())],
+        scratch_shapes=[pltpu.VMEM((slots * PBLK, width), BF16), pltpu.SemaphoreType.DMA((2,))],
         compiler_params=params(),
         name="collect",
     )(target, pinned(back.reshape(slots * PBLK, width)))

time: 162 us -> 160 us (0.988)
  transfers between devices with their start and end apart: 8 -> 8, of which waited for: 4 -> 5; matrix products, arithmetic and copies ran while one was open for 1% -> 1% of each run, Pallas kernels for 8% -> 8%
where the time goes in v5:
time: 160 us
  waiting for transfers between devices  89.8 us (56%)
  Pallas kernels  30.4 us (19%)
  starting transfers between devices  30.1 us (19%)
  blocking collectives  7.38 us (5%)
    all_to_all x1, waiting for transfers between devices, per_device(): pool = lax.all_to_all(panels, 'dp', split_axis=0, concat_axis=0, tiled=True)  49.5 us
    all_to_all x1, waiting for transfers between devices, per_device(): lax.all_to_all(slot_grad, 'dp', split_axis=0, concat_axis=0, tiled=True)  37.5 us
    all_to_all x1, starting transfers between devices, per_device(): pool = lax.all_to_all(panels, 'dp', split_axis=0, concat_axis=0, tiled=True)  13.3 us
    ppermute x6, starting transfers between devices, shift_by(): lax.ppermute(part, 'tensor', [(i, (i + s) % shards) for i in range(shards)])  8.67 us
    all_to_all x1, starting transfers between devices, per_device(): lax.all_to_all(slot_grad, 'dp', split_axis=0, concat_axis=0, tiled=True)  8.12 us
    pallas_call x1, Pallas kernels, per_device(): pl.pallas_call(partial(passage_kernel, bounds, shards, per_shard, rows),...  7.64 us
    psum x1, blocking collectives, per_device(): loss = lax.psum(loss, 'tensor')  7.38 us
    pallas_call x1, Pallas kernels, per_device(): pl.pallas_call(partial(query_kernel, bounds, rows, 1.0 / weight_total), o...  5.81 us
  transfers between devices with their start and end apart: 8, of which 5 were waited for; matrix products, arithmetic and copies ran while one was open for 1% of the time, Pallas kernels for 8%

profile of v5, /device:TPU:1, one launch (start us, length us, event | category | flops | bytes accessed | tf_op | source)
XLA Modules:
  0.0 160.0 jit_solution(7789239704920753897)
XLA Ops:
  0.6 3.2 %pack.1 = bf16[64,16,1024]{2,1,0:T(8,128)(2,1)} custom-call(s32[1]{0:T(128)} %bitcast.1.first_ref, s32[16,512]{1,0:T(8,128)} %bitcast.8, bf16[16,16,1024]{2,1,0:T(8,128)(2,1)} %bitcast.7), custom_call_target="tpu_custom_call" | custom-call | tf_op jit(solution)/shard_map/pack/pallas_call | solution.py:609
  3.8 0.0 copy-start.2
  3.9 0.0 copy-start
  3.9 0.0 copy-start.3
  3.9 13.3 %all-to-all-start = ((bf16[64,16,1024]{2,1,0:T(8,128)(2,1)}), bf16[64,16,1024]{2,1,0:T(8,128)(2,1)S(1)}, u32[]{:S(2)}, u32[]{:S(2)}) async-start(bf16[64,16,1024]{2,1,0:T(8,128)(2,1)} %pack.1), calls=%async_computation | async-start | bytes 4194304 | tf_op jit(solution)/shard_map/all_to_all | solution.py:631
  17.2 0.0 copy-done.2
  17.2 0.1 constant_dynamic-slice_fusion
  17.3 0.1 copy.16
  17.4 0.1 add.57
  17.5 0.1 add.58
  17.6 0.1 broadcast_in_dim.40
  17.6 0.1 broadcast_in_dim.41
  17.7 0.1 add.60
  17.8 0.1 reshape.83.slot_ref
  17.9 0.0 copy-done
  17.9 1.0 prep.1
  18.9 0.0 copy-done.3
  18.9 0.1 convert_element_type.10.pos_ref
  19.0 49.5 %all-to-all-done.pool_ref = bf16[64,16,1024]{2,1,0:T(8,128)(2,1)S(1)} async-done(((bf16[64,16,1024]{2,1,0:T(8,128)(2,1)}), bf16[64,16,1024]{2,1,0:T(8,128)(2,1)S(1)}, u32[]{:S(2)}, u32[]{:S(2)}) %all-to-all-start) | async-done | bytes 2097184 | tf_op jit(solution)/shard_map/all_to_all | solution.py:631
  68.4 2.9 %dots.1 = (f32[64,16,128]{2,1,0:T(8,128)S(1)}, f32[136,256]{1,0:T(8,128)S(1)}, f32[136,256]{1,0:T(8,128)S(1)}, f32[136,256]{1,0:T(8,128)S(1)}, f32[136,256]{1,0:T(8,128)S(1)}) custom-call(s32[128]{0:T(128)S(1)} %reshape.83.slot_ref, s32[1]{0:T(128)} %bitcast.shard_ref, bf16[512,1024]{1,0:T(8,128)(2,1)S(1)} %copy-done, ...), custom_call_target="tpu_custom_call" | custom-call | tf_op jit(solution)/shard_map/dots/pallas_call | solution.py:650
  71.4 1.3 collective-permute-start
  72.6 2.5 %collective-permute-start.1 = (f32[136,256]{1,0:T(8,128)S(1)}, f32[136,256]{1,0:T(8,128)S(1)}, u32[]{:S(2)}, u32[]{:S(2)}) collective-permute-start(f32[136,256]{1,0:T(8,128)S(1)} %get-tuple-element.32), channel_id=1, source_target_pairs={{0,2},{1,3},{2,0},{3,1},{4,6},{5,7},{6,4},{7,5},{8,10},{9,11},{10,... | collective-permute-start | bytes 417800 | tf_op jit(solution)/shard_map/ppermute | solution.py:645
  75.1 1.2 collective-permute-start.2
  76.3 5.6 %low.1 = (f32[5,512,256]{2,1,0:T(8,128)}, f32[8,8,64]{2,1,0:T(8,128)}, f32[8,8,256]{2,1,0:T(8,128)}, f32[8,64]{1,0:T(8,128)S(1)}) custom-call(s32[128]{0:T(128)S(1)} %reshape.83.slot_ref, s32[1]{0:T(128)} %bitcast.shard_ref, bf16[512,1024]{1,0:T(8,128)(2,1)S(1)} %copy-done, bf16[64,16,1024]{2,1,0:T(8,128)(2,1)S(1)} %all-to-all-done.pool_ref, ...), custom_call_target="tpu_custom_call" | custom-call | tf_op jit(solution)/shard_map/low/pallas_call | solution.py:661
  81.8 0.0 collective-permute-done.refs_1_
  81.8 0.0 collective-permute-done.1.refs_2_
  81.9 0.0 collective-permute-done.2.refs_3_
  81.9 1.2 high.1
  83.1 0.7 collective-permute-start.3
  83.7 2.2 %collective-permute-start.4 = (bf16[160,256]{1,0:T(8,128)(2,1)}, bf16[160,256]{1,0:T(8,128)(2,1)}, u32[]{:S(2)}, u32[]{:S(2)}) collective-permute-start(bf16[160,256]{1,0:T(8,128)(2,1)} %get-tuple-element.36), channel_id=1, source_target_pairs={{0,2},{1,3},{2,0},{3,1},{4,6},{5,7},{6,4},{7,5},{8,10},{9,11},{10,... | collective-permute-start | bytes 245768 | tf_op jit(solution)/shard_map/ppermute | solution.py:645
  85.9 1.0 collective-permute-start.5
  86.9 0.1 reshape.87.slot_ref
  86.9 1.0 collective-permute-done.3.refs_1_
  87.9 1.1 collective-permute-done.4.refs_2_
  89.0 0.8 collective-permute-done.5.refs_3_
  89.8 7.6 %passage.1 = (bf16[64,16,1024]{2,1,0:T(8,128)(2,1)}, bf16[5,512,256]{2,1,0:T(8,128)(2,1)}, f32[8,8,64]{2,1,0:T(8,128)}) custom-call(s32[128]{0:T(128)S(1)} %reshape.87.slot_ref, s32[1]{0:T(128)} %bitcast.shard_ref, bf16[512,1024]{1,0:T(8,128)(2,1)S(1)} %copy-done, bf16[64,16,1024]{2,1,0:T(8,128)(2,1)S(1)} %all-to-all-done.pool_ref, ...), custom_call_target="tpu_custom_call" | custom-call | tf_op jit(solution)/shard_map/passage/pallas_call | solution.py:696
  97.5 0.0 copy-start.1
  97.5 8.1 %all-to-all-start.1 = ((bf16[64,16,1024]{2,1,0:T(8,128)(2,1)}), bf16[64,16,1024]{2,1,0:T(8,128)(2,1)}, u32[]{:S(2)}, u32[]{:S(2)}) async-start(bf16[64,16,1024]{2,1,0:T(8,128)(2,1)} %get-tuple-element.43), calls=%async_computation.1 | async-start | bytes 4194304 | tf_op jit(solution)/shard_map/all_to_all | solution.py:725
  105.6 0.1 fusion.2
  105.7 0.1 reduce_max.14
  105.7 0.1 reduce_max.18
  105.9 0.1 add_select_fusion.2
  106.0 0.1 select_n.63.target_ref
  106.1 0.0 copy-done.1
  106.1 5.8 %query.1 = (bf16[512,1024]{1,0:T(8,128)(2,1)}, f32[4,128]{1,0:T(4,128)S(1)}) custom-call(s32[128]{0:T(128)S(1)} %reshape.83.slot_ref, s32[1]{0:T(128)} %bitcast.shard_ref, bf16[512,1024]{1,0:T(8,128)(2,1)S(1)} %copy-done, bf16[64,16,1024]{2,1,0:T(8,128)(2,1)S(1)} %all-to-all-done.pool_ref, f32[8,8,64]{2,1,0:T(8,128)S(1)} %copy-done.1, ...), custom_call_target="tpu_custom_call" | custom-call | tf_op jit(solution)/shard_map/query/pallas_call | solution.py:727
  111.9 7.4 %psum.7 = f32[512]{0:T(512)} all-reduce(f32[512]{0:T(512)S(1)} %bitcast.6), channel_id=1, replica_groups=mesh['dp'=64,'tensor'=4] {'tensor'}, use_global_device_ids=true, to_apply=%region_2.3 | all-reduce | flops 512 | bytes 4096 | tf_op jit(solution)/shard_map/psum | solution.py:739
  119.3 37.5 %all-to-all-done.1 = bf16[64,16,1024]{2,1,0:T(8,128)(2,1)} async-done(((bf16[64,16,1024]{2,1,0:T(8,128)(2,1)}), bf16[64,16,1024]{2,1,0:T(8,128)(2,1)}, u32[]{:S(2)}, u32[]{:S(2)}) %all-to-all-start.1) | async-done | bytes 2097184 | tf_op jit(solution)/shard_map/all_to_all | solution.py:725
  156.8 3.1 %collect.1 = bf16[256,1024]{1,0:T(8,128)(2,1)} custom-call(s32[1,1024]{1,0:T(1,128)S(1)} %select_n.63.target_ref, bf16[1024,1024]{1,0:T(8,128)(2,1)} %bitcast.4.back_hbm), custom_call_target="tpu_custom_call" | custom-call | tf_op jit(solution)/shard_map/collect/pallas_call | solution.py:741
  (7 shorter events, 0.0 us)
Async XLA Ops:
  3.8 13.3 %copy-start.2 = (s32[512,16]{0,1:T(8,128)S(1)}, s32[512,16]{0,1:T(8,128)}, u32[]{:S(2)}) copy-start(s32[512,16]{0,1:T(8,128)} %param.6) | copy-start | bytes 98308
  3.9 14.1 %copy-start = (bf16[512,1024]{1,0:T(8,128)(2,1)S(1)}, bf16[512,1024]{1,0:T(8,128)(2,1)}, u32[]{:S(2)}) copy-start(bf16[512,1024]{1,0:T(8,128)(2,1)} %query_ref.9) | copy-start | bytes 3145732
  3.9 15.0 %copy-start.3 = (s32[512]{0:T(512)S(1)}, s32[512]{0:T(512)}, u32[]{:S(2)}) copy-start(s32[512]{0:T(512)} %param.7) | copy-start | bytes 6148
  3.9 64.6 %all-to-all-start = ((bf16[64,16,1024]{2,1,0:T(8,128)(2,1)}), bf16[64,16,1024]{2,1,0:T(8,128)(2,1)S(1)}, u32[]{:S(2)}, u32[]{:S(2)}) async-start(bf16[64,16,1024]{2,1,0:T(8,128)(2,1)} %pack.1), calls=%async_computation | async-start | bytes 4194304 | tf_op jit(solution)/shard_map/all_to_all | solution.py:631
  71.4 10.5 %collective-permute-start = (f32[136,256]{1,0:T(8,128)S(1)}, f32[136,256]{1,0:T(8,128)S(1)}, u32[]{:S(2)}, u32[]{:S(2)}) collective-permute-start(f32[136,256]{1,0:T(8,128)S(1)} %get-tuple-element.31), channel_id=1, source_target_pairs={{0,1},{1,2},{2,3},{3,0},{4,5},{5,6},{6,7},{7,4},{8,9},{9,10},{10,1... | collective-permute-start | bytes 417800 | tf_op jit(solution)/shard_map/ppermute | solution.py:645
  72.6 9.2 %collective-permute-start.1 = (f32[136,256]{1,0:T(8,128)S(1)}, f32[136,256]{1,0:T(8,128)S(1)}, u32[]{:S(2)}, u32[]{:S(2)}) collective-permute-start(f32[136,256]{1,0:T(8,128)S(1)} %get-tuple-element.32), channel_id=1, source_target_pairs={{0,2},{1,3},{2,0},{3,1},{4,6},{5,7},{6,4},{7,5},{8,10},{9,11},{10,... | collective-permute-start | bytes 417800 | tf_op jit(solution)/shard_map/ppermute | solution.py:645
  75.1 6.8 %collective-permute-start.2 = (f32[136,256]{1,0:T(8,128)S(1)}, f32[136,256]{1,0:T(8,128)S(1)}, u32[]{:S(2)}, u32[]{:S(2)}) collective-permute-start(f32[136,256]{1,0:T(8,128)S(1)} %get-tuple-element.33), channel_id=1, source_target_pairs={{0,3},{1,0},{2,1},{3,2},{4,7},{5,4},{6,5},{7,6},{8,11},{9,8},{10,9... | collective-permute-start | bytes 417800 | tf_op jit(solution)/shard_map/ppermute | solution.py:645
  83.1 4.8 %collective-permute-start.3 = (bf16[160,256]{1,0:T(8,128)(2,1)}, bf16[160,256]{1,0:T(8,128)(2,1)}, u32[]{:S(2)}, u32[]{:S(2)}) collective-permute-start(bf16[160,256]{1,0:T(8,128)(2,1)} %get-tuple-element.35), channel_id=1, source_target_pairs={{0,1},{1,2},{2,3},{3,0},{4,5},{5,6},{6,7},{7,4},{8,9},{9,10},{10,1... | collective-permute-start | bytes 245768 | tf_op jit(solution)/shard_map/ppermute | solution.py:645
  83.7 5.2 %collective-permute-start.4 = (bf16[160,256]{1,0:T(8,128)(2,1)}, bf16[160,256]{1,0:T(8,128)(2,1)}, u32[]{:S(2)}, u32[]{:S(2)}) collective-permute-start(bf16[160,256]{1,0:T(8,128)(2,1)} %get-tuple-element.36), channel_id=1, source_target_pairs={{0,2},{1,3},{2,0},{3,1},{4,6},{5,7},{6,4},{7,5},{8,10},{9,11},{10,... | collective-permute-start | bytes 245768 | tf_op jit(solution)/shard_map/ppermute | solution.py:645
  85.9 3.9 %collective-permute-start.5 = (bf16[160,256]{1,0:T(8,128)(2,1)}, bf16[160,256]{1,0:T(8,128)(2,1)}, u32[]{:S(2)}, u32[]{:S(2)}) collective-permute-start(bf16[160,256]{1,0:T(8,128)(2,1)} %get-tuple-element.37), channel_id=1, source_target_pairs={{0,3},{1,0},{2,1},{3,2},{4,7},{5,4},{6,5},{7,6},{8,11},{9,8},{10,9... | collective-permute-start | bytes 245768 | tf_op jit(solution)/shard_map/ppermute | solution.py:645
  97.5 8.6 %copy-start.1 = (f32[8,8,64]{2,1,0:T(8,128)S(1)}, f32[8,8,64]{2,1,0:T(8,128)}, u32[]{:S(2)}) copy-start(f32[8,8,64]{2,1,0:T(8,128)} %get-tuple-element.38.row_ref) | copy-start | bytes 49156
  97.5 59.3 %all-to-all-start.1 = ((bf16[64,16,1024]{2,1,0:T(8,128)(2,1)}), bf16[64,16,1024]{2,1,0:T(8,128)(2,1)}, u32[]{:S(2)}, u32[]{:S(2)}) async-start(bf16[64,16,1024]{2,1,0:T(8,128)(2,1)} %get-tuple-element.43), calls=%async_computation.1 | async-start | bytes 4194304 | tf_op jit(solution)/shard_map/all_to_all | solution.py:725

commit v6 on v5

--- a/solution.py
+++ b/solution.py
@@ -122,7 +122,7 @@
 
 
 def pack_kernel(
-    first_ref, lists_hbm, block_hbm, out_hbm, lists_ref, block_ref, out_ref, row_ref, wanted_ref, lists_sem, in_sem, row_sem, out_sem
+    first_ref, lists_hbm, block_hbm, out_hbm, lists_ref, block_ref, row_ref, wanted_ref, lists_sem, in_sem, row_sem, out_sem
 ):
     load = pltpu.make_async_copy(block_hbm, block_ref, in_sem)
     lists = pltpu.make_async_copy(lists_hbm, lists_ref, lists_sem)
@@ -134,7 +134,7 @@
     row = jnp.broadcast_to(jnp.max(local, axis=0, keepdims=True), row_ref.shape)
     size = row.shape[1]
     step = 1
-    while step < size // out_ref.shape[0]:
+    while step < size // out_hbm.shape[0]:
         row = jnp.maximum(row, pltpu.roll(row, size - step, 1))
         step *= 2
     row_ref[...] = row.astype(jnp.int32)
@@ -142,19 +142,14 @@
     save.start()
     save.wait()
     load.wait()
-    share = size // out_ref.shape[0]
-    part_size = out_ref.shape[0] // CHUNKS
-    for chunk in range(CHUNKS):
-
-        def one(i, carry):
-            d = chunk * part_size + i
-            out_ref[d] = block_ref[wanted_ref[0, d * share]]
-            return carry
-
-        lax.fori_loop(0, part_size, one, 0, unroll=8)
-        part = pl.ds(chunk * part_size, part_size)
-        pltpu.make_async_copy(out_ref.at[part], out_hbm.at[part], out_sem).start()
-    pltpu.make_async_copy(out_ref, out_hbm, out_sem).wait()
+    share = size // out_hbm.shape[0]
+
+    def one(d, carry):
+        pltpu.make_async_copy(block_ref.at[wanted_ref[0, d * share]], out_hbm.at[d], out_sem).start()
+        return carry
+
+    lax.fori_loop(0, out_hbm.shape[0], one, 0, unroll=8)
+    pltpu.make_async_copy(out_hbm, out_hbm, out_sem).wait()
 
 
 def prep_kernel(split, rows, query_ref, full_ref, mask_ref):
@@ -172,12 +167,14 @@
 
 
 def dots_kernel(
-    shards, per_shard, rows, level, shifts, slot_ref, shard_ref, query_ref, pool_ref, full_ref, norm_ref, *refs
+    bounds, shards, per_shard, rows, shifts, slot_ref, shard_ref, query_ref, pool_ref, full_ref, pp_ref, *refs
 ):
-    outs, cand_ref = refs[:-1], refs[-1]
+    outs, (norm_ref, cand_ref) = refs[:-2], refs[-2:]
+    pool_norms(pool_ref, norm_ref, bounds)
     count, _, width = cand_ref.shape
     shard = shard_ref[0]
     base = per_shard * rows
+    last = len(bounds) - 1
     for shift, out_ref in zip(shifts, outs):
         target = lax.rem(shard + shift, shards)
         for k in range(per_shard):
@@ -186,17 +183,10 @@
             query = query_ref[pl.ds(block * rows, rows), :]
             cand = cand_ref[...].reshape(count * PBLK, width)
             out_ref[k * rows : (k + 1) * rows, :] = contract(query, cand, 1, 1)
-            out_ref[base + k : base + k + 1, :] = norm_rows(norm_ref, slot_ref, block, count)[level : level + 1, :]
+            pp = norm_rows(norm_ref, slot_ref, block, count)
+            pp_ref[block] = pp
+            out_ref[base + k : base + k + 1, :] = pp[last : last + 1, :]
             out_ref[base + per_shard : base + per_shard + 1, k * rows : (k + 1) * rows] = full_ref[block]
-
-
-def first_dots_kernel(
-    bounds, shards, per_shard, rows, shifts, slot_ref, shard_ref, query_ref, pool_ref, full_ref, norm_ref, *refs
-):
-    pool_norms(pool_ref, norm_ref, bounds)
-    dots_kernel(
-        shards, per_shard, rows, len(bounds) - 1, shifts, slot_ref, shard_ref, query_ref, pool_ref, full_ref, norm_ref, *refs
-    )
 
 
 def prefix_dots(bounds, rows, block, query_ref, cand_ref):
@@ -217,7 +207,7 @@
 
 
 def low_kernel(
-    bounds, rows, slot_ref, shard_ref, query_ref, pool_ref, norm_ref, ids_ref, pos_ref,
+    bounds, rows, slot_ref, shard_ref, query_ref, pool_ref, pp_ref, ids_ref, pos_ref,
     coef_hbm, row_hbm, col_hbm, loss_ref, cand_ref, term_ref, coef_ref, row_ref, col_ref, sem, row_sem, col_sem,
 ):
     count = cand_ref.shape[1]
@@ -232,7 +222,7 @@
         def one(block, cand_ref, term_ref):
             here = pl.ds(block * rows, rows)
             take_blocks(pool_ref, slot_ref, block, count, cand_ref)
-            pp = norm_rows(norm_ref, slot_ref, block, count)
+            pp = pp_ref[block]
             ids = ids_ref[pl.ds(block, 1), :]
             live = ids >= 0.0
             labels = jnp.where(ids == to_col(pos_ref[pl.ds(block, 1), :]), 1.0, 0.0)
@@ -439,15 +429,12 @@
                     lanes = slice(start, start + grad.shape[1])
                     sum_ref[slot, :, lanes] = sum_ref[slot, :, lanes] + grad[n * PBLK : (n + 1) * PBLK, :]
 
-        def step(pair, carry):
+        for pair in range(pairs):
             pair_load(pair).wait()
             for j in range(2):
                 one(pair * 2 + j)
             here = pair_rows(pair)
             pltpu.make_async_copy(half_ref.at[:, here], half_hbm.at[:, here], half_sem).start()
-            return carry
-
-        lax.fori_loop(0, pairs, step, 0)
         copy = pltpu.make_async_copy(half_ref, half_hbm, half_sem)
         level_of = lax.broadcasted_iota(jnp.int32, (LANES, width), 0)
         column = lax.broadcasted_iota(jnp.int32, (LANES, width), 1)
@@ -614,7 +601,6 @@
         scratch_shapes=[
             pltpu.VMEM((count, neg_lists.shape[0]), jnp.int32),
             pltpu.VMEM((local_blocks, PBLK, width), BF16),
-            pltpu.VMEM(pool_shape, BF16),
             pltpu.VMEM((8, neg_lists.shape[0]), jnp.int32),
             pltpu.SMEM((8, neg_lists.shape[0]), jnp.int32),
             pltpu.SemaphoreType.DMA(()),
@@ -646,13 +632,12 @@
 
     cand_scratch = pltpu.VMEM((count, PBLK, width), BF16)
     message = jax.ShapeDtypeStruct((base + AUX, cands), F32)
-    norm_shape = (slots, PBLK, LANES)
-    norms, far, right, left, here = pl.pallas_call(
-        partial(first_dots_kernel, bounds, shards, per_shard, rows, (2, 1, 3, 0)),
-        out_shape=[jax.ShapeDtypeStruct(norm_shape, F32)] + [message] * shards,
+    norm_rows_of, far, right, left, here = pl.pallas_call(
+        partial(dots_kernel, bounds, shards, per_shard, rows, (2, 1, 3, 0)),
+        out_shape=[jax.ShapeDtypeStruct((blocks, 8, cands), F32)] + [message] * shards,
         in_specs=[smem(), smem(), vmem(), vmem(), vmem()],
         out_specs=[vmem()] * (shards + 1),
-        scratch_shapes=[cand_scratch],
+        scratch_shapes=[pltpu.VMEM((slots, PBLK, LANES), F32), cand_scratch],
         compiler_params=params(),
         name="dots",
     )(slot, shard_arr, queries, pool, full_norms)
@@ -680,7 +665,7 @@
         ],
         compiler_params=params(),
         name="low",
-    )(slot, shard_arr, queries, pool, norms, ids, pos)
+    )(slot, shard_arr, queries, pool, norm_rows_of, ids, pos)
     *coefs, high_loss = pl.pallas_call(
         partial(high_kernel, shards, per_shard, rows, [size / MINP for size in high_sizes]),
         out_shape=[jax.ShapeDtypeStruct((base + COEF_AUX, cands), BF16)] * shards

time: 160 us -> 160 us (level)
  transfers between devices with their start and end apart: 8 -> 8, of which waited for: 5 -> 6; matrix products, arithmetic and copies ran while one was open for 1% -> 1% of each run, Pallas kernels for 8% -> 7%
where the time goes in v6:
time: 160 us
  waiting for transfers between devices  90.7 us (57%)
  starting transfers between devices  30.1 us (19%)
  Pallas kernels  29.3 us (18%)
  blocking collectives  7.38 us (5%)
    all_to_all x1, waiting for transfers between devices, per_device(): pool = lax.all_to_all(panels, 'dp', split_axis=0, concat_axis=0, tiled=True)  49.5 us
    all_to_all x1, waiting for transfers between devices, per_device(): lax.all_to_all(slot_grad, 'dp', split_axis=0, concat_axis=0, tiled=True)  37.5 us
    all_to_all x1, starting transfers between devices, per_device(): pool = lax.all_to_all(panels, 'dp', split_axis=0, concat_axis=0, tiled=True)  13.3 us
    ppermute x6, starting transfers between devices, shift_by(): lax.ppermute(part, 'tensor', [(i, (i + s) % shards) for i in range(shards)])  9.06 us
    all_to_all x1, starting transfers between devices, per_device(): lax.all_to_all(slot_grad, 'dp', split_axis=0, concat_axis=0, tiled=True)  7.73 us
    pallas_call x1, Pallas kernels, per_device(): pl.pallas_call(partial(passage_kernel, bounds, shards, per_shard, rows),...  7.48 us
    psum x1, blocking collectives, per_device(): loss = lax.psum(loss, 'tensor')  7.38 us
    pallas_call x1, Pallas kernels, per_device(): pl.pallas_call(partial(query_kernel, bounds, rows, 1.0 / weight_total), o...  5.82 us
  transfers between devices with their start and end apart: 8, of which 6 were waited for; matrix products, arithmetic and copies ran while one was open for 1% of the time, Pallas kernels for 7%

profile of v6, /device:TPU:1, one launch (start us, length us, event | category | flops | bytes accessed | tf_op | source)
XLA Modules:
  0.0 159.8 jit_solution(10287508970594459906)
XLA Ops:
  0.6 3.2 %pack.1 = bf16[64,16,1024]{2,1,0:T(8,128)(2,1)} custom-call(s32[1]{0:T(128)} %bitcast.1.first_ref, s32[16,512]{1,0:T(8,128)} %bitcast.8, bf16[16,16,1024]{2,1,0:T(8,128)(2,1)} %bitcast.7), custom_call_target="tpu_custom_call" | custom-call | tf_op jit(solution)/shard_map/pack/pallas_call | solution.py:596
  3.8 0.0 copy-start.2
  3.8 0.0 copy-start
  3.8 0.0 copy-start.3
  3.8 13.3 %all-to-all-start = ((bf16[64,16,1024]{2,1,0:T(8,128)(2,1)}), bf16[64,16,1024]{2,1,0:T(8,128)(2,1)S(1)}, u32[]{:S(2)}, u32[]{:S(2)}) async-start(bf16[64,16,1024]{2,1,0:T(8,128)(2,1)} %pack.1), calls=%async_computation | async-start | bytes 4194304 | tf_op jit(solution)/shard_map/all_to_all | solution.py:617
  17.1 0.0 copy-done.2
  17.2 0.1 constant_dynamic-slice_fusion
  17.2 0.1 copy.16
  17.3 0.1 add.57
  17.4 0.1 add.58
  17.5 0.1 broadcast_in_dim.40
  17.6 0.1 broadcast_in_dim.41
  17.7 0.1 add.60
  17.8 0.1 reshape.83.slot_ref
  17.9 0.0 copy-done
  17.9 1.0 prep.1
  18.8 0.0 copy-done.3
  18.8 0.1 convert_element_type.10.pos_ref
  18.9 49.5 %all-to-all-done.pool_ref = bf16[64,16,1024]{2,1,0:T(8,128)(2,1)S(1)} async-done(((bf16[64,16,1024]{2,1,0:T(8,128)(2,1)}), bf16[64,16,1024]{2,1,0:T(8,128)(2,1)S(1)}, u32[]{:S(2)}, u32[]{:S(2)}) %all-to-all-start) | async-done | bytes 2097184 | tf_op jit(solution)/shard_map/all_to_all | solution.py:617
  68.4 2.9 %dots.1 = (f32[8,8,256]{2,1,0:T(8,128)S(1)}, f32[136,256]{1,0:T(8,128)S(1)}, f32[136,256]{1,0:T(8,128)S(1)}, f32[136,256]{1,0:T(8,128)S(1)}, f32[136,256]{1,0:T(8,128)S(1)}) custom-call(s32[128]{0:T(128)S(1)} %reshape.83.slot_ref, s32[1]{0:T(128)} %bitcast.shard_ref, bf16[512,1024]{1,0:T(8,128)(2,1)S(1)} %copy-done, ...), custom_call_target="tpu_custom_call" | custom-call | tf_op jit(solution)/shard_map/dots/pallas_call | solution.py:635
  71.3 1.3 collective-permute-start
  72.6 2.5 %collective-permute-start.1 = (f32[136,256]{1,0:T(8,128)S(1)}, f32[136,256]{1,0:T(8,128)S(1)}, u32[]{:S(2)}, u32[]{:S(2)}) collective-permute-start(f32[136,256]{1,0:T(8,128)S(1)} %get-tuple-element.32), channel_id=1, source_target_pairs={{0,2},{1,3},{2,0},{3,1},{4,6},{5,7},{6,4},{7,5},{8,10},{9,11},{10,... | collective-permute-start | bytes 417800 | tf_op jit(solution)/shard_map/ppermute | solution.py:631
  75.1 1.2 collective-permute-start.2
  76.2 4.7 %low.1 = (f32[5,512,256]{2,1,0:T(8,128)}, f32[8,8,64]{2,1,0:T(8,128)}, f32[8,8,256]{2,1,0:T(8,128)}, f32[8,64]{1,0:T(8,128)S(1)}) custom-call(s32[128]{0:T(128)S(1)} %reshape.83.slot_ref, s32[1]{0:T(128)} %bitcast.shard_ref, bf16[512,1024]{1,0:T(8,128)(2,1)S(1)} %copy-done, bf16[64,16,1024]{2,1,0:T(8,128)(2,1)S(1)} %all-to-all-done.pool_ref, ...), custom_call_target="tpu_custom_call" | custom-call | tf_op jit(solution)/shard_map/low/pallas_call | solution.py:646
  81.0 0.0 collective-permute-done.refs_1_
  81.0 0.5 collective-permute-done.1.refs_2_
  81.4 0.0 collective-permute-done.2.refs_3_
  81.4 1.2 high.1
  82.6 1.1 collective-permute-start.3
  83.7 2.2 %collective-permute-start.4 = (bf16[160,256]{1,0:T(8,128)(2,1)}, bf16[160,256]{1,0:T(8,128)(2,1)}, u32[]{:S(2)}, u32[]{:S(2)}) collective-permute-start(bf16[160,256]{1,0:T(8,128)(2,1)} %get-tuple-element.36), channel_id=1, source_target_pairs={{0,2},{1,3},{2,0},{3,1},{4,6},{5,7},{6,4},{7,5},{8,10},{9,11},{10,... | collective-permute-start | bytes 245768 | tf_op jit(solution)/shard_map/ppermute | solution.py:631
  85.9 0.9 collective-permute-start.5
  86.8 0.1 reshape.87.slot_ref
  86.9 0.6 collective-permute-done.3.refs_1_
  87.5 1.5 collective-permute-done.4.refs_2_
  89.0 1.2 collective-permute-done.5.refs_3_
  90.2 7.5 %passage.1 = (bf16[64,16,1024]{2,1,0:T(8,128)(2,1)}, bf16[5,512,256]{2,1,0:T(8,128)(2,1)}, f32[8,8,64]{2,1,0:T(8,128)}) custom-call(s32[128]{0:T(128)S(1)} %reshape.87.slot_ref, s32[1]{0:T(128)} %bitcast.shard_ref, bf16[512,1024]{1,0:T(8,128)(2,1)S(1)} %copy-done, bf16[64,16,1024]{2,1,0:T(8,128)(2,1)S(1)} %all-to-all-done.pool_ref, ...), custom_call_target="tpu_custom_call" | custom-call | tf_op jit(solution)/shard_map/passage/pallas_call | solution.py:681
  97.7 0.0 copy-start.1
  97.7 7.7 %all-to-all-start.1 = ((bf16[64,16,1024]{2,1,0:T(8,128)(2,1)}), bf16[64,16,1024]{2,1,0:T(8,128)(2,1)}, u32[]{:S(2)}, u32[]{:S(2)}) async-start(bf16[64,16,1024]{2,1,0:T(8,128)(2,1)} %get-tuple-element.43), calls=%async_computation.1 | async-start | bytes 4194304 | tf_op jit(solution)/shard_map/all_to_all | solution.py:710
  105.4 0.1 fusion.2
  105.5 0.1 reduce_max.14
  105.6 0.1 reduce_max.18
  105.7 0.1 add_select_fusion.2
  105.8 0.1 select_n.63.target_ref
  105.9 0.0 copy-done.1
  105.9 5.8 %query.1 = (bf16[512,1024]{1,0:T(8,128)(2,1)}, f32[4,128]{1,0:T(4,128)S(1)}) custom-call(s32[128]{0:T(128)S(1)} %reshape.83.slot_ref, s32[1]{0:T(128)} %bitcast.shard_ref, bf16[512,1024]{1,0:T(8,128)(2,1)S(1)} %copy-done, bf16[64,16,1024]{2,1,0:T(8,128)(2,1)S(1)} %all-to-all-done.pool_ref, f32[8,8,64]{2,1,0:T(8,128)S(1)} %copy-done.1, ...), custom_call_target="tpu_custom_call" | custom-call | tf_op jit(solution)/shard_map/query/pallas_call | solution.py:712
  111.7 7.4 %psum.7 = f32[512]{0:T(512)} all-reduce(f32[512]{0:T(512)S(1)} %bitcast.6), channel_id=1, replica_groups=mesh['dp'=64,'tensor'=4] {'tensor'}, use_global_device_ids=true, to_apply=%region_2.3 | all-reduce | flops 512 | bytes 4096 | tf_op jit(solution)/shard_map/psum | solution.py:724
  119.1 37.5 %all-to-all-done.1 = bf16[64,16,1024]{2,1,0:T(8,128)(2,1)} async-done(((bf16[64,16,1024]{2,1,0:T(8,128)(2,1)}), bf16[64,16,1024]{2,1,0:T(8,128)(2,1)}, u32[]{:S(2)}, u32[]{:S(2)}) %all-to-all-start.1) | async-done | bytes 2097184 | tf_op jit(solution)/shard_map/all_to_all | solution.py:710
  156.6 3.1 %collect.1 = bf16[256,1024]{1,0:T(8,128)(2,1)} custom-call(s32[1,1024]{1,0:T(1,128)S(1)} %select_n.63.target_ref, bf16[1024,1024]{1,0:T(8,128)(2,1)} %bitcast.4.back_hbm), custom_call_target="tpu_custom_call" | custom-call | tf_op jit(solution)/shard_map/collect/pallas_call | solution.py:726
  (7 shorter events, 0.0 us)
Async XLA Ops:
  3.8 13.3 %copy-start.2 = (s32[512,16]{0,1:T(8,128)S(1)}, s32[512,16]{0,1:T(8,128)}, u32[]{:S(2)}) copy-start(s32[512,16]{0,1:T(8,128)} %param.6) | copy-start | bytes 98308
  3.8 14.1 %copy-start = (bf16[512,1024]{1,0:T(8,128)(2,1)S(1)}, bf16[512,1024]{1,0:T(8,128)(2,1)}, u32[]{:S(2)}) copy-start(bf16[512,1024]{1,0:T(8,128)(2,1)} %query_ref.9) | copy-start | bytes 3145732
  3.8 15.0 %copy-start.3 = (s32[512]{0:T(512)S(1)}, s32[512]{0:T(512)}, u32[]{:S(2)}) copy-start(s32[512]{0:T(512)} %param.7) | copy-start | bytes 6148
  3.8 64.6 %all-to-all-start = ((bf16[64,16,1024]{2,1,0:T(8,128)(2,1)}), bf16[64,16,1024]{2,1,0:T(8,128)(2,1)S(1)}, u32[]{:S(2)}, u32[]{:S(2)}) async-start(bf16[64,16,1024]{2,1,0:T(8,128)(2,1)} %pack.1), calls=%async_computation | async-start | bytes 4194304 | tf_op jit(solution)/shard_map/all_to_all | solution.py:617
  71.3 9.6 %collective-permute-start = (f32[136,256]{1,0:T(8,128)S(1)}, f32[136,256]{1,0:T(8,128)S(1)}, u32[]{:S(2)}, u32[]{:S(2)}) collective-permute-start(f32[136,256]{1,0:T(8,128)S(1)} %get-tuple-element.31), channel_id=1, source_target_pairs={{0,1},{1,2},{2,3},{3,0},{4,5},{5,6},{6,7},{7,4},{8,9},{9,10},{10,1... | collective-permute-start | bytes 417800 | tf_op jit(solution)/shard_map/ppermute | solution.py:631
  72.6 8.8 %collective-permute-start.1 = (f32[136,256]{1,0:T(8,128)S(1)}, f32[136,256]{1,0:T(8,128)S(1)}, u32[]{:S(2)}, u32[]{:S(2)}) collective-permute-start(f32[136,256]{1,0:T(8,128)S(1)} %get-tuple-element.32), channel_id=1, source_target_pairs={{0,2},{1,3},{2,0},{3,1},{4,6},{5,7},{6,4},{7,5},{8,10},{9,11},{10,... | collective-permute-start | bytes 417800 | tf_op jit(solution)/shard_map/ppermute | solution.py:631
  75.1 6.4 %collective-permute-start.2 = (f32[136,256]{1,0:T(8,128)S(1)}, f32[136,256]{1,0:T(8,128)S(1)}, u32[]{:S(2)}, u32[]{:S(2)}) collective-permute-start(f32[136,256]{1,0:T(8,128)S(1)} %get-tuple-element.33), channel_id=1, source_target_pairs={{0,3},{1,0},{2,1},{3,2},{4,7},{5,4},{6,5},{7,6},{8,11},{9,8},{10,9... | collective-permute-start | bytes 417800 | tf_op jit(solution)/shard_map/ppermute | solution.py:631
  82.6 4.8 %collective-permute-start.3 = (bf16[160,256]{1,0:T(8,128)(2,1)}, bf16[160,256]{1,0:T(8,128)(2,1)}, u32[]{:S(2)}, u32[]{:S(2)}) collective-permute-start(bf16[160,256]{1,0:T(8,128)(2,1)} %get-tuple-element.35), channel_id=1, source_target_pairs={{0,1},{1,2},{2,3},{3,0},{4,5},{5,6},{6,7},{7,4},{8,9},{9,10},{10,1... | collective-permute-start | bytes 245768 | tf_op jit(solution)/shard_map/ppermute | solution.py:631
  83.7 5.2 %collective-permute-start.4 = (bf16[160,256]{1,0:T(8,128)(2,1)}, bf16[160,256]{1,0:T(8,128)(2,1)}, u32[]{:S(2)}, u32[]{:S(2)}) collective-permute-start(bf16[160,256]{1,0:T(8,128)(2,1)} %get-tuple-element.36), channel_id=1, source_target_pairs={{0,2},{1,3},{2,0},{3,1},{4,6},{5,7},{6,4},{7,5},{8,10},{9,11},{10,... | collective-permute-start | bytes 245768 | tf_op jit(solution)/shard_map/ppermute | solution.py:631
  85.9 4.3 %collective-permute-start.5 = (bf16[160,256]{1,0:T(8,128)(2,1)}, bf16[160,256]{1,0:T(8,128)(2,1)}, u32[]{:S(2)}, u32[]{:S(2)}) collective-permute-start(bf16[160,256]{1,0:T(8,128)(2,1)} %get-tuple-element.37), channel_id=1, source_target_pairs={{0,3},{1,0},{2,1},{3,2},{4,7},{5,4},{6,5},{7,6},{8,11},{9,8},{10,9... | collective-permute-start | bytes 245768 | tf_op jit(solution)/shard_map/ppermute | solution.py:631
  97.7 8.2 %copy-start.1 = (f32[8,8,64]{2,1,0:T(8,128)S(1)}, f32[8,8,64]{2,1,0:T(8,128)}, u32[]{:S(2)}) copy-start(f32[8,8,64]{2,1,0:T(8,128)} %get-tuple-element.38.row_ref) | copy-start | bytes 49156
  97.7 58.9 %all-to-all-start.1 = ((bf16[64,16,1024]{2,1,0:T(8,128)(2,1)}), bf16[64,16,1024]{2,1,0:T(8,128)(2,1)}, u32[]{:S(2)}, u32[]{:S(2)}) async-start(bf16[64,16,1024]{2,1,0:T(8,128)(2,1)} %get-tuple-element.43), calls=%async_computation.1 | async-start | bytes 4194304 | tf_op jit(solution)/shard_map/all_to_all | solution.py:710

commit v7 on v6

--- a/solution.py
+++ b/solution.py
@@ -342,13 +342,28 @@
     return packed[:AUX] + packed[AUX : 2 * AUX] + packed[2 * AUX : 3 * AUX]
 
 
+def stage_kernel(shard_ref, row_hbm, col_hbm, coef_hbm, after_ref, row_ref, col_ref, coef_ref, sem):
+    del after_ref
+
+    @pl.when(shard_ref[0] == 0)
+    def _():
+        copies = [
+            pltpu.make_async_copy(source, target, sem.at[i])
+            for i, (source, target) in enumerate(((row_hbm, row_ref), (col_hbm, col_ref), (coef_hbm, coef_ref)))
+        ]
+        for copy in copies:
+            copy.start()
+        for copy in copies:
+            copy.wait()
+
+
 def passage_kernel(
-    bounds, shards, per_shard, rows, slot_ref, shard_ref, query_ref, pool_ref, mask_ref, low_row_hbm, low_col_hbm,
-    low_coef_hbm, *refs
+    bounds, shards, per_shard, rows, slot_ref, shard_ref, query_ref, pool_ref, mask_ref, low_row_ref, low_col_ref,
+    low_coef_ref, *refs
 ):
     ins = refs[:shards]
-    out_hbm, half_hbm, row_hbm, coef_ref, row_ref, col_ref, spread_ref, sum_ref, scale_ref, out_ref, half_ref = refs[shards:-8]
-    low_row_ref, low_col_ref, low_coef_ref, out_sem, half_sem, row_sem, low_sem, pair_sem = refs[-8:]
+    out_hbm, half_hbm, row_hbm, coef_ref, row_ref, col_ref, spread_ref, sum_ref, scale_ref, out_ref, half_ref = refs[shards:-3]
+    out_sem, half_sem, row_sem = refs[-3:]
     shard = shard_ref[0]
     base = per_shard * rows
     blocks = shards * per_shard
@@ -356,27 +371,15 @@
     cands = coef_ref.shape[1]
     count = cands // PBLK
 
-    loads = [
-        pltpu.make_async_copy(low_row_hbm, low_row_ref, low_sem.at[0]),
-        pltpu.make_async_copy(low_col_hbm, low_col_ref, low_sem.at[1]),
-    ]
     pairs = blocks // 2
 
     def pair_rows(pair):
         return pl.ds(pair * 2 * rows, 2 * rows)
 
-    def pair_load(pair):
-        here = pair_rows(pair)
-        return pltpu.make_async_copy(low_coef_hbm.at[:, here], low_coef_ref.at[:, here], pair_sem.at[pair])
-
     row_copy = pltpu.make_async_copy(row_ref, row_hbm, row_sem)
 
     @pl.when(shard == 0)
     def _():
-        for load in loads:
-            load.start()
-        for pair in range(pairs):
-            pair_load(pair).start()
         sum_ref[...] = jnp.zeros_like(sum_ref)
 
     scale_ref[...] = jnp.zeros_like(scale_ref)
@@ -405,8 +408,6 @@
     @pl.when(shard == 0)
     def _():
         levels = len(bounds)
-        for load in loads:
-            load.wait()
         row_ref[...] = row_ref[...] + low_row_ref[...]
         row_copy.start()
 
@@ -430,7 +431,6 @@
                     sum_ref[slot, :, lanes] = sum_ref[slot, :, lanes] + grad[n * PBLK : (n + 1) * PBLK, :]
 
         for pair in range(pairs):
-            pair_load(pair).wait()
             for j in range(2):
                 one(pair * 2 + j)
             here = pair_rows(pair)
@@ -675,13 +675,26 @@
         compiler_params=params(),
         name="high",
     )(shard_arr, ids, pos, pinned(low_row), *arrived)
+    staged_row, staged_col, staged_coef = pl.pallas_call(
+        stage_kernel,
+        out_shape=[
+            jax.ShapeDtypeStruct((blocks, 8, rows), F32),
+            jax.ShapeDtypeStruct((blocks, 8, cands), F32),
+            jax.ShapeDtypeStruct((levels, total_rows, cands), F32),
+        ],
+        in_specs=[smem()] + [hbm()] * 3 + [pl.BlockSpec(memory_space=pl.ANY)],
+        out_specs=[vmem()] * 3,
+        scratch_shapes=[pltpu.SemaphoreType.DMA((3,))],
+        compiler_params=params(),
+        name="stage",
+    )(shard_arr, pinned(low_row), pinned(low_col), pinned(low_coef), high_loss)
     coefs = [coefs[0]] + [shift_by(coefs[s], s) for s in range(1, shards)]
 
     half_shape = (levels, total_rows, cands)
     slot_grad, half, row_table = pl.pallas_call(
         partial(passage_kernel, bounds, shards, per_shard, rows),
         out_shape=[pltpu.HBM(pool_shape, BF16), pltpu.HBM(half_shape, BF16), pltpu.HBM((blocks, 8, rows), F32)],
-        in_specs=[smem(), smem()] + [vmem()] * 3 + [hbm()] * 3 + [vmem()] * shards,
+        in_specs=[smem(), smem()] + [vmem()] * (6 + shards),
         out_specs=[hbm()] * 3,
         scratch_shapes=[
             pltpu.VMEM((total_rows, cands), BF16),
@@ -692,20 +705,15 @@
             pltpu.VMEM((slots + 1, PBLK, LANES), F32),
             pltpu.VMEM(pool_shape, BF16),
             pltpu.VMEM(half_shape, BF16),
-            pltpu.VMEM((blocks, 8, rows), F32),
-            pltpu.VMEM((blocks, 8, cands), F32),
-            pltpu.VMEM((levels, total_rows, cands), F32),
-            pltpu.SemaphoreType.DMA(()),
-            pltpu.SemaphoreType.DMA(()),
-            pltpu.SemaphoreType.DMA(()),
-            pltpu.SemaphoreType.DMA((2,)),
-            pltpu.SemaphoreType.DMA((blocks // 2,)),
+            pltpu.SemaphoreType.DMA(()),
+            pltpu.SemaphoreType.DMA(()),
+            pltpu.SemaphoreType.DMA(()),
         ],
         compiler_params=params(),
         name="passage",
     )(
         spare_slot, shard_arr, queries, pool, masked,
-        pinned(low_row), pinned(low_col), pinned(low_coef), *coefs,
+        staged_row, staged_col, staged_coef, *coefs,
     )
     back = lax.all_to_all(slot_grad, "dp", split_axis=0, concat_axis=0, tiled=True)
 

time: 160 us -> 159 us (level)
  waiting for transfers between devices: 90.7 us -> 88.9 us
    ppermute x6, waiting for transfers between devices: 3.76 us -> 1.88 us  [shift_by(): lax.ppermute(part, 'tensor', [(i, (i + s) % shards) for i in range(shards)])]
    pallas_call x0 -> x1, Pallas kernels: none -> 1.83 us  [per_device(): pl.pallas_call(stage_kernel, out_shape=[jax.ShapeDtypeStruct((blocks, 8,...]
  transfers between devices with their start and end apart: 8 -> 8, of which waited for: 6 -> 5; matrix products, arithmetic and copies ran while one was open for 1% -> 1% of each run, Pallas kernels for 7% -> 8%
where the time goes in v7:
time: 159 us; the launch traced here: 158 us
  waiting for transfers between devices  88.9 us (56%)
  starting transfers between devices  30.1 us (19%)
  Pallas kernels  29.9 us (19%)
  blocking collectives  7.38 us (5%)
    all_to_all x1, waiting for transfers between devices, per_device(): pool = lax.all_to_all(panels, 'dp', split_axis=0, concat_axis=0, tiled=True)  49.5 us
    all_to_all x1, waiting for transfers between devices, per_device(): lax.all_to_all(slot_grad, 'dp', split_axis=0, concat_axis=0, tiled=True)  37.5 us
    all_to_all x1, starting transfers between devices, per_device(): pool = lax.all_to_all(panels, 'dp', split_axis=0, concat_axis=0, tiled=True)  13.3 us
    ppermute x6, starting transfers between devices, shift_by(): lax.ppermute(part, 'tensor', [(i, (i + s) % shards) for i in range(shards)])  9.05 us
    all_to_all x1, starting transfers between devices, per_device(): lax.all_to_all(slot_grad, 'dp', split_axis=0, concat_axis=0, tiled=True)  7.7 us
    psum x1, blocking collectives, per_device(): loss = lax.psum(loss, 'tensor')  7.38 us
    pallas_call x1, Pallas kernels, per_device(): pl.pallas_call(partial(passage_kernel, bounds, shards, per_shard, rows),...  6.11 us
    pallas_call x1, Pallas kernels, per_device(): pl.pallas_call(partial(query_kernel, bounds, rows, 1.0 / weight_total), o...  5.82 us
  transfers between devices with their start and end apart: 8, of which 5 were waited for; matrix products, arithmetic and copies ran while one was open for 1% of the time, Pallas kernels for 8%

profile of v7, /device:TPU:1, one launch (start us, length us, event | category | flops | bytes accessed | tf_op | source)
XLA Modules:
  0.0 158.4 jit_solution(9104830791503269366)
XLA Ops:
  0.6 3.2 %pack.1 = bf16[64,16,1024]{2,1,0:T(8,128)(2,1)} custom-call(s32[1]{0:T(128)} %bitcast.1.first_ref, s32[16,512]{1,0:T(8,128)} %bitcast.8, bf16[16,16,1024]{2,1,0:T(8,128)(2,1)} %bitcast.7), custom_call_target="tpu_custom_call" | custom-call | tf_op jit(solution)/shard_map/pack/pallas_call | solution.py:596
  3.8 0.0 copy-start.2
  3.8 0.0 copy-start
  3.8 0.0 copy-start.3
  3.9 13.3 %all-to-all-start = ((bf16[64,16,1024]{2,1,0:T(8,128)(2,1)}), bf16[64,16,1024]{2,1,0:T(8,128)(2,1)S(1)}, u32[]{:S(2)}, u32[]{:S(2)}) async-start(bf16[64,16,1024]{2,1,0:T(8,128)(2,1)} %pack.1), calls=%async_computation | async-start | bytes 4194304 | tf_op jit(solution)/shard_map/all_to_all | solution.py:617
  17.2 0.0 copy-done.2
  17.2 0.1 constant_dynamic-slice_fusion
  17.2 0.1 copy.16
  17.3 0.1 reshape.83.slot_ref
  17.4 0.0 copy-done
  17.4 0.9 prep.1
  18.4 0.1 add.57
  18.5 0.1 add.58
  18.6 0.1 broadcast_in_dim.40
  18.6 0.1 broadcast_in_dim.41
  18.8 0.1 add.60
  18.8 0.0 copy-done.3
  18.8 0.1 convert_element_type.10.pos_ref
  18.9 49.5 %all-to-all-done.pool_ref = bf16[64,16,1024]{2,1,0:T(8,128)(2,1)S(1)} async-done(((bf16[64,16,1024]{2,1,0:T(8,128)(2,1)}), bf16[64,16,1024]{2,1,0:T(8,128)(2,1)S(1)}, u32[]{:S(2)}, u32[]{:S(2)}) %all-to-all-start) | async-done | bytes 2097184 | tf_op jit(solution)/shard_map/all_to_all | solution.py:617
  68.4 2.9 %dots.1 = (f32[8,8,256]{2,1,0:T(8,128)S(1)}, f32[136,256]{1,0:T(8,128)S(1)}, f32[136,256]{1,0:T(8,128)S(1)}, f32[136,256]{1,0:T(8,128)S(1)}, f32[136,256]{1,0:T(8,128)S(1)}) custom-call(s32[128]{0:T(128)S(1)} %reshape.83.slot_ref, s32[1]{0:T(128)} %bitcast.shard_ref, bf16[512,1024]{1,0:T(8,128)(2,1)S(1)} %copy-done, ...), custom_call_target="tpu_custom_call" | custom-call | tf_op jit(solution)/shard_map/dots/pallas_call | solution.py:635
  71.3 1.3 collective-permute-start
  72.6 2.4 %collective-permute-start.1 = (f32[136,256]{1,0:T(8,128)S(1)}, f32[136,256]{1,0:T(8,128)S(1)}, u32[]{:S(2)}, u32[]{:S(2)}) collective-permute-start(f32[136,256]{1,0:T(8,128)S(1)} %get-tuple-element.35), channel_id=1, source_target_pairs={{0,2},{1,3},{2,0},{3,1},{4,6},{5,7},{6,4},{7,5},{8,10},{9,11},{10,... | collective-permute-start | bytes 417800 | tf_op jit(solution)/shard_map/ppermute | solution.py:631
  75.1 1.2 collective-permute-start.2
  76.2 4.8 %low.1 = (f32[5,512,256]{2,1,0:T(8,128)}, f32[8,8,64]{2,1,0:T(8,128)}, f32[8,8,256]{2,1,0:T(8,128)}, f32[8,64]{1,0:T(8,128)S(1)}) custom-call(s32[128]{0:T(128)S(1)} %reshape.83.slot_ref, s32[1]{0:T(128)} %bitcast.shard_ref, bf16[512,1024]{1,0:T(8,128)(2,1)S(1)} %copy-done, bf16[64,16,1024]{2,1,0:T(8,128)(2,1)S(1)} %all-to-all-done.pool_ref, ...), custom_call_target="tpu_custom_call" | custom-call | tf_op jit(solution)/shard_map/low/pallas_call | solution.py:646
  81.0 0.0 collective-permute-done.refs_1_
  81.0 0.4 collective-permute-done.1.refs_2_
  81.4 0.0 collective-permute-done.2.refs_3_
  81.4 1.2 high.1
  82.7 1.1 collective-permute-start.3
  83.7 2.2 %collective-permute-start.4 = (bf16[160,256]{1,0:T(8,128)(2,1)}, bf16[160,256]{1,0:T(8,128)(2,1)}, u32[]{:S(2)}, u32[]{:S(2)}) collective-permute-start(bf16[160,256]{1,0:T(8,128)(2,1)} %get-tuple-element.43), channel_id=1, source_target_pairs={{0,2},{1,3},{2,0},{3,1},{4,6},{5,7},{6,4},{7,5},{8,10},{9,11},{10,... | collective-permute-start | bytes 245768 | tf_op jit(solution)/shard_map/ppermute | solution.py:631
  85.9 0.9 collective-permute-start.5
  86.8 0.1 reshape.87.slot_ref
  86.9 1.8 %stage.1 = (f32[8,8,64]{2,1,0:T(8,128)S(1)}, f32[8,8,256]{2,1,0:T(8,128)S(1)}, f32[5,512,256]{2,1,0:T(8,128)S(1)}) custom-call(s32[1]{0:T(128)} %bitcast.shard_ref, f32[8,8,64]{2,1,0:T(8,128)} %get-tuple-element.30.after_ref.row_hbm, f32[8,8,256]{2,1,0:T(8,128)} %get-tuple-element.31.col_hbm, f32[5,512,256]{2,1,0:T(8,128)} %get-tuple-element.32.coef_hbm, ...), custom_call_target="tpu_custom_call" | custom-call | tf_op jit(solution)/shard_map/stage/pallas_call | solution.py:678
  88.8 0.0 collective-permute-done.3.refs_1_
  88.8 0.2 collective-permute-done.4.refs_2_
  89.0 1.2 collective-permute-done.5.refs_3_
  90.2 6.1 %passage.1 = (bf16[64,16,1024]{2,1,0:T(8,128)(2,1)}, bf16[5,512,256]{2,1,0:T(8,128)(2,1)}, f32[8,8,64]{2,1,0:T(8,128)}) custom-call(s32[128]{0:T(128)S(1)} %reshape.87.slot_ref, s32[1]{0:T(128)} %bitcast.shard_ref, bf16[512,1024]{1,0:T(8,128)(2,1)S(1)} %copy-done, bf16[64,16,1024]{2,1,0:T(8,128)(2,1)S(1)} %all-to-all-done.pool_ref, ...), custom_call_target="tpu_custom_call" | custom-call | tf_op jit(solution)/shard_map/passage/pallas_call | solution.py:694
  96.3 0.0 copy-start.1
  96.3 7.7 %all-to-all-start.1 = ((bf16[64,16,1024]{2,1,0:T(8,128)(2,1)}), bf16[64,16,1024]{2,1,0:T(8,128)(2,1)}, u32[]{:S(2)}, u32[]{:S(2)}) async-start(bf16[64,16,1024]{2,1,0:T(8,128)(2,1)} %get-tuple-element.49), calls=%async_computation.1 | async-start | bytes 4194304 | tf_op jit(solution)/shard_map/all_to_all | solution.py:718
  104.1 0.1 fusion.2
  104.1 0.1 reduce_max.14
  104.2 0.1 reduce_max.18
  104.3 0.1 add_select_fusion.2
  104.4 0.1 select_n.63.target_ref
  104.5 0.0 copy-done.1
  104.5 5.8 %query.1 = (bf16[512,1024]{1,0:T(8,128)(2,1)}, f32[4,128]{1,0:T(4,128)S(1)}) custom-call(s32[128]{0:T(128)S(1)} %reshape.83.slot_ref, s32[1]{0:T(128)} %bitcast.shard_ref, bf16[512,1024]{1,0:T(8,128)(2,1)S(1)} %copy-done, bf16[64,16,1024]{2,1,0:T(8,128)(2,1)S(1)} %all-to-all-done.pool_ref, f32[8,8,64]{2,1,0:T(8,128)S(1)} %copy-done.1, ...), custom_call_target="tpu_custom_call" | custom-call | tf_op jit(solution)/shard_map/query/pallas_call | solution.py:720
  110.3 7.4 %psum.7 = f32[512]{0:T(512)} all-reduce(f32[512]{0:T(512)S(1)} %bitcast.6), channel_id=1, replica_groups=mesh['dp'=64,'tensor'=4] {'tensor'}, use_global_device_ids=true, to_apply=%region_2.3 | all-reduce | flops 512 | bytes 4096 | tf_op jit(solution)/shard_map/psum | solution.py:732
  117.7 37.5 %all-to-all-done.1 = bf16[64,16,1024]{2,1,0:T(8,128)(2,1)} async-done(((bf16[64,16,1024]{2,1,0:T(8,128)(2,1)}), bf16[64,16,1024]{2,1,0:T(8,128)(2,1)}, u32[]{:S(2)}, u32[]{:S(2)}) %all-to-all-start.1) | async-done | bytes 2097184 | tf_op jit(solution)/shard_map/all_to_all | solution.py:718
  155.2 3.1 %collect.1 = bf16[256,1024]{1,0:T(8,128)(2,1)} custom-call(s32[1,1024]{1,0:T(1,128)S(1)} %select_n.63.target_ref, bf16[1024,1024]{1,0:T(8,128)(2,1)} %bitcast.4.back_hbm), custom_call_target="tpu_custom_call" | custom-call | tf_op jit(solution)/shard_map/collect/pallas_call | solution.py:734
  (7 shorter events, 0.0 us)
Async XLA Ops:
  3.8 13.3 %copy-start.2 = (s32[512,16]{0,1:T(8,128)S(1)}, s32[512,16]{0,1:T(8,128)}, u32[]{:S(2)}) copy-start(s32[512,16]{0,1:T(8,128)} %param.6) | copy-start | bytes 98308
  3.8 13.6 %copy-start = (bf16[512,1024]{1,0:T(8,128)(2,1)S(1)}, bf16[512,1024]{1,0:T(8,128)(2,1)}, u32[]{:S(2)}) copy-start(bf16[512,1024]{1,0:T(8,128)(2,1)} %query_ref.9) | copy-start | bytes 3145732
  3.8 15.0 %copy-start.3 = (s32[512]{0:T(512)S(1)}, s32[512]{0:T(512)}, u32[]{:S(2)}) copy-start(s32[512]{0:T(512)} %param.7) | copy-start | bytes 6148
  3.9 64.6 %all-to-all-start = ((bf16[64,16,1024]{2,1,0:T(8,128)(2,1)}), bf16[64,16,1024]{2,1,0:T(8,128)(2,1)S(1)}, u32[]{:S(2)}, u32[]{:S(2)}) async-start(bf16[64,16,1024]{2,1,0:T(8,128)(2,1)} %pack.1), calls=%async_computation | async-start | bytes 4194304 | tf_op jit(solution)/shard_map/all_to_all | solution.py:617
  71.3 9.7 %collective-permute-start = (f32[136,256]{1,0:T(8,128)S(1)}, f32[136,256]{1,0:T(8,128)S(1)}, u32[]{:S(2)}, u32[]{:S(2)}) collective-permute-start(f32[136,256]{1,0:T(8,128)S(1)} %get-tuple-element.34), channel_id=1, source_target_pairs={{0,1},{1,2},{2,3},{3,0},{4,5},{5,6},{6,7},{7,4},{8,9},{9,10},{10,1... | collective-permute-start | bytes 417800 | tf_op jit(solution)/shard_map/ppermute | solution.py:631
  72.6 8.8 %collective-permute-start.1 = (f32[136,256]{1,0:T(8,128)S(1)}, f32[136,256]{1,0:T(8,128)S(1)}, u32[]{:S(2)}, u32[]{:S(2)}) collective-permute-start(f32[136,256]{1,0:T(8,128)S(1)} %get-tuple-element.35), channel_id=1, source_target_pairs={{0,2},{1,3},{2,0},{3,1},{4,6},{5,7},{6,4},{7,5},{8,10},{9,11},{10,... | collective-permute-start | bytes 417800 | tf_op jit(solution)/shard_map/ppermute | solution.py:631
  75.1 6.4 %collective-permute-start.2 = (f32[136,256]{1,0:T(8,128)S(1)}, f32[136,256]{1,0:T(8,128)S(1)}, u32[]{:S(2)}, u32[]{:S(2)}) collective-permute-start(f32[136,256]{1,0:T(8,128)S(1)} %get-tuple-element.36), channel_id=1, source_target_pairs={{0,3},{1,0},{2,1},{3,2},{4,7},{5,4},{6,5},{7,6},{8,11},{9,8},{10,9... | collective-permute-start | bytes 417800 | tf_op jit(solution)/shard_map/ppermute | solution.py:631
  82.7 6.1 %collective-permute-start.3 = (bf16[160,256]{1,0:T(8,128)(2,1)}, bf16[160,256]{1,0:T(8,128)(2,1)}, u32[]{:S(2)}, u32[]{:S(2)}) collective-permute-start(bf16[160,256]{1,0:T(8,128)(2,1)} %get-tuple-element.42), channel_id=1, source_target_pairs={{0,1},{1,2},{2,3},{3,0},{4,5},{5,6},{6,7},{7,4},{8,9},{9,10},{10,1... | collective-permute-start | bytes 245768 | tf_op jit(solution)/shard_map/ppermute | solution.py:631
  83.7 5.2 %collective-permute-start.4 = (bf16[160,256]{1,0:T(8,128)(2,1)}, bf16[160,256]{1,0:T(8,128)(2,1)}, u32[]{:S(2)}, u32[]{:S(2)}) collective-permute-start(bf16[160,256]{1,0:T(8,128)(2,1)} %get-tuple-element.43), channel_id=1, source_target_pairs={{0,2},{1,3},{2,0},{3,1},{4,6},{5,7},{6,4},{7,5},{8,10},{9,11},{10,... | collective-permute-start | bytes 245768 | tf_op jit(solution)/shard_map/ppermute | solution.py:631
  85.9 4.3 %collective-permute-start.5 = (bf16[160,256]{1,0:T(8,128)(2,1)}, bf16[160,256]{1,0:T(8,128)(2,1)}, u32[]{:S(2)}, u32[]{:S(2)}) collective-permute-start(bf16[160,256]{1,0:T(8,128)(2,1)} %get-tuple-element.44), channel_id=1, source_target_pairs={{0,3},{1,0},{2,1},{3,2},{4,7},{5,4},{6,5},{7,6},{8,11},{9,8},{10,9... | collective-permute-start | bytes 245768 | tf_op jit(solution)/shard_map/ppermute | solution.py:631
  96.3 8.2 %copy-start.1 = (f32[8,8,64]{2,1,0:T(8,128)S(1)}, f32[8,8,64]{2,1,0:T(8,128)}, u32[]{:S(2)}) copy-start(f32[8,8,64]{2,1,0:T(8,128)} %get-tuple-element.45.row_ref) | copy-start | bytes 49156
  96.3 58.9 %all-to-all-start.1 = ((bf16[64,16,1024]{2,1,0:T(8,128)(2,1)}), bf16[64,16,1024]{2,1,0:T(8,128)(2,1)}, u32[]{:S(2)}, u32[]{:S(2)}) async-start(bf16[64,16,1024]{2,1,0:T(8,128)(2,1)} %get-tuple-element.49), calls=%async_computation.1 | async-start | bytes 4194304 | tf_op jit(solution)/shard_map/all_to_all | solution.py:718

commit v8 on v7

--- a/solution.py
+++ b/solution.py
@@ -92,8 +92,8 @@
     def lane_sum(part):
         return jnp.sum(part, axis=1, keepdims=True)
 
-    def step(i, carry):
-        here = pl.ds(i * step_slots, step_slots)
+    def step(i):
+        here = slice(i * step_slots, (i + 1) * step_slots)
         wide = pool_ref[here].reshape(rows, pool_ref.shape[2]).astype(F32)
         square = wide * wide
         result, before, inside = None, None, None
@@ -111,9 +111,9 @@
             before = total
             result = jnp.broadcast_to(total, (rows, LANES)) if result is None else jnp.where(lane == level, total, result)
         norm_ref[here] = result.reshape(step_slots, PBLK, LANES)
-        return carry
-
-    lax.fori_loop(0, pool_ref.shape[0] // step_slots, step, 0, unroll=4)
+
+    for i in range(pool_ref.shape[0] // step_slots):
+        step(i)
 
 
 def norm_rows(norm_ref, slot_ref, block, count):

time: 159 us -> 158 us (level)
  no operation moved by 1% of the time
where the time goes in v8:
time: 158 us; the launch traced here: 157 us
  waiting for transfers between devices  88.9 us (56%)
  starting transfers between devices  30.1 us (19%)
  Pallas kernels  28.9 us (18%)
  blocking collectives  7.38 us (5%)
    all_to_all x1, waiting for transfers between devices, per_device(): pool = lax.all_to_all(panels, 'dp', split_axis=0, concat_axis=0, tiled=True)  49.5 us
    all_to_all x1, waiting for transfers between devices, per_device(): lax.all_to_all(slot_grad, 'dp', split_axis=0, concat_axis=0, tiled=True)  37.5 us
    all_to_all x1, starting transfers between devices, per_device(): pool = lax.all_to_all(panels, 'dp', split_axis=0, concat_axis=0, tiled=True)  13.3 us
    ppermute x6, starting transfers between devices, shift_by(): lax.ppermute(part, 'tensor', [(i, (i + s) % shards) for i in range(shards)])  9.06 us
    all_to_all x1, starting transfers between devices, per_device(): lax.all_to_all(slot_grad, 'dp', split_axis=0, concat_axis=0, tiled=True)  7.71 us
    psum x1, blocking collectives, per_device(): loss = lax.psum(loss, 'tensor')  7.38 us
    pallas_call x1, Pallas kernels, per_device(): pl.pallas_call(partial(passage_kernel, bounds, shards, per_shard, rows),...  6.11 us
    pallas_call x1, Pallas kernels, per_device(): pl.pallas_call(partial(query_kernel, bounds, rows, 1.0 / weight_total), o...  5.81 us
  transfers between devices with their start and end apart: 8, of which 5 were waited for; matrix products, arithmetic and copies ran while one was open for 1% of the time, Pallas kernels for 8%

profile of v8, /device:TPU:1, one launch (start us, length us, event | category | flops | bytes accessed | tf_op | source)
XLA Modules:
  0.0 157.5 jit_solution(6024724161590413792)
XLA Ops:
  0.6 3.2 %pack.1 = bf16[64,16,1024]{2,1,0:T(8,128)(2,1)} custom-call(s32[1]{0:T(128)} %bitcast.1.first_ref, s32[16,512]{1,0:T(8,128)} %bitcast.8, bf16[16,16,1024]{2,1,0:T(8,128)(2,1)} %bitcast.7), custom_call_target="tpu_custom_call" | custom-call | tf_op jit(solution)/shard_map/pack/pallas_call | solution.py:596
  3.8 0.0 copy-start.2
  3.8 0.0 copy-start
  3.8 0.0 copy-start.3
  3.9 13.3 %all-to-all-start = ((bf16[64,16,1024]{2,1,0:T(8,128)(2,1)}), bf16[64,16,1024]{2,1,0:T(8,128)(2,1)S(1)}, u32[]{:S(2)}, u32[]{:S(2)}) async-start(bf16[64,16,1024]{2,1,0:T(8,128)(2,1)} %pack.1), calls=%async_computation | async-start | bytes 4194304 | tf_op jit(solution)/shard_map/all_to_all | solution.py:617
  17.2 0.0 copy-done.2
  17.2 0.1 constant_dynamic-slice_fusion
  17.2 0.1 copy.16
  17.3 0.1 reshape.83.slot_ref
  17.4 0.0 copy-done
  17.4 0.9 prep.1
  18.4 0.1 add.57
  18.5 0.1 add.58
  18.6 0.1 broadcast_in_dim.40
  18.6 0.1 broadcast_in_dim.41
  18.8 0.1 add.60
  18.8 0.0 copy-done.3
  18.8 0.1 convert_element_type.10.pos_ref
  18.9 49.5 %all-to-all-done.pool_ref = bf16[64,16,1024]{2,1,0:T(8,128)(2,1)S(1)} async-done(((bf16[64,16,1024]{2,1,0:T(8,128)(2,1)}), bf16[64,16,1024]{2,1,0:T(8,128)(2,1)S(1)}, u32[]{:S(2)}, u32[]{:S(2)}) %all-to-all-start) | async-done | bytes 2097184 | tf_op jit(solution)/shard_map/all_to_all | solution.py:617
  68.4 2.0 %dots.1 = (f32[8,8,256]{2,1,0:T(8,128)S(1)}, f32[136,256]{1,0:T(8,128)S(1)}, f32[136,256]{1,0:T(8,128)S(1)}, f32[136,256]{1,0:T(8,128)S(1)}, f32[136,256]{1,0:T(8,128)S(1)}) custom-call(s32[128]{0:T(128)S(1)} %reshape.83.slot_ref, s32[1]{0:T(128)} %bitcast.shard_ref, bf16[512,1024]{1,0:T(8,128)(2,1)S(1)} %copy-done, ...), custom_call_target="tpu_custom_call" | custom-call | tf_op jit(solution)/shard_map/dots/pallas_call | solution.py:635
  70.4 1.3 collective-permute-start
  71.7 2.4 %collective-permute-start.1 = (f32[136,256]{1,0:T(8,128)S(1)}, f32[136,256]{1,0:T(8,128)S(1)}, u32[]{:S(2)}, u32[]{:S(2)}) collective-permute-start(f32[136,256]{1,0:T(8,128)S(1)} %get-tuple-element.35), channel_id=1, source_target_pairs={{0,2},{1,3},{2,0},{3,1},{4,6},{5,7},{6,4},{7,5},{8,10},{9,11},{10,... | collective-permute-start | bytes 417800 | tf_op jit(solution)/shard_map/ppermute | solution.py:631
  74.1 1.2 collective-permute-start.2
  75.3 4.8 %low.1 = (f32[5,512,256]{2,1,0:T(8,128)}, f32[8,8,64]{2,1,0:T(8,128)}, f32[8,8,256]{2,1,0:T(8,128)}, f32[8,64]{1,0:T(8,128)S(1)}) custom-call(s32[128]{0:T(128)S(1)} %reshape.83.slot_ref, s32[1]{0:T(128)} %bitcast.shard_ref, bf16[512,1024]{1,0:T(8,128)(2,1)S(1)} %copy-done, bf16[64,16,1024]{2,1,0:T(8,128)(2,1)S(1)} %all-to-all-done.pool_ref, ...), custom_call_target="tpu_custom_call" | custom-call | tf_op jit(solution)/shard_map/low/pallas_call | solution.py:646
  80.0 0.0 collective-permute-done.refs_1_
  80.1 0.4 collective-permute-done.1.refs_2_
  80.5 0.0 collective-permute-done.2.refs_3_
  80.5 1.2 high.1
  81.7 1.1 collective-permute-start.3
  82.8 2.2 %collective-permute-start.4 = (bf16[160,256]{1,0:T(8,128)(2,1)}, bf16[160,256]{1,0:T(8,128)(2,1)}, u32[]{:S(2)}, u32[]{:S(2)}) collective-permute-start(bf16[160,256]{1,0:T(8,128)(2,1)} %get-tuple-element.43), channel_id=1, source_target_pairs={{0,2},{1,3},{2,0},{3,1},{4,6},{5,7},{6,4},{7,5},{8,10},{9,11},{10,... | collective-permute-start | bytes 245768 | tf_op jit(solution)/shard_map/ppermute | solution.py:631
  84.9 0.9 collective-permute-start.5
  85.9 0.1 reshape.87.slot_ref
  86.0 1.8 %stage.1 = (f32[8,8,64]{2,1,0:T(8,128)S(1)}, f32[8,8,256]{2,1,0:T(8,128)S(1)}, f32[5,512,256]{2,1,0:T(8,128)S(1)}) custom-call(s32[1]{0:T(128)} %bitcast.shard_ref, f32[8,8,64]{2,1,0:T(8,128)} %get-tuple-element.30.after_ref.row_hbm, f32[8,8,256]{2,1,0:T(8,128)} %get-tuple-element.31.col_hbm, f32[5,512,256]{2,1,0:T(8,128)} %get-tuple-element.32.coef_hbm, ...), custom_call_target="tpu_custom_call" | custom-call | tf_op jit(solution)/shard_map/stage/pallas_call | solution.py:678
  87.8 0.0 collective-permute-done.3.refs_1_
  87.8 0.2 collective-permute-done.4.refs_2_
  88.0 1.2 collective-permute-done.5.refs_3_
  89.2 6.1 %passage.1 = (bf16[64,16,1024]{2,1,0:T(8,128)(2,1)}, bf16[5,512,256]{2,1,0:T(8,128)(2,1)}, f32[8,8,64]{2,1,0:T(8,128)}) custom-call(s32[128]{0:T(128)S(1)} %reshape.87.slot_ref, s32[1]{0:T(128)} %bitcast.shard_ref, bf16[512,1024]{1,0:T(8,128)(2,1)S(1)} %copy-done, bf16[64,16,1024]{2,1,0:T(8,128)(2,1)S(1)} %all-to-all-done.pool_ref, ...), custom_call_target="tpu_custom_call" | custom-call | tf_op jit(solution)/shard_map/passage/pallas_call | solution.py:694
  95.4 0.0 copy-start.1
  95.4 7.7 %all-to-all-start.1 = ((bf16[64,16,1024]{2,1,0:T(8,128)(2,1)}), bf16[64,16,1024]{2,1,0:T(8,128)(2,1)}, u32[]{:S(2)}, u32[]{:S(2)}) async-start(bf16[64,16,1024]{2,1,0:T(8,128)(2,1)} %get-tuple-element.49), calls=%async_computation.1 | async-start | bytes 4194304 | tf_op jit(solution)/shard_map/all_to_all | solution.py:718
  103.1 0.1 fusion.2
  103.2 0.1 reduce_max.14
  103.2 0.1 reduce_max.18
  103.4 0.1 add_select_fusion.2
  103.5 0.1 select_n.63.target_ref
  103.6 0.0 copy-done.1
  103.6 5.8 %query.1 = (bf16[512,1024]{1,0:T(8,128)(2,1)}, f32[4,128]{1,0:T(4,128)S(1)}) custom-call(s32[128]{0:T(128)S(1)} %reshape.83.slot_ref, s32[1]{0:T(128)} %bitcast.shard_ref, bf16[512,1024]{1,0:T(8,128)(2,1)S(1)} %copy-done, bf16[64,16,1024]{2,1,0:T(8,128)(2,1)S(1)} %all-to-all-done.pool_ref, f32[8,8,64]{2,1,0:T(8,128)S(1)} %copy-done.1, ...), custom_call_target="tpu_custom_call" | custom-call | tf_op jit(solution)/shard_map/query/pallas_call | solution.py:720
  109.4 7.4 %psum.7 = f32[512]{0:T(512)} all-reduce(f32[512]{0:T(512)S(1)} %bitcast.6), channel_id=1, replica_groups=mesh['dp'=64,'tensor'=4] {'tensor'}, use_global_device_ids=true, to_apply=%region_2.3 | all-reduce | flops 512 | bytes 4096 | tf_op jit(solution)/shard_map/psum | solution.py:732
  116.8 37.5 %all-to-all-done.1 = bf16[64,16,1024]{2,1,0:T(8,128)(2,1)} async-done(((bf16[64,16,1024]{2,1,0:T(8,128)(2,1)}), bf16[64,16,1024]{2,1,0:T(8,128)(2,1)}, u32[]{:S(2)}, u32[]{:S(2)}) %all-to-all-start.1) | async-done | bytes 2097184 | tf_op jit(solution)/shard_map/all_to_all | solution.py:718
  154.3 3.1 %collect.1 = bf16[256,1024]{1,0:T(8,128)(2,1)} custom-call(s32[1,1024]{1,0:T(1,128)S(1)} %select_n.63.target_ref, bf16[1024,1024]{1,0:T(8,128)(2,1)} %bitcast.4.back_hbm), custom_call_target="tpu_custom_call" | custom-call | tf_op jit(solution)/shard_map/collect/pallas_call | solution.py:734
  (7 shorter events, 0.0 us)
Async XLA Ops:
  3.8 13.3 %copy-start.2 = (s32[512,16]{0,1:T(8,128)S(1)}, s32[512,16]{0,1:T(8,128)}, u32[]{:S(2)}) copy-start(s32[512,16]{0,1:T(8,128)} %param.6) | copy-start | bytes 98308
  3.8 13.6 %copy-start = (bf16[512,1024]{1,0:T(8,128)(2,1)S(1)}, bf16[512,1024]{1,0:T(8,128)(2,1)}, u32[]{:S(2)}) copy-start(bf16[512,1024]{1,0:T(8,128)(2,1)} %query_ref.9) | copy-start | bytes 3145732
  3.8 15.0 %copy-start.3 = (s32[512]{0:T(512)S(1)}, s32[512]{0:T(512)}, u32[]{:S(2)}) copy-start(s32[512]{0:T(512)} %param.7) | copy-start | bytes 6148
  3.9 64.6 %all-to-all-start = ((bf16[64,16,1024]{2,1,0:T(8,128)(2,1)}), bf16[64,16,1024]{2,1,0:T(8,128)(2,1)S(1)}, u32[]{:S(2)}, u32[]{:S(2)}) async-start(bf16[64,16,1024]{2,1,0:T(8,128)(2,1)} %pack.1), calls=%async_computation | async-start | bytes 4194304 | tf_op jit(solution)/shard_map/all_to_all | solution.py:617
  70.4 9.7 %collective-permute-start = (f32[136,256]{1,0:T(8,128)S(1)}, f32[136,256]{1,0:T(8,128)S(1)}, u32[]{:S(2)}, u32[]{:S(2)}) collective-permute-start(f32[136,256]{1,0:T(8,128)S(1)} %get-tuple-element.34), channel_id=1, source_target_pairs={{0,1},{1,2},{2,3},{3,0},{4,5},{5,6},{6,7},{7,4},{8,9},{9,10},{10,1... | collective-permute-start | bytes 417800 | tf_op jit(solution)/shard_map/ppermute | solution.py:631
  71.7 8.8 %collective-permute-start.1 = (f32[136,256]{1,0:T(8,128)S(1)}, f32[136,256]{1,0:T(8,128)S(1)}, u32[]{:S(2)}, u32[]{:S(2)}) collective-permute-start(f32[136,256]{1,0:T(8,128)S(1)} %get-tuple-element.35), channel_id=1, source_target_pairs={{0,2},{1,3},{2,0},{3,1},{4,6},{5,7},{6,4},{7,5},{8,10},{9,11},{10,... | collective-permute-start | bytes 417800 | tf_op jit(solution)/shard_map/ppermute | solution.py:631
  74.1 6.4 %collective-permute-start.2 = (f32[136,256]{1,0:T(8,128)S(1)}, f32[136,256]{1,0:T(8,128)S(1)}, u32[]{:S(2)}, u32[]{:S(2)}) collective-permute-start(f32[136,256]{1,0:T(8,128)S(1)} %get-tuple-element.36), channel_id=1, source_target_pairs={{0,3},{1,0},{2,1},{3,2},{4,7},{5,4},{6,5},{7,6},{8,11},{9,8},{10,9... | collective-permute-start | bytes 417800 | tf_op jit(solution)/shard_map/ppermute | solution.py:631
  81.7 6.1 %collective-permute-start.3 = (bf16[160,256]{1,0:T(8,128)(2,1)}, bf16[160,256]{1,0:T(8,128)(2,1)}, u32[]{:S(2)}, u32[]{:S(2)}) collective-permute-start(bf16[160,256]{1,0:T(8,128)(2,1)} %get-tuple-element.42), channel_id=1, source_target_pairs={{0,1},{1,2},{2,3},{3,0},{4,5},{5,6},{6,7},{7,4},{8,9},{9,10},{10,1... | collective-permute-start | bytes 245768 | tf_op jit(solution)/shard_map/ppermute | solution.py:631
  82.8 5.2 %collective-permute-start.4 = (bf16[160,256]{1,0:T(8,128)(2,1)}, bf16[160,256]{1,0:T(8,128)(2,1)}, u32[]{:S(2)}, u32[]{:S(2)}) collective-permute-start(bf16[160,256]{1,0:T(8,128)(2,1)} %get-tuple-element.43), channel_id=1, source_target_pairs={{0,2},{1,3},{2,0},{3,1},{4,6},{5,7},{6,4},{7,5},{8,10},{9,11},{10,... | collective-permute-start | bytes 245768 | tf_op jit(solution)/shard_map/ppermute | solution.py:631
  84.9 4.3 %collective-permute-start.5 = (bf16[160,256]{1,0:T(8,128)(2,1)}, bf16[160,256]{1,0:T(8,128)(2,1)}, u32[]{:S(2)}, u32[]{:S(2)}) collective-permute-start(bf16[160,256]{1,0:T(8,128)(2,1)} %get-tuple-element.44), channel_id=1, source_target_pairs={{0,3},{1,0},{2,1},{3,2},{4,7},{5,4},{6,5},{7,6},{8,11},{9,8},{10,9... | collective-permute-start | bytes 245768 | tf_op jit(solution)/shard_map/ppermute | solution.py:631
  95.4 8.2 %copy-start.1 = (f32[8,8,64]{2,1,0:T(8,128)S(1)}, f32[8,8,64]{2,1,0:T(8,128)}, u32[]{:S(2)}) copy-start(f32[8,8,64]{2,1,0:T(8,128)} %get-tuple-element.45.row_ref) | copy-start | bytes 49156
  95.4 58.9 %all-to-all-start.1 = ((bf16[64,16,1024]{2,1,0:T(8,128)(2,1)}), bf16[64,16,1024]{2,1,0:T(8,128)(2,1)}, u32[]{:S(2)}, u32[]{:S(2)}) async-start(bf16[64,16,1024]{2,1,0:T(8,128)(2,1)} %get-tuple-element.49), calls=%async_computation.1 | async-start | bytes 4194304 | tf_op jit(solution)/shard_map/all_to_all | solution.py:718

commit v9 on v8

--- a/solution.py
+++ b/solution.py
@@ -371,11 +371,6 @@
     cands = coef_ref.shape[1]
     count = cands // PBLK
 
-    pairs = blocks // 2
-
-    def pair_rows(pair):
-        return pl.ds(pair * 2 * rows, 2 * rows)
-
     row_copy = pltpu.make_async_copy(row_ref, row_hbm, row_sem)
 
     @pl.when(shard == 0)
@@ -411,51 +406,53 @@
         row_ref[...] = row_ref[...] + low_row_ref[...]
         row_copy.start()
 
-        def one(block):
-            here = pl.ds(block * rows, rows)
-            add_scales(block, True)
-            base_coef = coef_ref[here, :].astype(F32)
-            coefs = [(base_coef + low_coef_ref[level, here, :]).astype(BF16) for level in range(levels)]
-            for level in range(levels):
-                half_ref[level, here, :] = coefs[level]
-            grads = [contract(coefs[0], mask_ref[0, here, :], 0, 0) + contract(coefs[1], mask_ref[1, here, :], 0, 0)]
-            starts = [0]
-            for level in range(2, levels):
-                lo, hi = bounds[level]
-                grads.append(contract(coefs[level], query_ref[here, lo:hi], 0, 0))
-                starts.append(lo)
-            for n in range(count):
-                slot = slot_ref[block * count + n]
-                for start, grad in zip(starts, grads):
-                    lanes = slice(start, start + grad.shape[1])
-                    sum_ref[slot, :, lanes] = sum_ref[slot, :, lanes] + grad[n * PBLK : (n + 1) * PBLK, :]
-
-        for pair in range(pairs):
-            for j in range(2):
-                one(pair * 2 + j)
-            here = pair_rows(pair)
-            pltpu.make_async_copy(half_ref.at[:, here], half_hbm.at[:, here], half_sem).start()
-        copy = pltpu.make_async_copy(half_ref, half_hbm, half_sem)
         level_of = lax.broadcasted_iota(jnp.int32, (LANES, width), 0)
         column = lax.broadcasted_iota(jnp.int32, (LANES, width), 1)
         member = jnp.zeros((LANES, width), F32)
         for level, (lo, hi) in enumerate(bounds):
             member = jnp.where((level_of == level) & (column >= lo) & (column < hi), 1.0, member)
         member = member.astype(BF16)
+        for block in range(blocks):
+            add_scales(block, True)
         step_slots = slots // CHUNKS
-        for chunk in range(CHUNKS):
-            part = slice(chunk * step_slots, (chunk + 1) * step_slots)
-            scale = scale_ref[part].reshape(step_slots * PBLK, LANES)
-            high = scale.astype(BF16)
-            rest = scale - high.astype(F32)
-            middle = rest.astype(BF16)
-            low = (rest - middle.astype(F32)).astype(BF16)
-            wide = contract(high, member, 1, 0) + contract(middle, member, 1, 0) + contract(low, member, 1, 0)
-            pool = pool_ref[part].reshape(step_slots * PBLK, width).astype(F32)
-            total = sum_ref[part].reshape(step_slots * PBLK, width)
-            out_ref[part] = (total - wide * pool).astype(BF16).reshape(step_slots, PBLK, width)
-            pltpu.make_async_copy(out_ref.at[part], out_hbm.at[part], out_sem).start()
-        copy.wait()
+        for group in (range(levels - 1, levels), range(levels - 1)):
+            left, right = bounds[group[0]][0], bounds[group[-1]][1]
+            for block in range(blocks):
+                here = pl.ds(block * rows, rows)
+                base_coef = coef_ref[here, :].astype(F32)
+                coefs = {level: (base_coef + low_coef_ref[level, here, :]).astype(BF16) for level in group}
+                for level in group:
+                    half_ref[level, here, :] = coefs[level]
+                grads = []
+                if left == 0:
+                    first = contract(coefs[0], mask_ref[0, here, :], 0, 0) + contract(coefs[1], mask_ref[1, here, :], 0, 0)
+                    grads.append((0, first))
+                for level in group:
+                    if level >= 2:
+                        lo, hi = bounds[level]
+                        grads.append((lo, contract(coefs[level], query_ref[here, lo:hi], 0, 0)))
+                for n in range(count):
+                    slot = slot_ref[block * count + n]
+                    for start, grad in grads:
+                        lanes = slice(start, start + grad.shape[1])
+                        sum_ref[slot, :, lanes] = sum_ref[slot, :, lanes] + grad[n * PBLK : (n + 1) * PBLK, :]
+            done = pl.ds(group[0], len(group))
+            pltpu.make_async_copy(half_ref.at[done], half_hbm.at[done], half_sem).start()
+            for chunk in range(CHUNKS):
+                part = slice(chunk * step_slots, (chunk + 1) * step_slots)
+                scale = scale_ref[part].reshape(step_slots * PBLK, LANES)
+                high = scale.astype(BF16)
+                rest = scale - high.astype(F32)
+                middle = rest.astype(BF16)
+                low = (rest - middle.astype(F32)).astype(BF16)
+                side = member[:, left:right]
+                wide = contract(high, side, 1, 0) + contract(middle, side, 1, 0) + contract(low, side, 1, 0)
+                pool = pool_ref[part, :, left:right].reshape(step_slots * PBLK, right - left).astype(F32)
+                total = sum_ref[part, :, left:right].reshape(step_slots * PBLK, right - left)
+                out_ref[part, :, left:right] = (total - wide * pool).astype(BF16).reshape(step_slots, PBLK, right - left)
+                lanes = pl.ds(left, right - left)
+                pltpu.make_async_copy(out_ref.at[part, :, lanes], out_hbm.at[part, :, lanes], out_sem).start()
+        pltpu.make_async_copy(half_ref, half_hbm, half_sem).wait()
         row_copy.wait()
         pltpu.make_async_copy(out_ref, out_hbm, out_sem).wait()
 
@@ -537,15 +534,15 @@
 
 def collect_kernel(target_ref, back_hbm, out_ref, back_ref, sem):
     rows = out_ref.shape[0]
-    size = back_ref.shape[0] // 2
+    size = back_ref.shape[0] // CHUNKS
     copies = []
-    for half in range(2):
+    for half in range(CHUNKS):
         part = pl.ds(half * size, size)
         copies.append(pltpu.make_async_copy(back_hbm.at[part], back_ref.at[part], sem.at[half]))
         copies[-1].start()
     here = lax.broadcasted_iota(jnp.int32, (rows, size), 0)
     total = None
-    for half in range(2):
+    for half in range(CHUNKS):
         part = slice(half * size, (half + 1) * size)
         choose = jnp.where(here == target_ref[:, part], 1.0, 0.0).astype(BF16)
         copies[half].wait()
@@ -736,7 +733,7 @@
         out_shape=jax.ShapeDtypeStruct((local_blocks * PBLK, width), BF16),
         in_specs=[vmem(), hbm()],
         out_specs=vmem(),
-        scratch_shapes=[pltpu.VMEM((slots * PBLK, width), BF16), pltpu.SemaphoreType.DMA((2,))],
+        scratch_shapes=[pltpu.VMEM((slots * PBLK, width), BF16), pltpu.SemaphoreType.DMA((CHUNKS,))],
         compiler_params=params(),
         name="collect",
     )(target, pinned(back.reshape(slots * PBLK, width)))

time: 158 us -> 158 us (level)
  no operation moved by 1% of the time
where the time goes in v9:
time: 158 us; the launch traced here: 157 us
  waiting for transfers between devices  88.8 us (56%)
  starting transfers between devices  30.1 us (19%)
  Pallas kernels  28.9 us (18%)
  blocking collectives  7.38 us (5%)
    all_to_all x1, waiting for transfers between devices, per_device(): pool = lax.all_to_all(panels, 'dp', split_axis=0, concat_axis=0, tiled=True)  49.5 us
    all_to_all x1, waiting for transfers between devices, per_device(): lax.all_to_all(slot_grad, 'dp', split_axis=0, concat_axis=0, tiled=True)  37.5 us
    all_to_all x1, starting transfers between devices, per_device(): pool = lax.all_to_all(panels, 'dp', split_axis=0, concat_axis=0, tiled=True)  13.3 us
    ppermute x6, starting transfers between devices, shift_by(): lax.ppermute(part, 'tensor', [(i, (i + s) % shards) for i in range(shards)])  9.07 us
    all_to_all x1, starting transfers between devices, per_device(): lax.all_to_all(slot_grad, 'dp', split_axis=0, concat_axis=0, tiled=True)  7.7 us
    psum x1, blocking collectives, per_device(): loss = lax.psum(loss, 'tensor')  7.38 us
    pallas_call x1, Pallas kernels, per_device(): pl.pallas_call(partial(passage_kernel, bounds, shards, per_shard, rows),...  6.26 us
    pallas_call x1, Pallas kernels, per_device(): pl.pallas_call(partial(query_kernel, bounds, rows, 1.0 / weight_total), o...  5.82 us
  transfers between devices with their start and end apart: 8, of which 5 were waited for; matrix products, arithmetic and copies ran while one was open for 1% of the time, Pallas kernels for 8%

profile of v9, /device:TPU:1, one launch (start us, length us, event | category | flops | bytes accessed | tf_op | source)
XLA Modules:
  0.0 157.5 jit_solution(3441262759260809111)
XLA Ops:
  0.6 3.2 %pack.1 = bf16[64,16,1024]{2,1,0:T(8,128)(2,1)} custom-call(s32[1]{0:T(128)} %bitcast.1.first_ref, s32[16,512]{1,0:T(8,128)} %bitcast.8, bf16[16,16,1024]{2,1,0:T(8,128)(2,1)} %bitcast.7), custom_call_target="tpu_custom_call" | custom-call | tf_op jit(solution)/shard_map/pack/pallas_call | solution.py:593
  3.8 0.0 copy-start.2
  3.8 0.0 copy-start
  3.8 0.0 copy-start.3
  3.9 13.3 %all-to-all-start = ((bf16[64,16,1024]{2,1,0:T(8,128)(2,1)}), bf16[64,16,1024]{2,1,0:T(8,128)(2,1)S(1)}, u32[]{:S(2)}, u32[]{:S(2)}) async-start(bf16[64,16,1024]{2,1,0:T(8,128)(2,1)} %pack.1), calls=%async_computation | async-start | bytes 4194304 | tf_op jit(solution)/shard_map/all_to_all | solution.py:614
  17.2 0.0 copy-done.2
  17.2 0.1 constant_dynamic-slice_fusion
  17.2 0.1 copy.16
  17.3 0.1 reshape.83.slot_ref
  17.4 0.0 copy-done
  17.4 0.9 prep.1
  18.4 0.1 add.57
  18.5 0.1 add.58
  18.6 0.1 broadcast_in_dim.40
  18.6 0.1 broadcast_in_dim.41
  18.8 0.1 add.60
  18.8 0.0 copy-done.3
  18.8 0.1 convert_element_type.10.pos_ref
  18.9 49.5 %all-to-all-done.pool_ref = bf16[64,16,1024]{2,1,0:T(8,128)(2,1)S(1)} async-done(((bf16[64,16,1024]{2,1,0:T(8,128)(2,1)}), bf16[64,16,1024]{2,1,0:T(8,128)(2,1)S(1)}, u32[]{:S(2)}, u32[]{:S(2)}) %all-to-all-start) | async-done | bytes 2097184 | tf_op jit(solution)/shard_map/all_to_all | solution.py:614
  68.4 2.0 %dots.1 = (f32[8,8,256]{2,1,0:T(8,128)S(1)}, f32[136,256]{1,0:T(8,128)S(1)}, f32[136,256]{1,0:T(8,128)S(1)}, f32[136,256]{1,0:T(8,128)S(1)}, f32[136,256]{1,0:T(8,128)S(1)}) custom-call(s32[128]{0:T(128)S(1)} %reshape.83.slot_ref, s32[1]{0:T(128)} %bitcast.shard_ref, bf16[512,1024]{1,0:T(8,128)(2,1)S(1)} %copy-done, ...), custom_call_target="tpu_custom_call" | custom-call | tf_op jit(solution)/shard_map/dots/pallas_call | solution.py:632
  70.4 1.3 collective-permute-start
  71.7 2.4 %collective-permute-start.1 = (f32[136,256]{1,0:T(8,128)S(1)}, f32[136,256]{1,0:T(8,128)S(1)}, u32[]{:S(2)}, u32[]{:S(2)}) collective-permute-start(f32[136,256]{1,0:T(8,128)S(1)} %get-tuple-element.35), channel_id=1, source_target_pairs={{0,2},{1,3},{2,0},{3,1},{4,6},{5,7},{6,4},{7,5},{8,10},{9,11},{10,... | collective-permute-start | bytes 417800 | tf_op jit(solution)/shard_map/ppermute | solution.py:628
  74.1 1.2 collective-permute-start.2
  75.3 4.8 %low.1 = (f32[5,512,256]{2,1,0:T(8,128)}, f32[8,8,64]{2,1,0:T(8,128)}, f32[8,8,256]{2,1,0:T(8,128)}, f32[8,64]{1,0:T(8,128)S(1)}) custom-call(s32[128]{0:T(128)S(1)} %reshape.83.slot_ref, s32[1]{0:T(128)} %bitcast.shard_ref, bf16[512,1024]{1,0:T(8,128)(2,1)S(1)} %copy-done, bf16[64,16,1024]{2,1,0:T(8,128)(2,1)S(1)} %all-to-all-done.pool_ref, ...), custom_call_target="tpu_custom_call" | custom-call | tf_op jit(solution)/shard_map/low/pallas_call | solution.py:643
  80.0 0.0 collective-permute-done.refs_1_
  80.1 0.4 collective-permute-done.1.refs_2_
  80.5 0.0 collective-permute-done.2.refs_3_
  80.5 1.2 high.1
  81.7 1.1 collective-permute-start.3
  82.8 2.2 %collective-permute-start.4 = (bf16[160,256]{1,0:T(8,128)(2,1)}, bf16[160,256]{1,0:T(8,128)(2,1)}, u32[]{:S(2)}, u32[]{:S(2)}) collective-permute-start(bf16[160,256]{1,0:T(8,128)(2,1)} %get-tuple-element.43), channel_id=1, source_target_pairs={{0,2},{1,3},{2,0},{3,1},{4,6},{5,7},{6,4},{7,5},{8,10},{9,11},{10,... | collective-permute-start | bytes 245768 | tf_op jit(solution)/shard_map/ppermute | solution.py:628
  84.9 0.9 collective-permute-start.5
  85.9 0.1 reshape.87.slot_ref
  86.0 1.8 %stage.1 = (f32[8,8,64]{2,1,0:T(8,128)S(1)}, f32[8,8,256]{2,1,0:T(8,128)S(1)}, f32[5,512,256]{2,1,0:T(8,128)S(1)}) custom-call(s32[1]{0:T(128)} %bitcast.shard_ref, f32[8,8,64]{2,1,0:T(8,128)} %get-tuple-element.30.after_ref.row_hbm, f32[8,8,256]{2,1,0:T(8,128)} %get-tuple-element.31.col_hbm, f32[5,512,256]{2,1,0:T(8,128)} %get-tuple-element.32.coef_hbm, ...), custom_call_target="tpu_custom_call" | custom-call | tf_op jit(solution)/shard_map/stage/pallas_call | solution.py:675
  87.8 0.0 collective-permute-done.3.refs_1_
  87.8 0.2 collective-permute-done.4.refs_2_
  88.0 1.2 collective-permute-done.5.refs_3_
  89.2 6.3 %passage.1 = (bf16[64,16,1024]{2,1,0:T(8,128)(2,1)}, bf16[5,512,256]{2,1,0:T(8,128)(2,1)}, f32[8,8,64]{2,1,0:T(8,128)}) custom-call(s32[128]{0:T(128)S(1)} %reshape.87.slot_ref, s32[1]{0:T(128)} %bitcast.shard_ref, bf16[512,1024]{1,0:T(8,128)(2,1)S(1)} %copy-done, bf16[64,16,1024]{2,1,0:T(8,128)(2,1)S(1)} %all-to-all-done.pool_ref, ...), custom_call_target="tpu_custom_call" | custom-call | tf_op jit(solution)/shard_map/passage/pallas_call | solution.py:691
  95.5 0.0 copy-start.1
  95.5 7.7 %all-to-all-start.1 = ((bf16[64,16,1024]{2,1,0:T(8,128)(2,1)}), bf16[64,16,1024]{2,1,0:T(8,128)(2,1)}, u32[]{:S(2)}, u32[]{:S(2)}) async-start(bf16[64,16,1024]{2,1,0:T(8,128)(2,1)} %get-tuple-element.49), calls=%async_computation.1 | async-start | bytes 4194304 | tf_op jit(solution)/shard_map/all_to_all | solution.py:715
  103.2 0.1 fusion.2
  103.3 0.1 reduce_max.14
  103.4 0.1 reduce_max.18
  103.5 0.1 add_select_fusion.2
  103.6 0.1 select_n.63.target_ref
  103.7 0.0 copy-done.1
  103.7 5.8 %query.1 = (bf16[512,1024]{1,0:T(8,128)(2,1)}, f32[4,128]{1,0:T(4,128)S(1)}) custom-call(s32[128]{0:T(128)S(1)} %reshape.83.slot_ref, s32[1]{0:T(128)} %bitcast.shard_ref, bf16[512,1024]{1,0:T(8,128)(2,1)S(1)} %copy-done, bf16[64,16,1024]{2,1,0:T(8,128)(2,1)S(1)} %all-to-all-done.pool_ref, f32[8,8,64]{2,1,0:T(8,128)S(1)} %copy-done.1, ...), custom_call_target="tpu_custom_call" | custom-call | tf_op jit(solution)/shard_map/query/pallas_call | solution.py:717
  109.5 7.4 %psum.7 = f32[512]{0:T(512)} all-reduce(f32[512]{0:T(512)S(1)} %bitcast.6), channel_id=1, replica_groups=mesh['dp'=64,'tensor'=4] {'tensor'}, use_global_device_ids=true, to_apply=%region_2.3 | all-reduce | flops 512 | bytes 4096 | tf_op jit(solution)/shard_map/psum | solution.py:729
  116.9 37.5 %all-to-all-done.1 = bf16[64,16,1024]{2,1,0:T(8,128)(2,1)} async-done(((bf16[64,16,1024]{2,1,0:T(8,128)(2,1)}), bf16[64,16,1024]{2,1,0:T(8,128)(2,1)}, u32[]{:S(2)}, u32[]{:S(2)}) %all-to-all-start.1) | async-done | bytes 2097184 | tf_op jit(solution)/shard_map/all_to_all | solution.py:715
  154.4 2.9 %collect.1 = bf16[256,1024]{1,0:T(8,128)(2,1)} custom-call(s32[1,1024]{1,0:T(1,128)S(1)} %select_n.63.target_ref, bf16[1024,1024]{1,0:T(8,128)(2,1)} %bitcast.4.back_hbm), custom_call_target="tpu_custom_call" | custom-call | tf_op jit(solution)/shard_map/collect/pallas_call | solution.py:731
  (7 shorter events, 0.0 us)
Async XLA Ops:
  3.8 13.3 %copy-start.2 = (s32[512,16]{0,1:T(8,128)S(1)}, s32[512,16]{0,1:T(8,128)}, u32[]{:S(2)}) copy-start(s32[512,16]{0,1:T(8,128)} %param.6) | copy-start | bytes 98308
  3.8 13.6 %copy-start = (bf16[512,1024]{1,0:T(8,128)(2,1)S(1)}, bf16[512,1024]{1,0:T(8,128)(2,1)}, u32[]{:S(2)}) copy-start(bf16[512,1024]{1,0:T(8,128)(2,1)} %query_ref.9) | copy-start | bytes 3145732
  3.8 15.0 %copy-start.3 = (s32[512]{0:T(512)S(1)}, s32[512]{0:T(512)}, u32[]{:S(2)}) copy-start(s32[512]{0:T(512)} %param.7) | copy-start | bytes 6148
  3.9 64.6 %all-to-all-start = ((bf16[64,16,1024]{2,1,0:T(8,128)(2,1)}), bf16[64,16,1024]{2,1,0:T(8,128)(2,1)S(1)}, u32[]{:S(2)}, u32[]{:S(2)}) async-start(bf16[64,16,1024]{2,1,0:T(8,128)(2,1)} %pack.1), calls=%async_computation | async-start | bytes 4194304 | tf_op jit(solution)/shard_map/all_to_all | solution.py:614
  70.4 9.7 %collective-permute-start = (f32[136,256]{1,0:T(8,128)S(1)}, f32[136,256]{1,0:T(8,128)S(1)}, u32[]{:S(2)}, u32[]{:S(2)}) collective-permute-start(f32[136,256]{1,0:T(8,128)S(1)} %get-tuple-element.34), channel_id=1, source_target_pairs={{0,1},{1,2},{2,3},{3,0},{4,5},{5,6},{6,7},{7,4},{8,9},{9,10},{10,1... | collective-permute-start | bytes 417800 | tf_op jit(solution)/shard_map/ppermute | solution.py:628
  71.7 8.8 %collective-permute-start.1 = (f32[136,256]{1,0:T(8,128)S(1)}, f32[136,256]{1,0:T(8,128)S(1)}, u32[]{:S(2)}, u32[]{:S(2)}) collective-permute-start(f32[136,256]{1,0:T(8,128)S(1)} %get-tuple-element.35), channel_id=1, source_target_pairs={{0,2},{1,3},{2,0},{3,1},{4,6},{5,7},{6,4},{7,5},{8,10},{9,11},{10,... | collective-permute-start | bytes 417800 | tf_op jit(solution)/shard_map/ppermute | solution.py:628
  74.1 6.4 %collective-permute-start.2 = (f32[136,256]{1,0:T(8,128)S(1)}, f32[136,256]{1,0:T(8,128)S(1)}, u32[]{:S(2)}, u32[]{:S(2)}) collective-permute-start(f32[136,256]{1,0:T(8,128)S(1)} %get-tuple-element.36), channel_id=1, source_target_pairs={{0,3},{1,0},{2,1},{3,2},{4,7},{5,4},{6,5},{7,6},{8,11},{9,8},{10,9... | collective-permute-start | bytes 417800 | tf_op jit(solution)/shard_map/ppermute | solution.py:628
  81.7 6.1 %collective-permute-start.3 = (bf16[160,256]{1,0:T(8,128)(2,1)}, bf16[160,256]{1,0:T(8,128)(2,1)}, u32[]{:S(2)}, u32[]{:S(2)}) collective-permute-start(bf16[160,256]{1,0:T(8,128)(2,1)} %get-tuple-element.42), channel_id=1, source_target_pairs={{0,1},{1,2},{2,3},{3,0},{4,5},{5,6},{6,7},{7,4},{8,9},{9,10},{10,1... | collective-permute-start | bytes 245768 | tf_op jit(solution)/shard_map/ppermute | solution.py:628
  82.8 5.2 %collective-permute-start.4 = (bf16[160,256]{1,0:T(8,128)(2,1)}, bf16[160,256]{1,0:T(8,128)(2,1)}, u32[]{:S(2)}, u32[]{:S(2)}) collective-permute-start(bf16[160,256]{1,0:T(8,128)(2,1)} %get-tuple-element.43), channel_id=1, source_target_pairs={{0,2},{1,3},{2,0},{3,1},{4,6},{5,7},{6,4},{7,5},{8,10},{9,11},{10,... | collective-permute-start | bytes 245768 | tf_op jit(solution)/shard_map/ppermute | solution.py:628
  84.9 4.3 %collective-permute-start.5 = (bf16[160,256]{1,0:T(8,128)(2,1)}, bf16[160,256]{1,0:T(8,128)(2,1)}, u32[]{:S(2)}, u32[]{:S(2)}) collective-permute-start(bf16[160,256]{1,0:T(8,128)(2,1)} %get-tuple-element.44), channel_id=1, source_target_pairs={{0,3},{1,0},{2,1},{3,2},{4,7},{5,4},{6,5},{7,6},{8,11},{9,8},{10,9... | collective-permute-start | bytes 245768 | tf_op jit(solution)/shard_map/ppermute | solution.py:628
  95.5 8.2 %copy-start.1 = (f32[8,8,64]{2,1,0:T(8,128)S(1)}, f32[8,8,64]{2,1,0:T(8,128)}, u32[]{:S(2)}) copy-start(f32[8,8,64]{2,1,0:T(8,128)} %get-tuple-element.45.row_ref) | copy-start | bytes 49156
  95.5 58.9 %all-to-all-start.1 = ((bf16[64,16,1024]{2,1,0:T(8,128)(2,1)}), bf16[64,16,1024]{2,1,0:T(8,128)(2,1)}, u32[]{:S(2)}, u32[]{:S(2)}) async-start(bf16[64,16,1024]{2,1,0:T(8,128)(2,1)} %get-tuple-element.49), calls=%async_computation.1 | async-start | bytes 4194304 | tf_op jit(solution)/shard_map/all_to_all | solution.py:715

commit v10 on v9

--- a/solution.py
+++ b/solution.py
@@ -148,7 +148,8 @@
         pltpu.make_async_copy(block_ref.at[wanted_ref[0, d * share]], out_hbm.at[d], out_sem).start()
         return carry
 
-    lax.fori_loop(0, out_hbm.shape[0], one, 0, unroll=8)
+    for d in range(out_hbm.shape[0]):
+        one(d, 0)
     pltpu.make_async_copy(out_hbm, out_hbm, out_sem).wait()
 
 

time: 158 us -> 158 us (level)
  no operation moved by 1% of the time
where the time goes in v10:
time: 158 us; the launch traced here: 157 us
  waiting for transfers between devices  88.8 us (56%)
  starting transfers between devices  30.1 us (19%)
  Pallas kernels  28.9 us (18%)
  blocking collectives  7.38 us (5%)
    all_to_all x1, waiting for transfers between devices, per_device(): pool = lax.all_to_all(panels, 'dp', split_axis=0, concat_axis=0, tiled=True)  49.5 us
    all_to_all x1, waiting for transfers between devices, per_device(): lax.all_to_all(slot_grad, 'dp', split_axis=0, concat_axis=0, tiled=True)  37.5 us
    all_to_all x1, starting transfers between devices, per_device(): pool = lax.all_to_all(panels, 'dp', split_axis=0, concat_axis=0, tiled=True)  13.3 us
    ppermute x6, starting transfers between devices, shift_by(): lax.ppermute(part, 'tensor', [(i, (i + s) % shards) for i in range(shards)])  9.06 us
    all_to_all x1, starting transfers between devices, per_device(): lax.all_to_all(slot_grad, 'dp', split_axis=0, concat_axis=0, tiled=True)  7.71 us
    psum x1, blocking collectives, per_device(): loss = lax.psum(loss, 'tensor')  7.38 us
    pallas_call x1, Pallas kernels, per_device(): pl.pallas_call(partial(passage_kernel, bounds, shards, per_shard, rows),...  6.26 us
    pallas_call x1, Pallas kernels, per_device(): pl.pallas_call(partial(query_kernel, bounds, rows, 1.0 / weight_total), o...  5.81 us
  transfers between devices with their start and end apart: 8, of which 5 were waited for; matrix products, arithmetic and copies ran while one was open for 1% of the time, Pallas kernels for 8%

profile of v10, /device:TPU:1, one launch (start us, length us, event | category | flops | bytes accessed | tf_op | source)
XLA Modules:
  0.0 157.5 jit_solution(9919015732412711053)
XLA Ops:
  0.6 3.2 %pack.1 = bf16[64,16,1024]{2,1,0:T(8,128)(2,1)} custom-call(s32[1]{0:T(128)} %bitcast.1.first_ref, s32[16,512]{1,0:T(8,128)} %bitcast.8, bf16[16,16,1024]{2,1,0:T(8,128)(2,1)} %bitcast.7), custom_call_target="tpu_custom_call" | custom-call | tf_op jit(solution)/shard_map/pack/pallas_call | solution.py:594
  3.8 0.0 copy-start.2
  3.8 0.0 copy-start
  3.8 0.0 copy-start.3
  3.8 13.3 %all-to-all-start = ((bf16[64,16,1024]{2,1,0:T(8,128)(2,1)}), bf16[64,16,1024]{2,1,0:T(8,128)(2,1)S(1)}, u32[]{:S(2)}, u32[]{:S(2)}) async-start(bf16[64,16,1024]{2,1,0:T(8,128)(2,1)} %pack.1), calls=%async_computation | async-start | bytes 4194304 | tf_op jit(solution)/shard_map/all_to_all | solution.py:615
  17.2 0.0 copy-done.2
  17.2 0.1 constant_dynamic-slice_fusion
  17.2 0.1 copy.16
  17.3 0.1 reshape.83.slot_ref
  17.4 0.0 copy-done
  17.4 0.9 prep.1
  18.4 0.1 add.57
  18.5 0.1 add.58
  18.6 0.1 broadcast_in_dim.40
  18.6 0.1 broadcast_in_dim.41
  18.8 0.1 add.60
  18.8 0.0 copy-done.3
  18.8 0.1 convert_element_type.10.pos_ref
  18.9 49.5 %all-to-all-done.pool_ref = bf16[64,16,1024]{2,1,0:T(8,128)(2,1)S(1)} async-done(((bf16[64,16,1024]{2,1,0:T(8,128)(2,1)}), bf16[64,16,1024]{2,1,0:T(8,128)(2,1)S(1)}, u32[]{:S(2)}, u32[]{:S(2)}) %all-to-all-start) | async-done | bytes 2097184 | tf_op jit(solution)/shard_map/all_to_all | solution.py:615
  68.4 2.0 %dots.1 = (f32[8,8,256]{2,1,0:T(8,128)S(1)}, f32[136,256]{1,0:T(8,128)S(1)}, f32[136,256]{1,0:T(8,128)S(1)}, f32[136,256]{1,0:T(8,128)S(1)}, f32[136,256]{1,0:T(8,128)S(1)}) custom-call(s32[128]{0:T(128)S(1)} %reshape.83.slot_ref, s32[1]{0:T(128)} %bitcast.shard_ref, bf16[512,1024]{1,0:T(8,128)(2,1)S(1)} %copy-done, ...), custom_call_target="tpu_custom_call" | custom-call | tf_op jit(solution)/shard_map/dots/pallas_call | solution.py:633
  70.4 1.3 collective-permute-start
  71.7 2.5 %collective-permute-start.1 = (f32[136,256]{1,0:T(8,128)S(1)}, f32[136,256]{1,0:T(8,128)S(1)}, u32[]{:S(2)}, u32[]{:S(2)}) collective-permute-start(f32[136,256]{1,0:T(8,128)S(1)} %get-tuple-element.35), channel_id=1, source_target_pairs={{0,2},{1,3},{2,0},{3,1},{4,6},{5,7},{6,4},{7,5},{8,10},{9,11},{10,... | collective-permute-start | bytes 417800 | tf_op jit(solution)/shard_map/ppermute | solution.py:629
  74.1 1.2 collective-permute-start.2
  75.3 4.8 %low.1 = (f32[5,512,256]{2,1,0:T(8,128)}, f32[8,8,64]{2,1,0:T(8,128)}, f32[8,8,256]{2,1,0:T(8,128)}, f32[8,64]{1,0:T(8,128)S(1)}) custom-call(s32[128]{0:T(128)S(1)} %reshape.83.slot_ref, s32[1]{0:T(128)} %bitcast.shard_ref, bf16[512,1024]{1,0:T(8,128)(2,1)S(1)} %copy-done, bf16[64,16,1024]{2,1,0:T(8,128)(2,1)S(1)} %all-to-all-done.pool_ref, ...), custom_call_target="tpu_custom_call" | custom-call | tf_op jit(solution)/shard_map/low/pallas_call | solution.py:644
  80.0 0.0 collective-permute-done.refs_1_
  80.1 0.4 collective-permute-done.1.refs_2_
  80.5 0.0 collective-permute-done.2.refs_3_
  80.5 1.2 high.1
  81.7 1.1 collective-permute-start.3
  82.8 2.2 %collective-permute-start.4 = (bf16[160,256]{1,0:T(8,128)(2,1)}, bf16[160,256]{1,0:T(8,128)(2,1)}, u32[]{:S(2)}, u32[]{:S(2)}) collective-permute-start(bf16[160,256]{1,0:T(8,128)(2,1)} %get-tuple-element.43), channel_id=1, source_target_pairs={{0,2},{1,3},{2,0},{3,1},{4,6},{5,7},{6,4},{7,5},{8,10},{9,11},{10,... | collective-permute-start | bytes 245768 | tf_op jit(solution)/shard_map/ppermute | solution.py:629
  84.9 0.9 collective-permute-start.5
  85.9 0.1 reshape.87.slot_ref
  86.0 1.8 %stage.1 = (f32[8,8,64]{2,1,0:T(8,128)S(1)}, f32[8,8,256]{2,1,0:T(8,128)S(1)}, f32[5,512,256]{2,1,0:T(8,128)S(1)}) custom-call(s32[1]{0:T(128)} %bitcast.shard_ref, f32[8,8,64]{2,1,0:T(8,128)} %get-tuple-element.30.after_ref.row_hbm, f32[8,8,256]{2,1,0:T(8,128)} %get-tuple-element.31.col_hbm, f32[5,512,256]{2,1,0:T(8,128)} %get-tuple-element.32.coef_hbm, ...), custom_call_target="tpu_custom_call" | custom-call | tf_op jit(solution)/shard_map/stage/pallas_call | solution.py:676
  87.8 0.0 collective-permute-done.3.refs_1_
  87.8 0.2 collective-permute-done.4.refs_2_
  88.0 1.2 collective-permute-done.5.refs_3_
  89.2 6.3 %passage.1 = (bf16[64,16,1024]{2,1,0:T(8,128)(2,1)}, bf16[5,512,256]{2,1,0:T(8,128)(2,1)}, f32[8,8,64]{2,1,0:T(8,128)}) custom-call(s32[128]{0:T(128)S(1)} %reshape.87.slot_ref, s32[1]{0:T(128)} %bitcast.shard_ref, bf16[512,1024]{1,0:T(8,128)(2,1)S(1)} %copy-done, bf16[64,16,1024]{2,1,0:T(8,128)(2,1)S(1)} %all-to-all-done.pool_ref, ...), custom_call_target="tpu_custom_call" | custom-call | tf_op jit(solution)/shard_map/passage/pallas_call | solution.py:692
  95.5 0.0 copy-start.1
  95.5 7.7 %all-to-all-start.1 = ((bf16[64,16,1024]{2,1,0:T(8,128)(2,1)}), bf16[64,16,1024]{2,1,0:T(8,128)(2,1)}, u32[]{:S(2)}, u32[]{:S(2)}) async-start(bf16[64,16,1024]{2,1,0:T(8,128)(2,1)} %get-tuple-element.49), calls=%async_computation.1 | async-start | bytes 4194304 | tf_op jit(solution)/shard_map/all_to_all | solution.py:716
  103.2 0.1 fusion.2
  103.3 0.1 reduce_max.14
  103.4 0.1 reduce_max.18
  103.5 0.1 add_select_fusion.2
  103.6 0.1 select_n.63.target_ref
  103.7 0.0 copy-done.1
  103.7 5.8 %query.1 = (bf16[512,1024]{1,0:T(8,128)(2,1)}, f32[4,128]{1,0:T(4,128)S(1)}) custom-call(s32[128]{0:T(128)S(1)} %reshape.83.slot_ref, s32[1]{0:T(128)} %bitcast.shard_ref, bf16[512,1024]{1,0:T(8,128)(2,1)S(1)} %copy-done, bf16[64,16,1024]{2,1,0:T(8,128)(2,1)S(1)} %all-to-all-done.pool_ref, f32[8,8,64]{2,1,0:T(8,128)S(1)} %copy-done.1, ...), custom_call_target="tpu_custom_call" | custom-call | tf_op jit(solution)/shard_map/query/pallas_call | solution.py:718
  109.5 7.4 %psum.7 = f32[512]{0:T(512)} all-reduce(f32[512]{0:T(512)S(1)} %bitcast.6), channel_id=1, replica_groups=mesh['dp'=64,'tensor'=4] {'tensor'}, use_global_device_ids=true, to_apply=%region_2.3 | all-reduce | flops 512 | bytes 4096 | tf_op jit(solution)/shard_map/psum | solution.py:730
  116.9 37.5 %all-to-all-done.1 = bf16[64,16,1024]{2,1,0:T(8,128)(2,1)} async-done(((bf16[64,16,1024]{2,1,0:T(8,128)(2,1)}), bf16[64,16,1024]{2,1,0:T(8,128)(2,1)}, u32[]{:S(2)}, u32[]{:S(2)}) %all-to-all-start.1) | async-done | bytes 2097184 | tf_op jit(solution)/shard_map/all_to_all | solution.py:716
  154.4 2.9 %collect.1 = bf16[256,1024]{1,0:T(8,128)(2,1)} custom-call(s32[1,1024]{1,0:T(1,128)S(1)} %select_n.63.target_ref, bf16[1024,1024]{1,0:T(8,128)(2,1)} %bitcast.4.back_hbm), custom_call_target="tpu_custom_call" | custom-call | tf_op jit(solution)/shard_map/collect/pallas_call | solution.py:732
  (7 shorter events, 0.0 us)
Async XLA Ops:
  3.8 13.3 %copy-start.2 = (s32[512,16]{0,1:T(8,128)S(1)}, s32[512,16]{0,1:T(8,128)}, u32[]{:S(2)}) copy-start(s32[512,16]{0,1:T(8,128)} %param.6) | copy-start | bytes 98308
  3.8 13.6 %copy-start = (bf16[512,1024]{1,0:T(8,128)(2,1)S(1)}, bf16[512,1024]{1,0:T(8,128)(2,1)}, u32[]{:S(2)}) copy-start(bf16[512,1024]{1,0:T(8,128)(2,1)} %query_ref.9) | copy-start | bytes 3145732
  3.8 15.0 %copy-start.3 = (s32[512]{0:T(512)S(1)}, s32[512]{0:T(512)}, u32[]{:S(2)}) copy-start(s32[512]{0:T(512)} %param.7) | copy-start | bytes 6148
  3.8 64.6 %all-to-all-start = ((bf16[64,16,1024]{2,1,0:T(8,128)(2,1)}), bf16[64,16,1024]{2,1,0:T(8,128)(2,1)S(1)}, u32[]{:S(2)}, u32[]{:S(2)}) async-start(bf16[64,16,1024]{2,1,0:T(8,128)(2,1)} %pack.1), calls=%async_computation | async-start | bytes 4194304 | tf_op jit(solution)/shard_map/all_to_all | solution.py:615
  70.4 9.7 %collective-permute-start = (f32[136,256]{1,0:T(8,128)S(1)}, f32[136,256]{1,0:T(8,128)S(1)}, u32[]{:S(2)}, u32[]{:S(2)}) collective-permute-start(f32[136,256]{1,0:T(8,128)S(1)} %get-tuple-element.34), channel_id=1, source_target_pairs={{0,1},{1,2},{2,3},{3,0},{4,5},{5,6},{6,7},{7,4},{8,9},{9,10},{10,1... | collective-permute-start | bytes 417800 | tf_op jit(solution)/shard_map/ppermute | solution.py:629
  71.7 8.8 %collective-permute-start.1 = (f32[136,256]{1,0:T(8,128)S(1)}, f32[136,256]{1,0:T(8,128)S(1)}, u32[]{:S(2)}, u32[]{:S(2)}) collective-permute-start(f32[136,256]{1,0:T(8,128)S(1)} %get-tuple-element.35), channel_id=1, source_target_pairs={{0,2},{1,3},{2,0},{3,1},{4,6},{5,7},{6,4},{7,5},{8,10},{9,11},{10,... | collective-permute-start | bytes 417800 | tf_op jit(solution)/shard_map/ppermute | solution.py:629
  74.1 6.4 %collective-permute-start.2 = (f32[136,256]{1,0:T(8,128)S(1)}, f32[136,256]{1,0:T(8,128)S(1)}, u32[]{:S(2)}, u32[]{:S(2)}) collective-permute-start(f32[136,256]{1,0:T(8,128)S(1)} %get-tuple-element.36), channel_id=1, source_target_pairs={{0,3},{1,0},{2,1},{3,2},{4,7},{5,4},{6,5},{7,6},{8,11},{9,8},{10,9... | collective-permute-start | bytes 417800 | tf_op jit(solution)/shard_map/ppermute | solution.py:629
  81.7 6.1 %collective-permute-start.3 = (bf16[160,256]{1,0:T(8,128)(2,1)}, bf16[160,256]{1,0:T(8,128)(2,1)}, u32[]{:S(2)}, u32[]{:S(2)}) collective-permute-start(bf16[160,256]{1,0:T(8,128)(2,1)} %get-tuple-element.42), channel_id=1, source_target_pairs={{0,1},{1,2},{2,3},{3,0},{4,5},{5,6},{6,7},{7,4},{8,9},{9,10},{10,1... | collective-permute-start | bytes 245768 | tf_op jit(solution)/shard_map/ppermute | solution.py:629
  82.8 5.2 %collective-permute-start.4 = (bf16[160,256]{1,0:T(8,128)(2,1)}, bf16[160,256]{1,0:T(8,128)(2,1)}, u32[]{:S(2)}, u32[]{:S(2)}) collective-permute-start(bf16[160,256]{1,0:T(8,128)(2,1)} %get-tuple-element.43), channel_id=1, source_target_pairs={{0,2},{1,3},{2,0},{3,1},{4,6},{5,7},{6,4},{7,5},{8,10},{9,11},{10,... | collective-permute-start | bytes 245768 | tf_op jit(solution)/shard_map/ppermute | solution.py:629
  84.9 4.3 %collective-permute-start.5 = (bf16[160,256]{1,0:T(8,128)(2,1)}, bf16[160,256]{1,0:T(8,128)(2,1)}, u32[]{:S(2)}, u32[]{:S(2)}) collective-permute-start(bf16[160,256]{1,0:T(8,128)(2,1)} %get-tuple-element.44), channel_id=1, source_target_pairs={{0,3},{1,0},{2,1},{3,2},{4,7},{5,4},{6,5},{7,6},{8,11},{9,8},{10,9... | collective-permute-start | bytes 245768 | tf_op jit(solution)/shard_map/ppermute | solution.py:629
  95.5 8.2 %copy-start.1 = (f32[8,8,64]{2,1,0:T(8,128)S(1)}, f32[8,8,64]{2,1,0:T(8,128)}, u32[]{:S(2)}) copy-start(f32[8,8,64]{2,1,0:T(8,128)} %get-tuple-element.45.row_ref) | copy-start | bytes 49156
  95.5 58.9 %all-to-all-start.1 = ((bf16[64,16,1024]{2,1,0:T(8,128)(2,1)}), bf16[64,16,1024]{2,1,0:T(8,128)(2,1)}, u32[]{:S(2)}, u32[]{:S(2)}) async-start(bf16[64,16,1024]{2,1,0:T(8,128)(2,1)} %get-tuple-element.49), calls=%async_computation.1 | async-start | bytes 4194304 | tf_op jit(solution)/shard_map/all_to_all | solution.py:716
